TPU v7x, 32 devices: a whole 2x2x4 slice. The times are simulated.
32 devices in a mesh: gx: 8 (over z, core), gy: 4 (over y, x).
Axes of the slice: x: 2, y: 2, z: 4, core: 2. Of those that a mesh axis runs over, the one named last changes fastest.
Arguments:
- adj_voltage: float32 [8, 256, 128], P('gx', 'gy'), may hold values from -6 to 6
- adj_gating: float32 [8, 256, 128], P('gx', 'gy'), may hold values from -1.2 to 1.2
- fwd_voltage: bfloat16 [2, 8, 256, 128], P(None, 'gx', 'gy'), may hold values from -0.099609375 to 1.09375
- fwd_gating: bfloat16 [2, 8, 256, 128], P(None, 'gx', 'gy'), may hold values from 0 to 2
- region_labels: int32 [8, 256, 1], P('gx', 'gy'), may hold values from 0 to 7
- region_axial: float32 [2, 8], replicated, may hold values from 0.6 to 3
- region_shear: float32 [8], replicated, may hold values from -0.5 to 0.5
- block_rate: float32 [2], replicated, may hold values from 8 to 32
- block_inverse: float32 [2, 128, 128], replicated, as said below
Outputs:
- voltage_adjoint: float32 [8, 256, 128], P('gx', 'gy')
- gating_adjoint: float32 [8, 256, 128], P('gx', 'gy')
Inputs may be any that keep to these rules, and one draw needn't show every extreme that they name: block_inverse[b] is the inverse of the 128 x 128 tridiagonal matrix with diagonal 1 + 2 block_rate[b] and off-diagonals -block_rate[b].
All inputs are finite; a program needn't handle non-finite values.
Results may differ from a plain program's by a relative error of at most 0.00065.
Values sent between devices are 32-bit elements; how exact they have to be, the bound alone decides.
No kernel may reach another device: no remote copies, remote signals or barrier semaphores. Data moves between devices by JAX's collectives and lax.ppermute only.
A program may use at most 64 MiB of HBM per device.

v0:
```python
import jax
import jax.numpy as jnp
from jax import lax
from jax.sharding import PartitionSpec as P

STEPS = 2
SWEEPS = 11
ZB = 128
LB = 128


FULL_PRECISION = lax.Precision.HIGHEST
TIME_STEP = 0.2
RECOVERY_RATE = 0.25
EXCITATION = 8.0
THRESHOLD = 0.15


def with_halo(x, sides, width):
    for axis, dim in sides:
        size, length = (lax.axis_size(axis), x.shape[dim])
        up = [(i, (i + 1) % size) for i in range(size - 1)]
        down = [(j, i) for i, j in up]
        last = lax.slice_in_dim(x, length - width, length, axis=dim)
        leading = lax.slice_in_dim(x, 0, width, axis=dim)
        before = lax.ppermute(last, axis, up)
        after = lax.ppermute(leading, axis, down)
        x = jnp.concatenate([before, x, after], axis=dim)
    return x


def lookup(labels, lookup_table):
    levels = jnp.arange(lookup_table.shape[0], dtype=jnp.int32)
    return jnp.sum(jnp.where(labels[..., None] == levels, lookup_table, 0.0), axis=-1)


def expand_blocks(block_values):
    block_shape = block_values.shape
    wide_form = jnp.broadcast_to(block_values[..., None], block_shape + (LB,))
    return wide_form.reshape(block_shape[0], block_shape[1], block_shape[2] * LB)


def coefficients(labels, region_axial, region_shear):
    tissue_block = (labels > 0).astype(jnp.float32)
    return (
        expand_blocks(tissue_block),
        expand_blocks(lookup(labels, region_axial[0]) * tissue_block),
        expand_blocks(lookup(labels, region_axial[1]) * tissue_block),
        expand_blocks(lookup(labels, region_shear) * tissue_block),
    )


def couplings(block_rate):
    zero_rate = jnp.zeros((1,), jnp.float32)
    inner_rate = jnp.minimum(block_rate[:-1], block_rate[1:])
    return (jnp.concatenate([zero_rate, inner_rate]), jnp.concatenate([inner_rate, zero_rate]))


def line_solve(line_cells, block_rate, block_inverse):
    item_count, length_cells, across = line_cells.shape
    blocks_count = length_cells // ZB
    shaped = line_cells.reshape(item_count, blocks_count, ZB, across)
    below_rate, after_rate = couplings(block_rate)
    base_blocks = jnp.einsum("bij,xbjy->xbiy", block_inverse, shaped, precision=FULL_PRECISION)
    zero_row = jnp.zeros((item_count, 1, across), jnp.float32)
    middle = jnp.zeros((item_count, blocks_count, ZB - 2, across), jnp.float32)

    def sweep_once(sweep_index, current):
        first_cells = current[:, :, 0, :]
        last_cells = current[:, :, ZB - 1, :]
        from_below = (
            jnp.concatenate([zero_row, last_cells[:, :-1, :]], axis=1) * below_rate[None, :, None]
        )
        from_above = (
            jnp.concatenate([first_cells[:, 1:, :], zero_row], axis=1) * after_rate[None, :, None]
        )
        coupling = jnp.concatenate(
            [from_below[:, :, None, :], middle, from_above[:, :, None, :]], axis=2
        )
        updated = jnp.einsum(
            "bij,xbjy->xbiy", block_inverse, shaped + coupling, precision=FULL_PRECISION
        )
        return updated

    current = lax.fori_loop(0, SWEEPS, sweep_once, base_blocks)
    return current.reshape(item_count, length_cells, across)


def cross_terms(ext_xx, ext_yy, ext_xy):
    pad_y = ((0, 0), (0, 0), (1, 1))
    ext_yy = jnp.pad(ext_yy, pad_y)
    ext_xy = jnp.pad(ext_xy, pad_y)
    term_xx = ext_xx[2:] - 2.0 * ext_xx[1:-1] + ext_xx[:-2]
    term_yy = ext_yy[1:-1, :, 2:] - 2.0 * ext_yy[1:-1, :, 1:-1] + ext_yy[1:-1, :, :-2]
    term_xy = (
        ext_xy[2:, :, 2:] - ext_xy[2:, :, :-2] - ext_xy[:-2, :, 2:] + ext_xy[:-2, :, :-2]
    ) * 0.25
    return term_xx + term_yy + 2.0 * term_xy


def per_device(
    adj_voltage,
    adj_gating,
    fwd_voltage,
    fwd_gating,
    region_labels,
    region_axial,
    region_shear,
    block_rate,
    block_inverse,
):
    groups = lax.axis_size("gy")
    row_count, depth_cells, width_cells = adj_voltage.shape
    narrow = width_cells // groups
    tissue, coef_xx, coef_yy, coef_xy = coefficients(region_labels, region_axial, region_shear)
    adjoint_v = adj_voltage
    adjoint_w = adj_gating
    for step_index in range(STEPS):
        later_index = STEPS - 1 - step_index
        outgoing = adjoint_v.reshape(row_count, 1, depth_cells, groups, narrow)
        pieces = lax.all_to_all(outgoing, "gy", split_axis=3, concat_axis=1, tiled=True)
        item_count = pieces.shape[0]
        line_cells = pieces.reshape(item_count, groups * depth_cells, narrow)
        solved_lines = line_solve(line_cells, block_rate, block_inverse)
        returned_form = solved_lines.reshape(item_count, groups, depth_cells, 1, narrow)
        returned = lax.all_to_all(returned_form, "gy", split_axis=1, concat_axis=3, tiled=True)
        solved = returned.reshape(item_count, depth_cells, width_cells)
        stacked = jnp.stack([coef_xx * solved, coef_yy * solved, coef_xy * solved])
        extended = with_halo(stacked, (("gx", 1),), 1)
        spread_term = cross_terms(extended[0], extended[1], extended[2])
        voltage_now = fwd_voltage[later_index].astype(jnp.float32)
        gating_now = fwd_gating[later_index].astype(jnp.float32)
        ionic_slope = (
            EXCITATION
            * (-3.0 * voltage_now * voltage_now + 2.0 * (1.0 + THRESHOLD) * voltage_now - THRESHOLD)
            - gating_now
        )
        next_v = tissue * (
            solved
            + TIME_STEP * spread_term
            + TIME_STEP * ionic_slope * solved
            + TIME_STEP * RECOVERY_RATE * EXCITATION * adjoint_w
        )
        adjoint_w = tissue * (
            (1.0 - TIME_STEP * RECOVERY_RATE) * adjoint_w - TIME_STEP * voltage_now * solved
        )
        adjoint_v = next_v
    return (adjoint_v, adjoint_w)


def solution(mesh):
    return jax.shard_map(
        per_device,
        mesh=mesh,
        in_specs=(
            P("gx", "gy", None),
            P("gx", "gy", None),
            P(None, "gx", "gy", None),
            P(None, "gx", "gy", None),
            P("gx", "gy", None),
            P(),
            P(),
            P(),
            P(),
        ),
        out_specs=(P("gx", "gy", None), P("gx", "gy", None)),
        check_vma=False,
    )
```

profile of v0, /device:TPU:1, one launch (start us, length us, event | category | flops | bytes accessed | tf_op | source)
XLA Modules:
  0.0 79.6 jit_solution(2943020983780482412)
XLA Ops:
  0.6 0.8 %copy.73 = f32[1,64,128]{1,2,0:T(8,128)S(1)} copy(f32[1,64,128]{2,1,0:T(8,128)} %param.13) | data formatting | bytes 65536 | tf_op args[0]
  1.5 0.7 reshape.981
  2.2 4.4 %all-to-all-start = ((f32[4,1,2048]{2,1,0:T(1,128)}), f32[4,1,2048]{2,1,0:T(1,128)S(1)}, u32[]{:S(2)}, u32[]{:S(2)}) async-start(f32[4,1,2048]{2,1,0:T(1,128)} %reshape.981), calls=%async_computation | async-start | bytes 65536 | tf_op jit(solution)/shard_map/all_to_all | solution.py:121
  6.6 0.6 fusion.69
  7.3 0.7 copy-done.3
  9.4 0.6 copy-done.4
  10.2 0.5 broadcast.556
  10.7 0.7 reduce.11
  11.9 0.7 copy-done
  12.8 9.9 %while.20 = (s32[]{:T(128)}, f32[1,2,128,32]{2,3,1,0:T(8,128)S(1)}, f32[1,2,128,32]{2,3,1,0:T(8,128)S(1)}, f32[2]{0:T(128)S(1)}, f32[2]{0:T(128)S(1)}, /*index=5...) while((s32[]{:T(128)}, f32[1,2,128,32]{2,3,1,0:T(8,128)S(1)}, f32[1,2,128,32]{2,3,1,0:T(8,128)S(1)}, ...), condition=%wide.region_1.2_spmd, body=%wide.region_0.1_spmd.sunk | while | flops 12607618 | bytes 202597 | solution.py:85
  13.4 0.4 convolution_bitcast_fusion.6
  14.3 0.4 convolution_bitcast_fusion.6
  15.2 0.4 convolution_bitcast_fusion.6
  16.1 0.4 convolution_bitcast_fusion.6
  17.0 0.4 convolution_bitcast_fusion.6
  17.9 0.4 convolution_bitcast_fusion.6
  18.8 0.4 convolution_bitcast_fusion.6
  19.7 0.4 convolution_bitcast_fusion.6
  20.6 0.4 convolution_bitcast_fusion.6
  21.5 0.4 convolution_bitcast_fusion.6
  22.4 0.4 convolution_bitcast_fusion.6
  22.9 0.7 reshape.983
  23.6 3.6 %all-to-all-start.1 = ((f32[4,1,2048]{2,1,0:T(1,128)}), f32[4,1,2048]{2,1,0:T(1,128)S(1)}, u32[]{:S(2)}, u32[]{:S(2)}) async-start(f32[4,1,2048]{2,1,0:T(1,128)} %reshape.983), calls=%async_computation.1 | async-start | bytes 65536 | tf_op jit(solution)/shard_map/all_to_all | solution.py:126
  27.3 3.6 %all-to-all-done.1 = f32[4,1,2048]{2,1,0:T(1,128)S(1)} async-done(((f32[4,1,2048]{2,1,0:T(1,128)}), f32[4,1,2048]{2,1,0:T(1,128)S(1)}, u32[]{:S(2)}, u32[]{:S(2)}) %all-to-all-start.1) | async-done | bytes 32800 | tf_op jit(solution)/shard_map/all_to_all | solution.py:126
  30.9 0.7 reduce.12
  31.7 4.8 %collective-permute-start = (f32[3,1,64,128]{2,3,1,0:T(8,128)S(1)}, f32[3,1,64,128]{2,3,1,0:T(8,128)S(1)}, u32[]{:S(2)}, u32[]{:S(2)}) collective-permute-start(f32[3,1,64,128]{2,3,1,0:T(8,128)S(1)} %pad_maximum_fusion.8), channel_id=1, source_target_pairs={{4,0},{8,4},{12,8},{16,12},{20,16},{24,20},{28,24},{5,1},{9,5},{13... | collective-permute-start | bytes 294920 | tf_op jit(solution)/shard_map/ppermute | solution.py:27
  36.5 3.1 %collective-permute-start.1 = (f32[3,1,64,128]{2,3,1,0:T(8,128)S(1)}, f32[3,1,64,128]{2,3,1,0:T(8,128)S(1)}, u32[]{:S(2)}, u32[]{:S(2)}) collective-permute-start(f32[3,1,64,128]{2,3,1,0:T(8,128)S(1)} %pad_maximum_fusion.8), channel_id=1, source_target_pairs={{0,4},{4,8},{8,12},{12,16},{16,20},{20,24},{24,28},{1,5},{5,9},{9,... | collective-permute-start | bytes 294920 | tf_op jit(solution)/shard_map/ppermute | solution.py:26
  39.9 0.6 copy-done.1
  40.6 0.4 collective-permute-done
  41.0 1.2 %collective-permute-done.1 = f32[3,1,64,128]{2,3,1,0:T(8,128)S(1)} collective-permute-done((f32[3,1,64,128]{2,3,1,0:T(8,128)S(1)}, f32[3,1,64,128]{2,3,1,0:T(8,128)S(1)}, u32[]{:S(2)}, u32[]{:S(2)}) %collective-permute-start.1) | collective-permute-done | bytes 98336 | tf_op jit(solution)/shard_map/ppermute | solution.py:26
  42.5 6.0 %all_to_all.60 = f32[4,1,2048]{2,1,0:T(1,128)S(1)} all-to-all(f32[4,1,2048]{2,1,0:T(1,128)S(1)} %reshape.985), channel_id=1, replica_groups=mesh['gx'=8,'gy'=4] {'gy'}, dimensions={0} | all-to-all | bytes 65536 | tf_op jit(solution)/shard_map/all_to_all | solution.py:121
  48.4 0.7 reduce.13
  49.8 9.9 %while.21 = (s32[]{:T(128)}, f32[1,2,128,32]{2,3,1,0:T(8,128)S(1)}, f32[1,2,128,32]{2,3,1,0:T(8,128)S(1)}, f32[2]{0:T(128)S(1)}, f32[2]{0:T(128)S(1)}, /*index=5...) while((s32[]{:T(128)}, f32[1,2,128,32]{2,3,1,0:T(8,128)S(1)}, f32[1,2,128,32]{2,3,1,0:T(8,128)S(1)}, ...), condition=%wide.region_6.7_spmd, body=%wide.region_5.6_spmd.sunk | while | flops 12607618 | bytes 202597 | solution.py:85
  50.4 0.4 convolution_bitcast_fusion.7
  51.3 0.4 convolution_bitcast_fusion.7
  52.2 0.4 convolution_bitcast_fusion.7
  53.1 0.4 convolution_bitcast_fusion.7
  54.0 0.4 convolution_bitcast_fusion.7
  54.9 0.4 convolution_bitcast_fusion.7
  55.8 0.4 convolution_bitcast_fusion.7
  60.0 6.0 %all_to_all.61 = f32[4,1,2048]{2,1,0:T(1,128)S(1)} all-to-all(f32[4,1,2048]{2,1,0:T(1,128)S(1)} %reshape.987), channel_id=1, replica_groups=mesh['gx'=8,'gy'=4] {'gy'}, dimensions={0} | all-to-all | bytes 65536 | tf_op jit(solution)/shard_map/all_to_all | solution.py:126
  66.0 0.7 reduce.14
  66.8 2.0 %collective-permute-start.2 = (f32[3,1,64,128]{2,3,1,0:T(8,128)S(1)}, f32[3,1,64,128]{2,3,1,0:T(8,128)S(1)}, u32[]{:S(2)}, u32[]{:S(2)}) collective-permute-start(f32[3,1,64,128]{2,3,1,0:T(8,128)S(1)} %pad_maximum_fusion.9), channel_id=1, source_target_pairs={{4,0},{8,4},{12,8},{16,12},{20,16},{24,20},{28,24},{5,1},{9,5},{13... | collective-permute-start | bytes 294920 | tf_op jit(solution)/shard_map/ppermute | solution.py:27
  68.8 6.6 %collective-permute-start.3 = (f32[3,1,64,128]{2,3,1,0:T(8,128)S(1)}, f32[3,1,64,128]{2,3,1,0:T(8,128)S(1)}, u32[]{:S(2)}, u32[]{:S(2)}) collective-permute-start(f32[3,1,64,128]{2,3,1,0:T(8,128)S(1)} %pad_maximum_fusion.9), channel_id=1, source_target_pairs={{0,4},{4,8},{8,12},{12,16},{16,20},{20,24},{24,28},{1,5},{5,9},{9,... | collective-permute-start | bytes 294920 | tf_op jit(solution)/shard_map/ppermute | solution.py:26
  75.7 1.2 %collective-permute-done.2 = f32[3,1,64,128]{2,3,1,0:T(8,128)S(1)} collective-permute-done((f32[3,1,64,128]{2,3,1,0:T(8,128)S(1)}, f32[3,1,64,128]{2,3,1,0:T(8,128)S(1)}, u32[]{:S(2)}, u32[]{:S(2)}) %collective-permute-start.2) | collective-permute-done | bytes 98336 | tf_op jit(solution)/shard_map/ppermute | solution.py:27
  76.9 1.2 %collective-permute-done.3 = f32[3,1,64,128]{2,3,1,0:T(8,128)S(1)} collective-permute-done((f32[3,1,64,128]{2,3,1,0:T(8,128)S(1)}, f32[3,1,64,128]{2,3,1,0:T(8,128)S(1)}, u32[]{:S(2)}, u32[]{:S(2)}) %collective-permute-start.3) | collective-permute-done | bytes 98336 | tf_op jit(solution)/shard_map/ppermute | solution.py:26
  78.2 0.7 copy.94
  78.9 0.7 copy.95
  (237 shorter events, 15.9 us)
Async XLA Ops:
  2.2 4.4 %copy-start.5 = (f32[2]{0:T(128)S(1)}, f32[2]{0:T(128)}, u32[]{:S(2)}) copy-start(f32[2]{0:T(128)} %param.20) | copy-start | bytes 28
  2.2 5.1 %copy-start.2 = (bf16[2,1,64,128]{3,2,1,0:T(8,128)(2,1)S(1)}, bf16[2,1,64,128]{3,2,1,0:T(8,128)(2,1)}, u32[]{:S(2)}) copy-start(bf16[2,1,64,128]{3,2,1,0:T(8,128)(2,1)} %param.15) | copy-start | bytes 98308
  2.2 8.0 %all-to-all-start = ((f32[4,1,2048]{2,1,0:T(1,128)}), f32[4,1,2048]{2,1,0:T(1,128)S(1)}, u32[]{:S(2)}, u32[]{:S(2)}) async-start(f32[4,1,2048]{2,1,0:T(1,128)} %reshape.981), calls=%async_computation | async-start | bytes 65536 | tf_op jit(solution)/shard_map/all_to_all | solution.py:121
  6.6 0.7 copy-start.6
  7.3 0.8 copy-start.3
  9.3 0.7 copy-start.4
  9.4 0.7 copy-start.7
  11.6 0.9 %copy-start = (f32[2,128,128]{2,1,0:T(8,128)S(1)}, f32[2,128,128]{2,1,0:T(8,128)}, u32[]{:S(2)}) copy-start(f32[2,128,128]{2,1,0:T(8,128)} %param.21) | copy-start | bytes 393220
  23.6 7.2 %all-to-all-start.1 = ((f32[4,1,2048]{2,1,0:T(1,128)}), f32[4,1,2048]{2,1,0:T(1,128)S(1)}, u32[]{:S(2)}, u32[]{:S(2)}) async-start(f32[4,1,2048]{2,1,0:T(1,128)} %reshape.983), calls=%async_computation.1 | async-start | bytes 65536 | tf_op jit(solution)/shard_map/all_to_all | solution.py:126
  31.7 9.3 %collective-permute-start = (f32[3,1,64,128]{2,3,1,0:T(8,128)S(1)}, f32[3,1,64,128]{2,3,1,0:T(8,128)S(1)}, u32[]{:S(2)}, u32[]{:S(2)}) collective-permute-start(f32[3,1,64,128]{2,3,1,0:T(8,128)S(1)} %pad_maximum_fusion.8), channel_id=1, source_target_pairs={{4,0},{8,4},{12,8},{16,12},{20,16},{24,20},{28,24},{5,1},{9,5},{13... | collective-permute-start | bytes 294920 | tf_op jit(solution)/shard_map/ppermute | solution.py:27
  36.5 5.7 %collective-permute-start.1 = (f32[3,1,64,128]{2,3,1,0:T(8,128)S(1)}, f32[3,1,64,128]{2,3,1,0:T(8,128)S(1)}, u32[]{:S(2)}, u32[]{:S(2)}) collective-permute-start(f32[3,1,64,128]{2,3,1,0:T(8,128)S(1)} %pad_maximum_fusion.8), channel_id=1, source_target_pairs={{0,4},{4,8},{8,12},{12,16},{16,20},{20,24},{24,28},{1,5},{5,9},{9,... | collective-permute-start | bytes 294920 | tf_op jit(solution)/shard_map/ppermute | solution.py:26
  39.8 0.8 copy-start.1
  66.8 10.0 %collective-permute-start.2 = (f32[3,1,64,128]{2,3,1,0:T(8,128)S(1)}, f32[3,1,64,128]{2,3,1,0:T(8,128)S(1)}, u32[]{:S(2)}, u32[]{:S(2)}) collective-permute-start(f32[3,1,64,128]{2,3,1,0:T(8,128)S(1)} %pad_maximum_fusion.9), channel_id=1, source_target_pairs={{4,0},{8,4},{12,8},{16,12},{20,16},{24,20},{28,24},{5,1},{9,5},{13... | collective-permute-start | bytes 294920 | tf_op jit(solution)/shard_map/ppermute | solution.py:27
  68.8 9.2 %collective-permute-start.3 = (f32[3,1,64,128]{2,3,1,0:T(8,128)S(1)}, f32[3,1,64,128]{2,3,1,0:T(8,128)S(1)}, u32[]{:S(2)}, u32[]{:S(2)}) collective-permute-start(f32[3,1,64,128]{2,3,1,0:T(8,128)S(1)} %pad_maximum_fusion.9), channel_id=1, source_target_pairs={{0,4},{4,8},{8,12},{12,16},{16,20},{20,24},{24,28},{1,5},{5,9},{9,... | collective-permute-start | bytes 294920 | tf_op jit(solution)/shard_map/ppermute | solution.py:26
where the time goes:
time: 80.4 us; the launch traced here: 79.6 us
  starting transfers between devices  24.5 us (30%)
  local copies, waits for them, and re-layouts  19.2 us (24%)
  blocking collectives  11.9 us (15%)
  matrix products  8.49 us (11%)
  waiting for transfers between devices  7.58 us (9%)
  other arithmetic  5.04 us (6%)
  between operations  2.16 us (3%)
    ppermute x2, starting transfers between devices, with_halo(): before = lax.ppermute(last, axis, up)  9.73 us
    dot_general x22, matrix products, sweep_once(): jnp.einsum('bij,xbjy->xbiy', block_inverse, shaped + coupling, precision=...  7.89 us
    unnamed x32, local copies, waits for them, and re-layouts  7.66 us
    ppermute x2, starting transfers between devices, with_halo(): after = lax.ppermute(leading, axis, down)  6.77 us
    all_to_all x1, blocking collectives, per_device(): lax.all_to_all(outgoing, 'gy', split_axis=3, concat_axis=1, tiled=True)  5.96 us
    all_to_all x1, blocking collectives, per_device(): lax.all_to_all(returned_form, 'gy', split_axis=1, concat_axis=3, tiled=True)  5.96 us
    concatenate x88, local copies, waits for them, and re-layouts, sweep_once(): jnp.concatenate([from_below[:, :, None, :], middle, from_above[:, :, None...  5.81 us
    all_to_all x1, starting transfers between devices, per_device(): lax.all_to_all(outgoing, 'gy', split_axis=3, concat_axis=1, tiled=True)  4.4 us
  transfers between devices with their start and end apart: 6, of which 5 were waited for; matrix products, arithmetic and copies ran while one was open for 2% of the time, Pallas kernels for 0%

commit v1 on v0

v1 whole, which is shorter than its diff:
```python
import jax
import jax.numpy as jnp
from jax import lax
from jax.experimental import pallas as pl
from jax.experimental.pallas import tpu as pltpu
from jax.sharding import PartitionSpec as P

STEPS = 2
SWEEPS = 11
ZB = 128
LB = 128
HB = 64

TIME_STEP = 0.2
RECOVERY_RATE = 0.25
EXCITATION = 8.0
THRESHOLD = 0.15

VMEM = pl.BlockSpec(memory_space=pltpu.VMEM)
SMEM = pl.BlockSpec(memory_space=pltpu.SMEM)


def half_product(field, inv_ref):
    me = lax.axis_index("gy")
    upper = lax.rem(me, 2) == 1
    matrix = inv_ref[lax.div(me, 2)]
    nothing = jnp.zeros_like(field)
    padded = jnp.concatenate(
        [jnp.where(upper, nothing, field), jnp.where(upper, field, nothing)], axis=0
    )
    product = jnp.dot(
        matrix, padded, precision=lax.Precision.HIGHEST, preferred_element_type=jnp.float32
    )
    own = jnp.where(upper, product[HB:], product[:HB])
    inner = jnp.where(upper, product[HB - 1 : HB], product[HB : HB + 1])
    outer = jnp.where(upper, product[ZB - 1 :], product[:1])
    return own, inner, outer


def write_product(field, inv_ref, own_ref, edge_ref):
    own, inner, outer = half_product(field, inv_ref)
    own_ref[...] = own
    row = lax.broadcasted_iota(jnp.int32, edge_ref.shape, 0)
    edge_ref[...] = jnp.where(row == 0, inner, jnp.where(row == 1, outer, 0.0))


def start_kernel(field_ref, inv_ref, own_ref, edge_ref):
    write_product(field_ref[...], inv_ref, own_ref, edge_ref)


def solved_half(own, edges, inv_ref, rate_ref):
    me = lax.axis_index("gy")
    upper = lax.rem(me, 2) == 1
    mine = lax.div(me, 2)
    blocks = inv_ref.shape[0]
    first, last, corner = [], [], []
    for block in range(blocks):
        low = edges[lax.bitwise_xor(2 * block, me)]
        high = edges[lax.bitwise_xor(2 * block + 1, me)]
        top, bottom = inv_ref[block, 0:1], inv_ref[block, ZB - 1 : ZB]
        mid_low, mid_high = inv_ref[block, HB - 1 : HB], inv_ref[block, HB : HB + 1]
        reach_first = top[:, HB : HB + 1] / mid_low[:, HB : HB + 1]
        reach_last = bottom[:, HB - 1 : HB] / mid_high[:, HB - 1 : HB]
        first.append(low[1:2] + reach_first * high[0:1])
        last.append(high[1:2] + reach_last * low[0:1])
        corner.append((top[:, 0:1], top[:, ZB - 1 :], bottom[:, 0:1], bottom[:, ZB - 1 :]))
    zero = jnp.zeros_like(first[0])

    def couple(u_first, u_last):
        below = [zero] + [
            jnp.minimum(rate_ref[b], rate_ref[b + 1]) * u_last[b] for b in range(blocks - 1)
        ]
        above = [
            jnp.minimum(rate_ref[b], rate_ref[b + 1]) * u_first[b + 1] for b in range(blocks - 1)
        ] + [zero]
        return below, above

    u_first, u_last = first, last
    for _ in range(SWEEPS - 1):
        below, above = couple(u_first, u_last)
        u_first = [
            first[b] + corner[b][0] * below[b] + corner[b][1] * above[b] for b in range(blocks)
        ]
        u_last = [
            last[b] + corner[b][2] * below[b] + corner[b][3] * above[b] for b in range(blocks)
        ]
    below, above = couple(u_first, u_last)
    from_below, from_above = below[0], above[0]
    for b in range(1, blocks):
        from_below = jnp.where(mine == b, below[b], from_below)
        from_above = jnp.where(mine == b, above[b], from_above)
    rows = inv_ref[mine, pl.ds(pl.multiple_of(lax.rem(me, 2) * HB, HB), HB), :]
    partner = edges[1][0:1]
    middle = inv_ref[mine, HB - 1 : HB + 1]
    bridge = jnp.where(upper, middle[1:2, HB - 1 : HB], middle[0:1, HB : HB + 1])
    across = jnp.where(upper, rows[:, HB - 1 : HB], rows[:, HB : HB + 1])
    return (
        own
        + across * (partner / bridge)
        + rows[:, 0:1] * from_below
        + rows[:, ZB - 1 :] * from_above
    )


def region_fields(label_ref, axial_ref, shear_ref, width):
    parts = []
    for block in range(width // LB):
        label = jnp.broadcast_to(label_ref[:, block : block + 1], (HB, LB))
        along = jnp.zeros((HB, LB), jnp.float32)
        across, shear = along, along
        for region in range(1, axial_ref.shape[1]):
            here = label == region
            along = jnp.where(here, axial_ref[0, region], along)
            across = jnp.where(here, axial_ref[1, region], across)
            shear = jnp.where(here, shear_ref[region], shear)
        parts.append(((label > 0).astype(jnp.float32), along, across, shear))
    return [jnp.concatenate(p, axis=1) if len(p) > 1 else p[0] for p in zip(*parts)]


def y_neighbours(field):
    width = field.shape[1]
    lane = lax.broadcasted_iota(jnp.int32, field.shape, 1)
    below = jnp.where(lane == 0, 0.0, pltpu.roll(field, 1, 1))
    above = jnp.where(lane == width - 1, 0.0, pltpu.roll(field, width - 1, 1))
    return below, above


def step_kernel(
    count, step, own_ref, *refs
):
    edge_refs = refs[:count]
    (inv_ref, rate_ref, label_ref, axial_ref, shear_ref, voltage_ref, gating_ref, w_ref) = refs[
        count : count + 8
    ]
    stay_ref, pair_ref, next_ref, w_out_ref, edges = refs[count + 8 :]
    for d in range(count):
        edges[d] = edge_refs[d][...]
    solved = solved_half(own_ref[...], edges, inv_ref, rate_ref)
    tissue, along, across, shear = region_fields(label_ref, axial_ref, shear_ref, solved.shape[1])
    voltage = voltage_ref[step].astype(jnp.float32)
    gating = gating_ref[step].astype(jnp.float32)
    slope = (
        EXCITATION
        * (-3.0 * voltage * voltage + 2.0 * (1.0 + THRESHOLD) * voltage - THRESHOLD)
        - gating
    )
    w = w_ref[...]
    flux_x = along * solved
    flux_y = across * solved
    y_below, y_above = y_neighbours(flux_y)
    s_below, s_above = y_neighbours(shear * solved)
    twist = 0.5 * (s_above - s_below)
    spread = y_above - 2.0 * flux_y + y_below - 2.0 * flux_x
    stay_ref[...] = tissue * (
        solved
        + TIME_STEP * spread
        + TIME_STEP * slope * solved
        + TIME_STEP * RECOVERY_RATE * EXCITATION * w
    )
    w_out_ref[...] = tissue * (
        (1.0 - TIME_STEP * RECOVERY_RATE) * w - TIME_STEP * voltage * solved
    )
    even = lax.rem(lax.axis_index("gx"), 2) == 0
    twist = jnp.where(even, -twist, twist)
    pair_ref[...] = TIME_STEP * (flux_x + twist)
    next_ref[...] = TIME_STEP * (flux_x - twist)


def labelled_tissue(label_ref, width):
    parts = [
        jnp.broadcast_to(label_ref[:, b : b + 1], (HB, LB)) > 0 for b in range(width // LB)
    ]
    return jnp.concatenate(parts, axis=1) if len(parts) > 1 else parts[0]


def joined(stay_ref, a_ref, b_ref, label_ref):
    here = labelled_tissue(label_ref, stay_ref.shape[1])
    return stay_ref[...] + jnp.where(here, a_ref[...] + b_ref[...], 0.0)


def between_kernel(stay_ref, a_ref, b_ref, label_ref, inv_ref, own_ref, edge_ref):
    write_product(joined(stay_ref, a_ref, b_ref, label_ref), inv_ref, own_ref, edge_ref)


def end_kernel(stay_ref, a_ref, b_ref, label_ref, out_ref):
    out_ref[...] = joined(stay_ref, a_ref, b_ref, label_ref)


def per_device(
    adj_voltage,
    adj_gating,
    fwd_voltage,
    fwd_gating,
    region_labels,
    region_axial,
    region_shear,
    block_rate,
    block_inverse,
):
    lanes, lines = lax.axis_size("gy"), lax.axis_size("gx")
    _, depth, width = adj_voltage.shape
    assert depth == HB and block_inverse.shape[1] == ZB
    f32 = jnp.float32
    plane = jax.ShapeDtypeStruct((HB, width), f32)
    edge = jax.ShapeDtypeStruct((8, width), f32)
    labels = region_labels[0]
    voltage, gating = fwd_voltage[:, 0], fwd_gating[:, 0]
    own, edges = pl.pallas_call(
        start_kernel, out_shape=(plane, edge), in_specs=[VMEM] * 2, out_specs=(VMEM, VMEM)
    )(adj_voltage[0], block_inverse)
    w = adj_gating[0]
    pair = [(i, i ^ 1) for i in range(lines)]
    after = [(i, j) for a in range(1, lines - 1, 2) for i, j in ((a, a + 1), (a + 1, a))]
    for step_index in range(STEPS):
        later = STEPS - 1 - step_index
        all_edges = [edges] + [
            lax.ppermute(edges, "gy", [(i, i ^ d) for i in range(lanes)]) for d in range(1, lanes)
        ]
        stay, to_pair, to_next, w = pl.pallas_call(
            lambda *refs: step_kernel(lanes, later, *refs),
            out_shape=(plane,) * 4,
            in_specs=[VMEM] * (lanes + 2)
            + [SMEM, VMEM, SMEM, SMEM]
            + [VMEM] * 3,
            out_specs=(VMEM,) * 4,
            scratch_shapes=[pltpu.VMEM((lanes, 8, width), f32)],
        )(
            own,
            *all_edges,
            block_inverse,
            block_rate,
            labels,
            region_axial,
            region_shear,
            voltage,
            gating,
            w,
        )
        a = lax.ppermute(to_pair, "gx", pair)
        b = lax.ppermute(to_next, "gx", after)
        if step_index < STEPS - 1:
            own, edges = pl.pallas_call(
                between_kernel, out_shape=(plane, edge), in_specs=[VMEM] * 5, out_specs=(VMEM, VMEM)
            )(stay, a, b, labels, block_inverse)
    out = pl.pallas_call(
        end_kernel, out_shape=plane, in_specs=[VMEM] * 4, out_specs=VMEM
    )(stay, a, b, labels)
    return (out[None], w[None])


def solution(mesh):
    return jax.shard_map(
        per_device,
        mesh=mesh,
        in_specs=(
            P("gx", "gy", None),
            P("gx", "gy", None),
            P(None, "gx", "gy", None),
            P(None, "gx", "gy", None),
            P("gx", "gy", None),
            P(),
            P(),
            P(),
            P(),
        ),
        out_specs=(P("gx", "gy", None), P("gx", "gy", None)),
        check_vma=False,
    )
```

time: 80.4 us -> 36.6 us (0.46)
  local copies, waits for them, and re-layouts: 19.2 us -> 3.13 us
  blocking collectives: 11.9 us -> 0 us
  Pallas kernels: 0 us -> 8.8 us
  matrix products: 8.49 us -> 0 us
  starting transfers between devices: 24.5 us -> 16.5 us
  other arithmetic: 5.04 us -> 0 us
  between operations: 2.16 us -> 0.7 us
    all_to_all x2 -> x0, blocking collectives: 11.9 us -> none  [the longest x1 5.96 us: per_device(): lax.all_to_all(outgoing, 'gy', split_axis=3, concat_axis=1, tiled=True)]
    pallas_call x0 -> x5, Pallas kernels: none -> 8.8 us  [the longest x2 3.68 us: per_device(): pl.pallas_call(lambda *refs: step_kernel(lanes, later, *refs), out_shape=...]
    dot_general x24 -> x0, matrix products: 8.49 us -> none  [the longest x22 7.89 us: sweep_once(): jnp.einsum('bij,xbjy->xbiy', block_inverse, shaped + coupling, precision=...]
    all_to_all x2 -> x0, starting transfers between devices: 8.01 us -> none  [the longest x1 4.4 us: per_device(): lax.all_to_all(outgoing, 'gy', split_axis=3, concat_axis=1, tiled=True)]
    concatenate x88 -> x0, local copies, waits for them, and re-layouts: 5.81 us -> none  [sweep_once(): jnp.concatenate([from_below[:, :, None, :], middle, from_above[:, :, None...]
    unnamed x32 -> x22, local copies, waits for them, and re-layouts: 7.66 us -> 2.41 us
    slice x70 -> x0, local copies, waits for them, and re-layouts: 4.33 us -> none  [the longest x22 3.58 us: sweep_once(): last_cells = current[:, :, ZB - 1, :]]
    all_to_all x2 -> x0, waiting for transfers between devices: 3.63 us -> none  [the longest x1 3.6 us: per_device(): lax.all_to_all(returned_form, 'gy', split_axis=1, concat_axis=3, tiled=True)]
  transfers between devices with their start and end apart: 6 -> 10, of which waited for: 5 -> 7; matrix products, arithmetic and copies ran while one was open for 2% -> 2% of each run, Pallas kernels for 0% -> 0%
where the time goes in v1:
time: 36.6 us; the launch traced here: 36.3 us
  starting transfers between devices  16.5 us (45%)
  Pallas kernels  8.8 us (24%)
  waiting for transfers between devices  7.17 us (20%)
  local copies, waits for them, and re-layouts  3.13 us (9%)
  between operations  0.7 us (2%)
    ppermute x2, starting transfers between devices, per_device(): b = lax.ppermute(to_next, 'gx', after)  8.1 us
    ppermute x6, starting transfers between devices, per_device(): lax.ppermute(edges, 'gy', [(i, i ^ d) for i in range(lanes)])  5.99 us
    ppermute x2, waiting for transfers between devices, per_device(): b = lax.ppermute(to_next, 'gx', after)  4.08 us
    pallas_call x2, Pallas kernels, per_device(): pl.pallas_call(lambda *refs: step_kernel(lanes, later, *refs), out_shape=...  3.68 us
    ppermute x6, waiting for transfers between devices, per_device(): lax.ppermute(edges, 'gy', [(i, i ^ d) for i in range(lanes)])  3.09 us
    unnamed x22, local copies, waits for them, and re-layouts  2.41 us
    ppermute x2, starting transfers between devices, per_device(): a = lax.ppermute(to_pair, 'gx', pair)  2.39 us
    pallas_call x1, Pallas kernels, per_device(): pl.pallas_call(between_kernel, out_shape=(plane, edge), in_specs=[VMEM] *...  1.88 us
  transfers between devices with their start and end apart: 10, of which 7 were waited for; matrix products, arithmetic and copies ran while one was open for 2% of the time, Pallas kernels for 0%

profile of v1, /device:TPU:1, one launch (start us, length us, event | category | flops | bytes accessed | tf_op | source)
XLA Modules:
  0.0 36.3 jit_solution(9611195995689060227)
XLA Ops:
  0.6 1.7 %shard_map.104 = (f32[64,128]{1,0:T(8,128)}, f32[8,128]{1,0:T(8,128)}) custom-call(f32[64,128]{1,0:T(8,128)} %bitcast.11, f32[2,128,128]{2,1,0:T(8,128)} %refs_5_.3), custom_call_target="tpu_custom_call" | custom-call | tf_op jit(solution)/shard_map/pallas_call | solution.py:208
  2.4 0.0 copy-start.10
  2.4 3.0 %collective-permute-start.2 = (f32[8,128]{1,0:T(8,128)}, f32[8,128]{1,0:T(8,128)S(1)}, u32[]{:S(2)}, u32[]{:S(2)}) collective-permute-start(f32[8,128]{1,0:T(8,128)} %get-tuple-element.15.refs_1_), channel_id=1, source_target_pairs={{0,3},{1,2},{2,1},{3,0},{4,7},{5,6},{6,5},{7,4},{8,11},{9,10},{10,... | collective-permute-start | bytes 12296 | tf_op jit(solution)/shard_map/ppermute | solution.py:217
  5.4 0.2 collective-permute-start.1
  5.6 0.1 collective-permute-start
  5.7 0.0 copy-done.10
  5.7 0.7 %copy.11.refs_7_.label_ref = s32[64,1]{1,0:T(8,128)} copy(s32[64,1]{0,1:T(1,128)S(1)} %bitcast.14) | data formatting | bytes 512 | tf_op jit(solution)/shard_map/squeeze | solution.py:206
  6.4 0.1 collective-permute-done.2.refs_4_
  6.6 0.0 copy-start.5
  6.6 1.5 %collective-permute-done.1.refs_3_ = f32[8,128]{1,0:T(8,128)S(1)} collective-permute-done((f32[8,128]{1,0:T(8,128)}, f32[8,128]{1,0:T(8,128)S(1)}, u32[]{:S(2)}, u32[]{:S(2)}) %collective-permute-start.1) | collective-permute-done | bytes 4128 | tf_op jit(solution)/shard_map/ppermute | solution.py:217
  8.0 0.0 copy-start.7
  8.0 0.2 collective-permute-done.refs_2_
  8.3 0.0 copy-start.9
  8.3 0.0 copy-done.5
  8.3 0.4 copy-done.7
  8.6 0.2 copy-done.9
  8.9 1.8 %shard_map.105 = (f32[64,128]{1,0:T(8,128)}, f32[64,128]{1,0:T(8,128)}, f32[64,128]{1,0:T(8,128)}, f32[64,128]{1,0:T(8,128)}) custom-call(f32[64,128]{1,0:T(8,128)} %get-tuple-element.14.refs_0_, f32[8,128]{1,0:T(8,128)} %get-tuple-element.15.refs_1_, f32[8,128]{1,0:T(8,128)} %copy-done.9, f32[8,128]{1,0:T(8,128)} %copy-done.7, f32[8,128]{1,0:T(8,128)} %copy-done.5, ...), custom_call_target="tpu_custom_call" | custom-call | tf_op jit(solution)/shard_map/pallas_call | solution.py:219
  10.7 2.4 %collective-permute-start.3 = (f32[64,128]{1,0:T(8,128)}, f32[64,128]{1,0:T(8,128)S(1)}, u32[]{:S(2)}, u32[]{:S(2)}) collective-permute-start(f32[64,128]{1,0:T(8,128)} %get-tuple-element.17), channel_id=1, source_target_pairs={{0,4},{4,0},{8,12},{12,8},{16,20},{20,16},{24,28},{28,24},{1,5},{5... | collective-permute-start | bytes 98312 | tf_op jit(solution)/shard_map/ppermute | solution.py:239
  13.1 3.1 %collective-permute-start.4 = (f32[64,128]{1,0:T(8,128)}, f32[64,128]{1,0:T(8,128)S(1)}, u32[]{:S(2)}, u32[]{:S(2)}) collective-permute-start(f32[64,128]{1,0:T(8,128)} %get-tuple-element.18), channel_id=1, source_target_pairs={{4,8},{8,4},{12,16},{16,12},{20,24},{24,20},{5,9},{9,5},{13,17},{1... | collective-permute-start | bytes 98312 | tf_op jit(solution)/shard_map/ppermute | solution.py:240
  16.2 0.0 collective-permute-done.3.a_ref
  16.2 0.0 copy-start.2
  16.2 2.3 %collective-permute-done.4.b_ref = f32[64,128]{1,0:T(8,128)S(1)} collective-permute-done((f32[64,128]{1,0:T(8,128)}, f32[64,128]{1,0:T(8,128)S(1)}, u32[]{:S(2)}, u32[]{:S(2)}) %collective-permute-start.4) | collective-permute-done | bytes 32800 | tf_op jit(solution)/shard_map/ppermute | solution.py:240
  18.5 0.0 copy-start.3
  18.5 0.0 copy-done.2
  18.5 0.6 %copy-done.3 = f32[64,128]{1,0:T(8,128)} copy-done((f32[64,128]{1,0:T(8,128)}, f32[64,128]{1,0:T(8,128)S(1)}, u32[]{:S(2)}) %copy-start.3) | copy-done | bytes 32792
  19.1 1.9 %shard_map.106 = (f32[64,128]{1,0:T(8,128)}, f32[8,128]{1,0:T(8,128)}) custom-call(f32[64,128]{1,0:T(8,128)} %get-tuple-element.16.stay_ref, f32[64,128]{1,0:T(8,128)} %copy-done.2, f32[64,128]{1,0:T(8,128)} %copy-done.3, s32[64,1]{1,0:T(8,128)} %copy.11.refs_7_.label_ref, f32[2,128,128]{2,1,0:T(8,128)} %refs_5_.3), custom_call_target="tpu_custom_call" | custom-call | tf_op jit(solution)/shard_map/pallas_call | solution.py:242
  21.0 1.2 %collective-permute-start.7 = (f32[8,128]{1,0:T(8,128)}, f32[8,128]{1,0:T(8,128)S(1)}, u32[]{:S(2)}, u32[]{:S(2)}) collective-permute-start(f32[8,128]{1,0:T(8,128)} %get-tuple-element.20.refs_1_), channel_id=1, source_target_pairs={{0,3},{1,2},{2,1},{3,0},{4,7},{5,6},{6,5},{7,4},{8,11},{9,10},{10,... | collective-permute-start | bytes 12296 | tf_op jit(solution)/shard_map/ppermute | solution.py:217
  22.2 0.0 collective-permute-start.6
  22.2 1.4 %collective-permute-start.5 = (f32[8,128]{1,0:T(8,128)}, f32[8,128]{1,0:T(8,128)S(1)}, u32[]{:S(2)}, u32[]{:S(2)}) collective-permute-start(f32[8,128]{1,0:T(8,128)} %get-tuple-element.20.refs_1_), channel_id=1, source_target_pairs={{0,1},{1,0},{2,3},{3,2},{4,5},{5,4},{6,7},{7,6},{8,9},{9,8},{10,11... | collective-permute-start | bytes 12296 | tf_op jit(solution)/shard_map/ppermute | solution.py:217
  23.7 0.9 %collective-permute-done.7.refs_4_ = f32[8,128]{1,0:T(8,128)S(1)} collective-permute-done((f32[8,128]{1,0:T(8,128)}, f32[8,128]{1,0:T(8,128)S(1)}, u32[]{:S(2)}, u32[]{:S(2)}) %collective-permute-start.7) | collective-permute-done | bytes 4128 | tf_op jit(solution)/shard_map/ppermute | solution.py:217
  24.6 0.0 copy-start.4
  24.6 0.3 collective-permute-done.6.refs_3_
  24.9 0.0 copy-start.6
  24.9 0.0 collective-permute-done.5.refs_2_
  24.9 0.0 copy-start.8
  24.9 0.2 copy-done.4
  25.1 0.3 copy-done.6
  25.5 0.0 copy-done.8
  25.5 1.8 %shard_map.107 = (f32[64,128]{1,0:T(8,128)}, f32[64,128]{1,0:T(8,128)}, f32[64,128]{1,0:T(8,128)}, f32[64,128]{1,0:T(8,128)}) custom-call(f32[64,128]{1,0:T(8,128)} %get-tuple-element.19.refs_0_, f32[8,128]{1,0:T(8,128)} %get-tuple-element.20.refs_1_, f32[8,128]{1,0:T(8,128)} %copy-done.8, f32[8,128]{1,0:T(8,128)} %copy-done.6, f32[8,128]{1,0:T(8,128)} %copy-done.4, ...), custom_call_target="tpu_custom_call" | custom-call | tf_op jit(solution)/shard_map/pallas_call | solution.py:219
  27.4 0.0 collective-permute-start.8
  27.4 5.0 %collective-permute-start.9 = (f32[64,128]{1,0:T(8,128)}, f32[64,128]{1,0:T(8,128)S(1)}, u32[]{:S(2)}, u32[]{:S(2)}) collective-permute-start(f32[64,128]{1,0:T(8,128)} %get-tuple-element.24), channel_id=1, source_target_pairs={{4,8},{8,4},{12,16},{16,12},{20,24},{24,20},{5,9},{9,5},{13,17},{1... | collective-permute-start | bytes 98312 | tf_op jit(solution)/shard_map/ppermute | solution.py:240
  32.4 0.0 collective-permute-done.8.a_ref
  32.4 0.0 copy-start
  32.4 1.8 %collective-permute-done.9.b_ref = f32[64,128]{1,0:T(8,128)S(1)} collective-permute-done((f32[64,128]{1,0:T(8,128)}, f32[64,128]{1,0:T(8,128)S(1)}, u32[]{:S(2)}, u32[]{:S(2)}) %collective-permute-start.9) | collective-permute-done | bytes 32800 | tf_op jit(solution)/shard_map/ppermute | solution.py:240
  34.2 0.0 copy-start.1
  34.2 0.0 copy-done
  34.2 0.6 %copy-done.1 = f32[64,128]{1,0:T(8,128)} copy-done((f32[64,128]{1,0:T(8,128)}, f32[64,128]{1,0:T(8,128)S(1)}, u32[]{:S(2)}) %copy-start.1) | copy-done | bytes 32792
  34.8 1.5 %shard_map.108 = f32[64,128]{1,0:T(8,128)} custom-call(f32[64,128]{1,0:T(8,128)} %get-tuple-element.22.stay_ref, f32[64,128]{1,0:T(8,128)} %copy-done, f32[64,128]{1,0:T(8,128)} %copy-done.1, s32[64,1]{1,0:T(8,128)} %copy.11.refs_7_.label_ref), custom_call_target="tpu_custom_call" | custom-call | tf_op jit(solution)/shard_map/pallas_call | solution.py:245
Async XLA Ops:
  2.4 3.3 %copy-start.10 = (s32[1,64,1]{1,2,0:T(1,128)S(1)}, s32[1,64,1]{1,2,0:T(1,128)}, u32[]{:S(2)}) copy-start(s32[1,64,1]{1,2,0:T(1,128)} %param.13) | copy-start | bytes 772
  2.4 4.2 %collective-permute-start.2 = (f32[8,128]{1,0:T(8,128)}, f32[8,128]{1,0:T(8,128)S(1)}, u32[]{:S(2)}, u32[]{:S(2)}) collective-permute-start(f32[8,128]{1,0:T(8,128)} %get-tuple-element.15.refs_1_), channel_id=1, source_target_pairs={{0,3},{1,2},{2,1},{3,0},{4,7},{5,6},{6,5},{7,4},{8,11},{9,10},{10,... | collective-permute-start | bytes 12296 | tf_op jit(solution)/shard_map/ppermute | solution.py:217
  5.4 2.7 %collective-permute-start.1 = (f32[8,128]{1,0:T(8,128)}, f32[8,128]{1,0:T(8,128)S(1)}, u32[]{:S(2)}, u32[]{:S(2)}) collective-permute-start(f32[8,128]{1,0:T(8,128)} %get-tuple-element.15.refs_1_), channel_id=1, source_target_pairs={{0,2},{1,3},{2,0},{3,1},{4,6},{5,7},{6,4},{7,5},{8,10},{9,11},{10,... | collective-permute-start | bytes 12296 | tf_op jit(solution)/shard_map/ppermute | solution.py:217
  5.6 2.7 %collective-permute-start = (f32[8,128]{1,0:T(8,128)}, f32[8,128]{1,0:T(8,128)S(1)}, u32[]{:S(2)}, u32[]{:S(2)}) collective-permute-start(f32[8,128]{1,0:T(8,128)} %get-tuple-element.15.refs_1_), channel_id=1, source_target_pairs={{0,1},{1,0},{2,3},{3,2},{4,5},{5,4},{6,7},{7,6},{8,9},{9,8},{10,11... | collective-permute-start | bytes 12296 | tf_op jit(solution)/shard_map/ppermute | solution.py:217
  6.6 1.7 %copy-start.5 = (f32[8,128]{1,0:T(8,128)}, f32[8,128]{1,0:T(8,128)S(1)}, u32[]{:S(2)}) copy-start(f32[8,128]{1,0:T(8,128)S(1)} %collective-permute-done.2.refs_4_) | copy-start | bytes 12292
  8.0 0.6 %copy-start.7 = (f32[8,128]{1,0:T(8,128)}, f32[8,128]{1,0:T(8,128)S(1)}, u32[]{:S(2)}) copy-start(f32[8,128]{1,0:T(8,128)S(1)} %collective-permute-done.1.refs_3_) | copy-start | bytes 12292
  8.3 0.6 %copy-start.9 = (f32[8,128]{1,0:T(8,128)}, f32[8,128]{1,0:T(8,128)S(1)}, u32[]{:S(2)}) copy-start(f32[8,128]{1,0:T(8,128)S(1)} %collective-permute-done.refs_2_) | copy-start | bytes 12292
  10.7 5.5 %collective-permute-start.3 = (f32[64,128]{1,0:T(8,128)}, f32[64,128]{1,0:T(8,128)S(1)}, u32[]{:S(2)}, u32[]{:S(2)}) collective-permute-start(f32[64,128]{1,0:T(8,128)} %get-tuple-element.17), channel_id=1, source_target_pairs={{0,4},{4,0},{8,12},{12,8},{16,20},{20,16},{24,28},{28,24},{1,5},{5... | collective-permute-start | bytes 98312 | tf_op jit(solution)/shard_map/ppermute | solution.py:239
  13.1 5.4 %collective-permute-start.4 = (f32[64,128]{1,0:T(8,128)}, f32[64,128]{1,0:T(8,128)S(1)}, u32[]{:S(2)}, u32[]{:S(2)}) collective-permute-start(f32[64,128]{1,0:T(8,128)} %get-tuple-element.18), channel_id=1, source_target_pairs={{4,8},{8,4},{12,16},{16,12},{20,24},{24,20},{5,9},{9,5},{13,17},{1... | collective-permute-start | bytes 98312 | tf_op jit(solution)/shard_map/ppermute | solution.py:240
  16.2 2.3 %copy-start.2 = (f32[64,128]{1,0:T(8,128)}, f32[64,128]{1,0:T(8,128)S(1)}, u32[]{:S(2)}) copy-start(f32[64,128]{1,0:T(8,128)S(1)} %collective-permute-done.3.a_ref) | copy-start | bytes 98308
  18.5 0.6 %copy-start.3 = (f32[64,128]{1,0:T(8,128)}, f32[64,128]{1,0:T(8,128)S(1)}, u32[]{:S(2)}) copy-start(f32[64,128]{1,0:T(8,128)S(1)} %collective-permute-done.4.b_ref) | copy-start | bytes 98308
  21.0 3.6 %collective-permute-start.7 = (f32[8,128]{1,0:T(8,128)}, f32[8,128]{1,0:T(8,128)S(1)}, u32[]{:S(2)}, u32[]{:S(2)}) collective-permute-start(f32[8,128]{1,0:T(8,128)} %get-tuple-element.20.refs_1_), channel_id=1, source_target_pairs={{0,3},{1,2},{2,1},{3,0},{4,7},{5,6},{6,5},{7,4},{8,11},{9,10},{10,... | collective-permute-start | bytes 12296 | tf_op jit(solution)/shard_map/ppermute | solution.py:217
  22.2 2.7 %collective-permute-start.6 = (f32[8,128]{1,0:T(8,128)}, f32[8,128]{1,0:T(8,128)S(1)}, u32[]{:S(2)}, u32[]{:S(2)}) collective-permute-start(f32[8,128]{1,0:T(8,128)} %get-tuple-element.20.refs_1_), channel_id=1, source_target_pairs={{0,2},{1,3},{2,0},{3,1},{4,6},{5,7},{6,4},{7,5},{8,10},{9,11},{10,... | collective-permute-start | bytes 12296 | tf_op jit(solution)/shard_map/ppermute | solution.py:217
  22.2 2.7 %collective-permute-start.5 = (f32[8,128]{1,0:T(8,128)}, f32[8,128]{1,0:T(8,128)S(1)}, u32[]{:S(2)}, u32[]{:S(2)}) collective-permute-start(f32[8,128]{1,0:T(8,128)} %get-tuple-element.20.refs_1_), channel_id=1, source_target_pairs={{0,1},{1,0},{2,3},{3,2},{4,5},{5,4},{6,7},{7,6},{8,9},{9,8},{10,11... | collective-permute-start | bytes 12296 | tf_op jit(solution)/shard_map/ppermute | solution.py:217
  24.6 0.6 %copy-start.4 = (f32[8,128]{1,0:T(8,128)}, f32[8,128]{1,0:T(8,128)S(1)}, u32[]{:S(2)}) copy-start(f32[8,128]{1,0:T(8,128)S(1)} %collective-permute-done.7.refs_4_) | copy-start | bytes 12292
  24.9 0.6 %copy-start.6 = (f32[8,128]{1,0:T(8,128)}, f32[8,128]{1,0:T(8,128)S(1)}, u32[]{:S(2)}) copy-start(f32[8,128]{1,0:T(8,128)S(1)} %collective-permute-done.6.refs_3_) | copy-start | bytes 12292
  24.9 0.6 %copy-start.8 = (f32[8,128]{1,0:T(8,128)}, f32[8,128]{1,0:T(8,128)S(1)}, u32[]{:S(2)}) copy-start(f32[8,128]{1,0:T(8,128)S(1)} %collective-permute-done.5.refs_2_) | copy-start | bytes 12292
  27.4 5.0 %collective-permute-start.8 = (f32[64,128]{1,0:T(8,128)}, f32[64,128]{1,0:T(8,128)S(1)}, u32[]{:S(2)}, u32[]{:S(2)}) collective-permute-start(f32[64,128]{1,0:T(8,128)} %get-tuple-element.23), channel_id=1, source_target_pairs={{0,4},{4,0},{8,12},{12,8},{16,20},{20,16},{24,28},{28,24},{1,5},{5... | collective-permute-start | bytes 98312 | tf_op jit(solution)/shard_map/ppermute | solution.py:239
  27.4 6.8 %collective-permute-start.9 = (f32[64,128]{1,0:T(8,128)}, f32[64,128]{1,0:T(8,128)S(1)}, u32[]{:S(2)}, u32[]{:S(2)}) collective-permute-start(f32[64,128]{1,0:T(8,128)} %get-tuple-element.24), channel_id=1, source_target_pairs={{4,8},{8,4},{12,16},{16,12},{20,24},{24,20},{5,9},{9,5},{13,17},{1... | collective-permute-start | bytes 98312 | tf_op jit(solution)/shard_map/ppermute | solution.py:240
  32.4 1.8 %copy-start = (f32[64,128]{1,0:T(8,128)}, f32[64,128]{1,0:T(8,128)S(1)}, u32[]{:S(2)}) copy-start(f32[64,128]{1,0:T(8,128)S(1)} %collective-permute-done.8.a_ref) | copy-start | bytes 98308
  34.2 0.6 %copy-start.1 = (f32[64,128]{1,0:T(8,128)}, f32[64,128]{1,0:T(8,128)S(1)}, u32[]{:S(2)}) copy-start(f32[64,128]{1,0:T(8,128)S(1)} %collective-permute-done.9.b_ref) | copy-start | bytes 98308

commit v2 on v1

--- a/solution.py
+++ b/solution.py
@@ -16,8 +16,10 @@
 EXCITATION = 8.0
 THRESHOLD = 0.15
 
+BOTH = ("gx", "gy")
 VMEM = pl.BlockSpec(memory_space=pltpu.VMEM)
 SMEM = pl.BlockSpec(memory_space=pltpu.SMEM)
+ROOM = pltpu.CompilerParams(vmem_limit_bytes=8 << 20)
 
 
 def half_product(field, inv_ref):
@@ -175,7 +177,11 @@
 
 def joined(stay_ref, a_ref, b_ref, label_ref):
     here = labelled_tissue(label_ref, stay_ref.shape[1])
-    return stay_ref[...] + jnp.where(here, a_ref[...] + b_ref[...], 0.0)
+    line = lax.axis_index("gx")
+    inside = jnp.logical_and(line > 0, line < lax.axis_size("gx") - 1)
+    return stay_ref[...] + jnp.where(
+        here, a_ref[...] + jnp.where(inside, b_ref[...], 0.0), 0.0
+    )
 
 
 def between_kernel(stay_ref, a_ref, b_ref, label_ref, inv_ref, own_ref, edge_ref):
@@ -184,6 +190,15 @@
 
 def end_kernel(stay_ref, a_ref, b_ref, label_ref, out_ref):
     out_ref[...] = joined(stay_ref, a_ref, b_ref, label_ref)
+
+
+def swaps(lines, lanes, partner):
+    found = []
+    for i in range(lines):
+        for j in range(lanes):
+            k, m = partner(i, j)
+            found.append((i * lanes + j, k * lanes + m))
+    return found
 
 
 def per_device(
@@ -206,15 +221,21 @@
     labels = region_labels[0]
     voltage, gating = fwd_voltage[:, 0], fwd_gating[:, 0]
     own, edges = pl.pallas_call(
-        start_kernel, out_shape=(plane, edge), in_specs=[VMEM] * 2, out_specs=(VMEM, VMEM)
+        start_kernel, out_shape=(plane, edge), in_specs=[VMEM] * 2, out_specs=(VMEM, VMEM), compiler_params=ROOM
     )(adj_voltage[0], block_inverse)
     w = adj_gating[0]
-    pair = [(i, i ^ 1) for i in range(lines)]
-    after = [(i, j) for a in range(1, lines - 1, 2) for i, j in ((a, a + 1), (a + 1, a))]
+    ends = (0, lines - 1)
+    pair = swaps(lines, lanes, lambda i, j: (i ^ 1, j))
+    after = swaps(
+        lines, lanes, lambda i, j: (i, j ^ 1) if i in ends else (i - 1 + 2 * (i % 2), j)
+    )
+    around = [
+        swaps(lines, lanes, lambda i, j: (i, j ^ d)) for d in range(1, lanes)
+    ]
     for step_index in range(STEPS):
         later = STEPS - 1 - step_index
         all_edges = [edges] + [
-            lax.ppermute(edges, "gy", [(i, i ^ d) for i in range(lanes)]) for d in range(1, lanes)
+            lax.ppermute(edges, BOTH, swap) for swap in around
         ]
         stay, to_pair, to_next, w = pl.pallas_call(
             lambda *refs: step_kernel(lanes, later, *refs),
@@ -223,6 +244,7 @@
             + [SMEM, VMEM, SMEM, SMEM]
             + [VMEM] * 3,
             out_specs=(VMEM,) * 4,
+            compiler_params=ROOM,
             scratch_shapes=[pltpu.VMEM((lanes, 8, width), f32)],
         )(
             own,
@@ -236,14 +258,14 @@
             gating,
             w,
         )
-        a = lax.ppermute(to_pair, "gx", pair)
-        b = lax.ppermute(to_next, "gx", after)
+        a = lax.ppermute(to_pair, BOTH, pair)
+        b = lax.ppermute(to_next, BOTH, after)
         if step_index < STEPS - 1:
             own, edges = pl.pallas_call(
-                between_kernel, out_shape=(plane, edge), in_specs=[VMEM] * 5, out_specs=(VMEM, VMEM)
+                between_kernel, out_shape=(plane, edge), in_specs=[VMEM] * 5, out_specs=(VMEM, VMEM), compiler_params=ROOM
             )(stay, a, b, labels, block_inverse)
     out = pl.pallas_call(
-        end_kernel, out_shape=plane, in_specs=[VMEM] * 4, out_specs=VMEM
+        end_kernel, out_shape=plane, in_specs=[VMEM] * 4, out_specs=VMEM, compiler_params=ROOM
     )(stay, a, b, labels)
     return (out[None], w[None])
 

time: 36.6 us -> 28.8 us (0.79)
  the two profiles are of different devices: /device:TPU:1 before, /device:TPU:0 now
where the time goes in v2:
time: 28.8 us; the launch traced here: 28.5 us
  waiting for transfers between devices  10.9 us (38%)
  starting transfers between devices  10.3 us (36%)
  Pallas kernels  3.37 us (12%)
  local copies, waits for them, and re-layouts  3.19 us (11%)
  between operations  0.72 us (2%)
    ppermute x6, starting transfers between devices, per_device(): all_edges = [edges] + [lax.ppermute(edges, BOTH, swap) for swap in around]  8.16 us
    ppermute x6, waiting for transfers between devices, per_device(): all_edges = [edges] + [lax.ppermute(edges, BOTH, swap) for swap in around]  5.09 us
    ppermute x2, waiting for transfers between devices, per_device(): b = lax.ppermute(to_next, BOTH, after)  4.81 us
    unnamed x20, local copies, waits for them, and re-layouts  3.1 us
    pallas_call x2, Pallas kernels, per_device(): pl.pallas_call(lambda *refs: step_kernel(lanes, later, *refs), out_shape=...  2.2 us
    ppermute x2, starting transfers between devices, per_device(): b = lax.ppermute(to_next, BOTH, after)  2.09 us
    ppermute x2, waiting for transfers between devices, per_device(): a = lax.ppermute(to_pair, BOTH, pair)  1 us
    pallas_call x1, Pallas kernels, per_device(): pl.pallas_call(end_kernel, out_shape=plane, in_specs=[VMEM] * 4, out_spec...  0.69 us
  transfers between devices with their start and end apart: 10, of which 9 were waited for; matrix products, arithmetic and copies ran while one was open for 0% of the time, Pallas kernels for 0%

profile of v2, /device:TPU:0, one launch (start us, length us, event | category | flops | bytes accessed | tf_op | source)
XLA Modules:
  0.0 28.5 jit_solution(3724592551848357931)
XLA Ops:
  0.6 0.0 copy-start
  0.6 0.9 %copy-done = f32[2,128,128]{2,1,0:T(8,128)S(1)} copy-done((f32[2,128,128]{2,1,0:T(8,128)S(1)}, f32[2,128,128]{2,1,0:T(8,128)}, u32[]{:S(2)}) %copy-start) | copy-done | bytes 131096
  1.5 0.0 copy-start.4
  1.5 0.8 %copy-done.4 = f32[1,64,128]{2,1,0:T(8,128)S(1)} copy-done((f32[1,64,128]{2,1,0:T(8,128)S(1)}, f32[1,64,128]{2,1,0:T(8,128)}, u32[]{:S(2)}) %copy-start.4) | copy-done | bytes 32792
  2.3 0.0 copy-start.9
  2.3 0.0 copy-start.1
  2.3 0.0 copy-start.3
  2.3 0.2 shard_map.104
  2.5 0.0 copy-start.2
  2.5 4.0 %collective-permute-start.2 = (f32[8,128]{1,0:T(8,128)S(1)}, f32[8,128]{1,0:T(8,128)S(1)}, u32[]{:S(2)}, u32[]{:S(2)}) collective-permute-start(f32[8,128]{1,0:T(8,128)S(1)} %get-tuple-element.15.refs_1_), channel_id=1, source_target_pairs={{0,3},{1,2},{2,1},{3,0},{4,7},{5,6},{6,5},{7,4},{8,11},{9,10},{10,... | collective-permute-start | bytes 12296 | tf_op jit(solution)/shard_map/ppermute | solution.py:238
  6.5 0.5 %collective-permute-start.1 = (f32[8,128]{1,0:T(8,128)S(1)}, f32[8,128]{1,0:T(8,128)S(1)}, u32[]{:S(2)}, u32[]{:S(2)}) collective-permute-start(f32[8,128]{1,0:T(8,128)S(1)} %get-tuple-element.15.refs_1_), channel_id=1, source_target_pairs={{0,2},{1,3},{2,0},{3,1},{4,6},{5,7},{6,4},{7,5},{8,10},{9,11},{10,... | collective-permute-start | bytes 12296 | tf_op jit(solution)/shard_map/ppermute | solution.py:238
  7.0 0.1 collective-permute-start
  7.1 0.0 copy-done.9
  7.1 0.1 copy.11.refs_7_.label_ref
  7.2 0.8 %collective-permute-done.2.refs_4_ = f32[8,128]{1,0:T(8,128)S(1)} collective-permute-done((f32[8,128]{1,0:T(8,128)S(1)}, f32[8,128]{1,0:T(8,128)S(1)}, u32[]{:S(2)}, u32[]{:S(2)}) %collective-permute-start.2) | collective-permute-done | bytes 4128 | tf_op jit(solution)/shard_map/ppermute | solution.py:238
  8.1 2.0 %collective-permute-done.1.refs_3_ = f32[8,128]{1,0:T(8,128)S(1)} collective-permute-done((f32[8,128]{1,0:T(8,128)S(1)}, f32[8,128]{1,0:T(8,128)S(1)}, u32[]{:S(2)}, u32[]{:S(2)}) %collective-permute-start.1) | collective-permute-done | bytes 4128 | tf_op jit(solution)/shard_map/ppermute | solution.py:238
  10.1 0.5 %collective-permute-done.refs_2_ = f32[8,128]{1,0:T(8,128)S(1)} collective-permute-done((f32[8,128]{1,0:T(8,128)S(1)}, f32[8,128]{1,0:T(8,128)S(1)}, u32[]{:S(2)}, u32[]{:S(2)}) %collective-permute-start) | collective-permute-done | bytes 4128 | tf_op jit(solution)/shard_map/ppermute | solution.py:238
  10.6 0.0 copy-start.8
  10.6 0.0 copy-start.6
  10.6 0.0 copy-start.7
  10.6 0.0 copy-done.1
  10.6 0.0 copy-done.3
  10.6 0.0 copy-done.2
  10.6 0.6 %copy-done.8 = f32[8]{0:T(128)S(1)} copy-done((f32[8]{0:T(128)S(1)}, f32[8]{0:T(128)}, u32[]{:S(2)}) %copy-start.8) | copy-done | bytes 56
  11.3 0.0 copy-done.6
  11.3 0.0 copy-done.7
  11.3 0.0 copy-start.5
  11.3 0.8 %copy-done.5 = f32[1,64,128]{2,1,0:T(8,128)S(1)} copy-done((f32[1,64,128]{2,1,0:T(8,128)S(1)}, f32[1,64,128]{2,1,0:T(8,128)}, u32[]{:S(2)}) %copy-start.5) | copy-done | bytes 32792
  12.1 0.8 %shard_map.105 = (f32[64,128]{1,0:T(8,128)S(1)}, f32[64,128]{1,0:T(8,128)S(1)}, f32[64,128]{1,0:T(8,128)S(1)}, f32[64,128]{1,0:T(8,128)S(1)}) custom-call(f32[64,128]{1,0:T(8,128)S(1)} %get-tuple-element.14.refs_0_, f32[8,128]{1,0:T(8,128)S(1)} %get-tuple-element.15.refs_1_, f32[8,128]{1,0:T(8,128)S(1)} %collective-permute-done.refs_2_, ...), custom_call_target="tpu_custom_call" | custom-call | tf_op jit(solution)/shard_map/pallas_call | solution.py:240
  12.9 0.1 collective-permute-start.3
  13.0 0.2 collective-permute-start.4
  13.2 1.0 %collective-permute-done.3.a_ref = f32[64,128]{1,0:T(8,128)S(1)} collective-permute-done((f32[64,128]{1,0:T(8,128)S(1)}, f32[64,128]{1,0:T(8,128)S(1)}, u32[]{:S(2)}, u32[]{:S(2)}) %collective-permute-start.3) | collective-permute-done | bytes 32800 | tf_op jit(solution)/shard_map/ppermute | solution.py:261
  14.2 2.8 %collective-permute-done.4.b_ref = f32[64,128]{1,0:T(8,128)S(1)} collective-permute-done((f32[64,128]{1,0:T(8,128)S(1)}, f32[64,128]{1,0:T(8,128)S(1)}, u32[]{:S(2)}, u32[]{:S(2)}) %collective-permute-start.4) | collective-permute-done | bytes 32800 | tf_op jit(solution)/shard_map/ppermute | solution.py:262
  17.0 0.3 shard_map.106
  17.2 1.6 %collective-permute-start.7 = (f32[8,128]{1,0:T(8,128)S(1)}, f32[8,128]{1,0:T(8,128)S(1)}, u32[]{:S(2)}, u32[]{:S(2)}) collective-permute-start(f32[8,128]{1,0:T(8,128)S(1)} %get-tuple-element.20.refs_1_), channel_id=1, source_target_pairs={{0,3},{1,2},{2,1},{3,0},{4,7},{5,6},{6,5},{7,4},{8,11},{9,10},{10,... | collective-permute-start | bytes 12296 | tf_op jit(solution)/shard_map/ppermute | solution.py:238
  18.8 0.1 collective-permute-start.6
  18.9 1.9 %collective-permute-start.5 = (f32[8,128]{1,0:T(8,128)S(1)}, f32[8,128]{1,0:T(8,128)S(1)}, u32[]{:S(2)}, u32[]{:S(2)}) collective-permute-start(f32[8,128]{1,0:T(8,128)S(1)} %get-tuple-element.20.refs_1_), channel_id=1, source_target_pairs={{0,1},{1,0},{2,3},{3,2},{4,5},{5,4},{6,7},{7,6},{8,9},{9,8},{10,11... | collective-permute-start | bytes 12296 | tf_op jit(solution)/shard_map/ppermute | solution.py:238
  20.8 1.0 %collective-permute-done.7.refs_4_ = f32[8,128]{1,0:T(8,128)S(1)} collective-permute-done((f32[8,128]{1,0:T(8,128)S(1)}, f32[8,128]{1,0:T(8,128)S(1)}, u32[]{:S(2)}, u32[]{:S(2)}) %collective-permute-start.7) | collective-permute-done | bytes 4128 | tf_op jit(solution)/shard_map/ppermute | solution.py:238
  21.8 0.6 %collective-permute-done.6.refs_3_ = f32[8,128]{1,0:T(8,128)S(1)} collective-permute-done((f32[8,128]{1,0:T(8,128)S(1)}, f32[8,128]{1,0:T(8,128)S(1)}, u32[]{:S(2)}, u32[]{:S(2)}) %collective-permute-start.6) | collective-permute-done | bytes 4128 | tf_op jit(solution)/shard_map/ppermute | solution.py:238
  22.4 0.1 collective-permute-done.5.refs_2_
  22.5 1.4 %shard_map.107 = (f32[64,128]{1,0:T(8,128)S(1)}, f32[64,128]{1,0:T(8,128)S(1)}, f32[64,128]{1,0:T(8,128)S(1)}, f32[64,128]{1,0:T(8,128)}) custom-call(f32[64,128]{1,0:T(8,128)S(1)} %get-tuple-element.19.refs_0_, f32[8,128]{1,0:T(8,128)S(1)} %get-tuple-element.20.refs_1_, f32[8,128]{1,0:T(8,128)S(1)} %collective-permute-done.5.refs_2_, ...), custom_call_target="tpu_custom_call" | custom-call | tf_op jit(solution)/shard_map/pallas_call | solution.py:240
  23.9 0.0 collective-permute-start.8
  23.9 1.9 %collective-permute-start.9 = (f32[64,128]{1,0:T(8,128)S(1)}, f32[64,128]{1,0:T(8,128)S(1)}, u32[]{:S(2)}, u32[]{:S(2)}) collective-permute-start(f32[64,128]{1,0:T(8,128)S(1)} %get-tuple-element.24), channel_id=1, source_target_pairs={{0,1},{1,0},{2,3},{3,2},{4,8},{5,9},{6,10},{7,11},{8,4},{9,5},{10,... | collective-permute-start | bytes 98312 | tf_op jit(solution)/shard_map/ppermute | solution.py:262
  25.8 0.0 collective-permute-done.8.a_ref
  25.8 2.0 %collective-permute-done.9.b_ref = f32[64,128]{1,0:T(8,128)S(1)} collective-permute-done((f32[64,128]{1,0:T(8,128)S(1)}, f32[64,128]{1,0:T(8,128)S(1)}, u32[]{:S(2)}, u32[]{:S(2)}) %collective-permute-start.9) | collective-permute-done | bytes 32800 | tf_op jit(solution)/shard_map/ppermute | solution.py:262
  27.8 0.7 %shard_map.108 = f32[64,128]{1,0:T(8,128)} custom-call(f32[64,128]{1,0:T(8,128)S(1)} %get-tuple-element.22.stay_ref, f32[64,128]{1,0:T(8,128)S(1)} %collective-permute-done.8.a_ref, f32[64,128]{1,0:T(8,128)S(1)} %collective-permute-done.9.b_ref, s32[64,1]{1,0:T(8,128)S(1)} %copy.11.refs_7_.label_ref), custom_call_target="tpu_custom_call" | custom-call | tf_op jit(solution)/shard_map/pallas_call | solution.py:267
Async XLA Ops:
  0.6 0.9 %copy-start = (f32[2,128,128]{2,1,0:T(8,128)S(1)}, f32[2,128,128]{2,1,0:T(8,128)}, u32[]{:S(2)}) copy-start(f32[2,128,128]{2,1,0:T(8,128)} %refs_5_.3) | copy-start | bytes 393220
  1.5 0.8 %copy-start.4 = (f32[1,64,128]{2,1,0:T(8,128)S(1)}, f32[1,64,128]{2,1,0:T(8,128)}, u32[]{:S(2)}) copy-start(f32[1,64,128]{2,1,0:T(8,128)} %param.9) | copy-start | bytes 98308
  2.3 4.8 %copy-start.9 = (s32[1,64,1]{1,2,0:T(1,128)S(1)}, s32[1,64,1]{1,2,0:T(1,128)}, u32[]{:S(2)}) copy-start(s32[1,64,1]{1,2,0:T(1,128)} %param.13) | copy-start | bytes 772
  2.3 8.3 %copy-start.1 = (f32[2,128,128]{2,1,0:T(8,128)S(1)}, f32[2,128,128]{2,1,0:T(8,128)}, u32[]{:S(2)}) copy-start(f32[2,128,128]{2,1,0:T(8,128)} %refs_5_.3) | copy-start | bytes 393220
  2.3 8.3 %copy-start.3 = (bf16[2,1,64,128]{3,2,1,0:T(8,128)(2,1)S(1)}, bf16[2,1,64,128]{3,2,1,0:T(8,128)(2,1)}, u32[]{:S(2)}) copy-start(bf16[2,1,64,128]{3,2,1,0:T(8,128)(2,1)} %param.12) | copy-start | bytes 98308
  2.5 8.1 %copy-start.2 = (bf16[2,1,64,128]{3,2,1,0:T(8,128)(2,1)S(1)}, bf16[2,1,64,128]{3,2,1,0:T(8,128)(2,1)}, u32[]{:S(2)}) copy-start(bf16[2,1,64,128]{3,2,1,0:T(8,128)(2,1)} %param.11) | copy-start | bytes 98308
  2.5 5.5 %collective-permute-start.2 = (f32[8,128]{1,0:T(8,128)S(1)}, f32[8,128]{1,0:T(8,128)S(1)}, u32[]{:S(2)}, u32[]{:S(2)}) collective-permute-start(f32[8,128]{1,0:T(8,128)S(1)} %get-tuple-element.15.refs_1_), channel_id=1, source_target_pairs={{0,3},{1,2},{2,1},{3,0},{4,7},{5,6},{6,5},{7,4},{8,11},{9,10},{10,... | collective-permute-start | bytes 12296 | tf_op jit(solution)/shard_map/ppermute | solution.py:238
  6.5 3.6 %collective-permute-start.1 = (f32[8,128]{1,0:T(8,128)S(1)}, f32[8,128]{1,0:T(8,128)S(1)}, u32[]{:S(2)}, u32[]{:S(2)}) collective-permute-start(f32[8,128]{1,0:T(8,128)S(1)} %get-tuple-element.15.refs_1_), channel_id=1, source_target_pairs={{0,2},{1,3},{2,0},{3,1},{4,6},{5,7},{6,4},{7,5},{8,10},{9,11},{10,... | collective-permute-start | bytes 12296 | tf_op jit(solution)/shard_map/ppermute | solution.py:238
  7.0 3.6 %collective-permute-start = (f32[8,128]{1,0:T(8,128)S(1)}, f32[8,128]{1,0:T(8,128)S(1)}, u32[]{:S(2)}, u32[]{:S(2)}) collective-permute-start(f32[8,128]{1,0:T(8,128)S(1)} %get-tuple-element.15.refs_1_), channel_id=1, source_target_pairs={{0,1},{1,0},{2,3},{3,2},{4,5},{5,4},{6,7},{7,6},{8,9},{9,8},{10,11... | collective-permute-start | bytes 12296 | tf_op jit(solution)/shard_map/ppermute | solution.py:238
  10.6 0.7 %copy-start.8 = (f32[8]{0:T(128)S(1)}, f32[8]{0:T(128)}, u32[]{:S(2)}) copy-start(f32[8]{0:T(128)} %refs_9_.3) | copy-start | bytes 100
  10.6 0.7 %copy-start.6 = (f32[2,8]{1,0:T(2,128)S(1)}, f32[2,8]{1,0:T(2,128)}, u32[]{:S(2)}) copy-start(f32[2,8]{1,0:T(2,128)} %refs_8_.3) | copy-start | bytes 196
  10.6 0.7 %copy-start.7 = (f32[2]{0:T(128)S(1)}, f32[2]{0:T(128)}, u32[]{:S(2)}) copy-start(f32[2]{0:T(128)} %refs_6_.3) | copy-start | bytes 28
  11.3 0.8 %copy-start.5 = (f32[1,64,128]{2,1,0:T(8,128)S(1)}, f32[1,64,128]{2,1,0:T(8,128)}, u32[]{:S(2)}) copy-start(f32[1,64,128]{2,1,0:T(8,128)} %param.10) | copy-start | bytes 98308
  12.9 1.3 %collective-permute-start.3 = (f32[64,128]{1,0:T(8,128)S(1)}, f32[64,128]{1,0:T(8,128)S(1)}, u32[]{:S(2)}, u32[]{:S(2)}) collective-permute-start(f32[64,128]{1,0:T(8,128)S(1)} %get-tuple-element.17), channel_id=1, source_target_pairs={{0,4},{1,5},{2,6},{3,7},{4,0},{5,1},{6,2},{7,3},{8,12},{9,13},{10,... | collective-permute-start | bytes 98312 | tf_op jit(solution)/shard_map/ppermute | solution.py:261
  13.0 4.0 %collective-permute-start.4 = (f32[64,128]{1,0:T(8,128)S(1)}, f32[64,128]{1,0:T(8,128)S(1)}, u32[]{:S(2)}, u32[]{:S(2)}) collective-permute-start(f32[64,128]{1,0:T(8,128)S(1)} %get-tuple-element.18), channel_id=1, source_target_pairs={{0,1},{1,0},{2,3},{3,2},{4,8},{5,9},{6,10},{7,11},{8,4},{9,5},{10,... | collective-permute-start | bytes 98312 | tf_op jit(solution)/shard_map/ppermute | solution.py:262
  17.2 4.6 %collective-permute-start.7 = (f32[8,128]{1,0:T(8,128)S(1)}, f32[8,128]{1,0:T(8,128)S(1)}, u32[]{:S(2)}, u32[]{:S(2)}) collective-permute-start(f32[8,128]{1,0:T(8,128)S(1)} %get-tuple-element.20.refs_1_), channel_id=1, source_target_pairs={{0,3},{1,2},{2,1},{3,0},{4,7},{5,6},{6,5},{7,4},{8,11},{9,10},{10,... | collective-permute-start | bytes 12296 | tf_op jit(solution)/shard_map/ppermute | solution.py:238
  18.8 3.6 %collective-permute-start.6 = (f32[8,128]{1,0:T(8,128)S(1)}, f32[8,128]{1,0:T(8,128)S(1)}, u32[]{:S(2)}, u32[]{:S(2)}) collective-permute-start(f32[8,128]{1,0:T(8,128)S(1)} %get-tuple-element.20.refs_1_), channel_id=1, source_target_pairs={{0,2},{1,3},{2,0},{3,1},{4,6},{5,7},{6,4},{7,5},{8,10},{9,11},{10,... | collective-permute-start | bytes 12296 | tf_op jit(solution)/shard_map/ppermute | solution.py:238
  18.9 3.6 %collective-permute-start.5 = (f32[8,128]{1,0:T(8,128)S(1)}, f32[8,128]{1,0:T(8,128)S(1)}, u32[]{:S(2)}, u32[]{:S(2)}) collective-permute-start(f32[8,128]{1,0:T(8,128)S(1)} %get-tuple-element.20.refs_1_), channel_id=1, source_target_pairs={{0,1},{1,0},{2,3},{3,2},{4,5},{5,4},{6,7},{7,6},{8,9},{9,8},{10,11... | collective-permute-start | bytes 12296 | tf_op jit(solution)/shard_map/ppermute | solution.py:238
  23.9 1.9 %collective-permute-start.8 = (f32[64,128]{1,0:T(8,128)S(1)}, f32[64,128]{1,0:T(8,128)S(1)}, u32[]{:S(2)}, u32[]{:S(2)}) collective-permute-start(f32[64,128]{1,0:T(8,128)S(1)} %get-tuple-element.23), channel_id=1, source_target_pairs={{0,4},{1,5},{2,6},{3,7},{4,0},{5,1},{6,2},{7,3},{8,12},{9,13},{10,... | collective-permute-start | bytes 98312 | tf_op jit(solution)/shard_map/ppermute | solution.py:261
  23.9 3.9 %collective-permute-start.9 = (f32[64,128]{1,0:T(8,128)S(1)}, f32[64,128]{1,0:T(8,128)S(1)}, u32[]{:S(2)}, u32[]{:S(2)}) collective-permute-start(f32[64,128]{1,0:T(8,128)S(1)} %get-tuple-element.24), channel_id=1, source_target_pairs={{0,1},{1,0},{2,3},{3,2},{4,8},{5,9},{6,10},{7,11},{8,4},{9,5},{10,... | collective-permute-start | bytes 98312 | tf_op jit(solution)/shard_map/ppermute | solution.py:262

commit v3 on v0

v3 whole, which is shorter than its diff:
```python
import jax
import jax.numpy as jnp
from jax import lax
from jax.experimental import pallas as pl
from jax.experimental.pallas import tpu as pltpu
from jax.sharding import PartitionSpec as P

SWEEPS = 11
ZB = 128
LB = 128
HB = 64
SLOTS = 5

TIME_STEP = 0.2
RECOVERY_RATE = 0.25
EXCITATION = 8.0
THRESHOLD = 0.15

BOTH = ("gx", "gy")
VMEM = pl.BlockSpec(memory_space=pltpu.VMEM)
HBM = pl.BlockSpec(memory_space=pltpu.HBM)
F32 = jnp.float32
EDGE_IN, EDGE_OUT, SUM_IN, SUM_OUT, WEIGHTS, SHARED = 0, 1, 2, 3, 4, 7


def gain(voltage, gating):
    slope = (
        EXCITATION
        * (-3.0 * voltage * voltage + 2.0 * (1.0 + THRESHOLD) * voltage - THRESHOLD)
        - gating
    )
    return 1.0 + TIME_STEP * slope


def first_kernel(
    voltage_in, gating_in, fwd_v_in, fwd_g_in, label_in, axial_in, shear_in, rate_in, inverse_in,
    near, far, fwd_v, fwd_g, w, inverse, axial, shear, rate, label, sems,
):
    pairs = [
        (fwd_v_in, fwd_v), (fwd_g_in, fwd_g), (gating_in, w), (label_in, label),
        (voltage_in, near.at[pl.ds(0, HB)]), (voltage_in, far.at[pl.ds(0, HB)]),
        (inverse_in, inverse), (axial_in, axial), (shear_in, shear), (rate_in, rate),
    ]
    copies = [pltpu.make_async_copy(a, b, sems.at[n]) for n, (a, b) in enumerate(pairs)]
    for copy in copies:
        copy.start()
    for copy in copies[:4]:
        copy.wait()
    later = fwd_v.shape[0] - 1
    near[HB : 2 * HB] = gain(fwd_v[later].astype(F32), fwd_g[later].astype(F32))
    near[2 * HB : 3 * HB] = TIME_STEP * RECOVERY_RATE * EXCITATION * w[...]
    blocks = label.shape[0]
    near[3 * HB :] = jnp.zeros((8, near.shape[1]), F32)
    near[3 * HB : 3 * HB + blocks, 0:HB] = label[...].astype(F32)
    far[HB:] = near[3 * HB :]
    for copy in copies[4:]:
        copy.wait()


def half_vectors(inverse, mine, upper):
    def row(index):
        return inverse[mine, index : index + 1, :]

    bridge = row(HB - 1)[:, HB : HB + 1]
    inner = jnp.where(upper, pltpu.roll(row(HB - 1), HB, 1), row(HB)) / bridge
    outer = jnp.where(upper, pltpu.roll(row(ZB - 1), HB, 1), row(0))
    rows = inverse[mine, pl.ds(pl.multiple_of(jnp.where(upper, HB, 0), HB), HB), :]
    swapped = jnp.where(upper, pltpu.roll(rows, HB, 1), rows)
    inner_column = jnp.where(upper, swapped[:, ZB - 1 :], swapped[:, HB : HB + 1]) / bridge
    outer_column = jnp.where(upper, swapped[:, HB - 1 : HB], swapped[:, 0:1])
    return inner, outer, inner_column, outer_column, bridge, swapped[:, :HB]


def y_shifts(plus, minus):
    width = plus.shape[1]
    lane = lax.broadcasted_iota(jnp.int32, plus.shape, 1)
    return jnp.where(lane == width - 1, 0.0, pltpu.roll(plus, width - 1, 1)) + jnp.where(
        lane == 0, 0.0, pltpu.roll(minus, 1, 1)
    )


def stencil(slot, field, center, coef, sign):
    along, across, shear, tissue = coef
    level = TIME_STEP * (across(slot) * field[slot])
    twist = (0.5 * TIME_STEP * sign) * (
        shear(slot + 1) * field[slot + 1] - shear(slot - 1) * field[slot - 1]
    )
    beside = TIME_STEP * (
        along(slot + 1) * field[slot + 1] + along(slot - 1) * field[slot - 1]
    )
    return center * field[slot] + tissue(slot) * (y_shifts(level + twist, level - twist) + beside)


def centre(gains, slot, coef):
    along, across, _, tissue = coef
    return tissue(slot) * gains - (2.0 * TIME_STEP) * (along(slot) + across(slot))


def coefficients(planes):
    return [lambda slot, k=k: planes[k * SLOTS + slot] for k in range(4)]


def orientation():
    line = lax.axis_index("gx")
    return jnp.where(lax.rem(line, 2) == 0, 1.0, -1.0)


def gather_kernel(
    near, pair, after, two_a, two_b, inverse, axial, shear,
    share, solved, centres, partial, planes, rows,
):
    width = near.shape[1]
    label_blocks = width // LB
    line, last = lax.axis_index("gx"), lax.axis_size("gx") - 1
    me = lax.axis_index("gy")
    upper, mine = lax.rem(me, 2) == 1, lax.div(me, 2)
    even = lax.rem(line, 2) == 0
    ahead = jnp.logical_or(lax.rem(line, 4) == 0, lax.rem(line, 4) == 3)
    inside = {
        1: jnp.logical_and(line > 0, line < last),
        4: jnp.where(even, line + 2 <= last, line >= 2),
        0: jnp.where(even, line >= 2, line + 2 <= last),
    }

    def two(first, part):
        a, b = two_a[part], two_b[part]
        return jnp.where(ahead, a, b) if first else jnp.where(ahead, b, a)

    body, tail = pl.ds(0, HB), pl.ds(HB, 8)
    fields = [two(False, body), after[0:HB], near[0:HB], pair[0:HB], two(True, body)]
    labels = [
        two(False, tail), after[3 * HB :], near[3 * HB :], pair[3 * HB :], two(True, tail),
    ]
    rows[...] = jnp.zeros(rows.shape, F32)
    for slot in range(SLOTS):
        label = labels[slot][:label_blocks, :LB]
        if slot in inside:
            label = jnp.where(inside[slot], label, 0.0)
        rows[slot * label_blocks : (slot + 1) * label_blocks] = label
    label = rows[...]
    zero = jnp.zeros(label.shape, F32)
    tables = [zero, zero, zero]
    for region in range(1, axial.shape[1]):
        here = label == float(region)
        for k, value in enumerate(
            (axial[0:1, region : region + 1], axial[1:2, region : region + 1],
             shear[0:1, region : region + 1])
        ):
            tables[k] = jnp.where(here, value, tables[k])
    tables.append((label > 0.0).astype(F32))
    columns = jnp.concatenate(tables, axis=0).T[:HB]
    count = label.shape[0]
    for k in range(4):
        for slot in range(SLOTS):
            for block in range(label_blocks):
                at = k * count + slot * label_blocks + block
                planes[k * SLOTS + slot, :, block * LB : (block + 1) * LB] = jnp.broadcast_to(
                    columns[:, at : at + 1], (HB, LB)
                )
    coef = coefficients(planes)
    sign = orientation()
    inner, outer, inner_column, outer_column, bridge, own = half_vectors(inverse, mine, upper)
    inner_plane = jnp.broadcast_to(inner_column, (HB, width))
    outer_plane = jnp.broadcast_to(outer_column, (HB, width))
    product = jnp.dot(
        own, jnp.concatenate(fields, axis=1),
        precision=lax.Precision.HIGHEST, preferred_element_type=F32,
    )
    parts = [product[:, slot * width : (slot + 1) * width] for slot in range(SLOTS)]
    share[...] = jnp.zeros(share.shape, F32)

    def total(tile, slot, value):
        share[tile, slot : slot + 1, :] = jnp.sum(value, axis=0, keepdims=True)

    for slot in range(SLOTS):
        solved[slot] = parts[slot]
        total(EDGE_IN, slot, bridge * (inner_plane * fields[slot]))
        total(EDGE_OUT, slot, outer_plane * fields[slot])
    weights = (inner_plane * inner_plane, inner_plane * outer_plane, outer_plane * outer_plane)
    sources = {1: after, 2: near, 3: pair}
    for slot in (1, 2, 3):
        gains = sources[slot][HB : 2 * HB]
        lead = sources[slot][2 * HB : 3 * HB]
        center = centre(gains, slot, coef)
        part = stencil(slot, parts, center, coef, sign) + coef[3](slot) * lead
        centres[slot - 1] = center
        partial[slot - 1] = part
        total(SUM_IN, slot, inner_plane * part)
        total(SUM_OUT, slot, outer_plane * part)
        for k, weight in enumerate(weights):
            total(WEIGHTS + k, slot, weight * center)
    if label_blocks == 1:
        lane = lax.broadcasted_iota(jnp.int32, (1, ZB), 1)
        inner = jnp.where(lane < HB, inner, 0.0)
        outer = jnp.where(lane < HB, outer, 0.0)
        vectors = (inner * inner, inner * outer, outer * outer)
        along, across, shears, tissue = tables
        up, down = count - 1, 1
        kinds = (
            across,
            tissue * pltpu.roll(along, up, 0),
            tissue * pltpu.roll(along, down, 0),
            tissue * pltpu.roll(shears, up, 0),
            tissue * pltpu.roll(shears, down, 0),
        )
        lanes = lax.broadcasted_iota(jnp.int32, (8, ZB), 1)
        packed = jnp.zeros((8, ZB), F32)
        for n, kind in enumerate(kinds):
            for k, vector in enumerate(vectors):
                value = jnp.sum(kind * vector, axis=1, keepdims=True)
                packed = jnp.where(lanes == 3 * n + k, value, packed)
        share[SHARED] = packed
    else:
        ones = jnp.ones((HB, width), F32)
        none = jnp.zeros((HB, width), F32)
        for slot in (1, 2, 3):
            here = coef[3](slot)
            kinds = (
                here * y_shifts(coef[1](slot), none),
                here * y_shifts(none, coef[1](slot)),
                here * coef[0](slot + 1),
                here * coef[0](slot - 1),
                here * y_shifts(coef[2](slot + 1), none),
                here * y_shifts(none, coef[2](slot + 1)),
                here * y_shifts(coef[2](slot - 1), none),
                here * y_shifts(none, coef[2](slot - 1)),
            )
            for n, kind in enumerate(kinds):
                for k, weight in enumerate(weights):
                    total(SHARED + 3 * n + k, slot, weight * kind)


def share_tiles(width):
    return SHARED + (1 if width == LB else 24)


def edge_couplings(edge_in, edge_out, inverse, rate, only=None):
    blocks = inverse.shape[0]
    first, last, corner, reach = [], [], [], []
    for b in range(blocks):
        top, bottom = inverse[b, 0:1], inverse[b, ZB - 1 : ZB]
        middle = inverse[b, HB - 1 : HB]
        bridge = middle[:, HB : HB + 1]
        first.append(edge_out[2 * b] + (top[:, HB : HB + 1] / bridge) * edge_in[2 * b + 1])
        last.append(edge_out[2 * b + 1] + (bottom[:, HB - 1 : HB] / bridge) * edge_in[2 * b])
        corner.append((top[:, 0:1], top[:, ZB - 1 :], bottom[:, 0:1], bottom[:, ZB - 1 :]))
        reach.append((middle[:, ZB - 1 :], inverse[b, HB : HB + 1][:, 0:1]))
    links = [jnp.minimum(rate[:, b : b + 1], rate[:, b + 1 : b + 2]) for b in range(blocks - 1)]
    down = [None] + [
        (links[b - 1] * corner[b][0], links[b] * corner[b][1] if b < blocks - 1 else None)
        for b in range(1, blocks)
    ]
    ups = [
        (links[b - 1] * corner[b][2] if b else None, links[b] * corner[b][3])
        for b in range(blocks - 1)
    ]
    u_first, u_last = list(first), list(last)
    for _ in range(SWEEPS - 1):
        n_first, n_last = list(first), list(last)
        for b in range(1, blocks):
            n_first[b] = first[b] + down[b][0] * u_last[b - 1]
            if down[b][1] is not None:
                n_first[b] = n_first[b] + down[b][1] * u_first[b + 1]
        for b in range(blocks - 1):
            n_last[b] = last[b] + ups[b][1] * u_first[b + 1]
            if ups[b][0] is not None:
                n_last[b] = n_last[b] + ups[b][0] * u_last[b - 1]
        u_first, u_last = n_first, n_last
    factors = []
    zero = jnp.zeros_like(first[0])
    for b in range(blocks):
        below = links[b - 1] * u_last[b - 1] if b else zero
        above = links[b] * u_first[b + 1] if b < blocks - 1 else zero
        factors.append((edge_in[2 * b + 1] + reach[b][0] * above, below))
        factors.append((edge_in[2 * b] + reach[b][1] * below, above))
    return factors


def shift_lanes(tile, by):
    width = tile.shape[1]
    lane = lax.broadcasted_iota(jnp.int32, tile.shape, 1)
    if by > 0:
        return jnp.where(lane == width - 1, 0.0, pltpu.roll(tile, width - 1, 1))
    return jnp.where(lane == 0, 0.0, pltpu.roll(tile, 1, 1))


def finish_kernel(halves, *refs):
    shares = refs[:halves]
    (solved, centres, partial, planes, inverse, rate, fwd_v, fwd_g, w_in) = refs[halves : halves + 9]
    out_v, out_w, board = refs[halves + 9 :]
    width = out_v.shape[1]
    me = lax.axis_index("gy")
    upper, mine = lax.rem(me, 2) == 1, lax.div(me, 2)
    sign = orientation()
    for d in range(halves):
        board[d] = shares[d][...]

    def tile(half, which):
        return board[lax.bitwise_xor(half, me), which]

    every = range(halves)
    first = edge_couplings(
        [tile(h, EDGE_IN) for h in every], [tile(h, EDGE_OUT) for h in every], inverse, rate
    )
    _, _, inner_column, outer_column, _, own = half_vectors(inverse, mine, upper)
    inner_plane = jnp.broadcast_to(inner_column, (HB, width))
    outer_plane = jnp.broadcast_to(outer_column, (HB, width))
    coef = coefficients(planes)

    def pick(factors):
        chosen = factors[0]
        for h in range(1, halves):
            chosen = [jnp.where(me == h, new, old) for new, old in zip(factors[h], chosen)]
        return chosen

    alpha, beta = pick(first)
    added = [
        inner_plane * alpha[s : s + 1] + outer_plane * beta[s : s + 1] for s in range(SLOTS)
    ]
    nexts = [
        partial[s - 1] + stencil(s, added, centres[s - 1], coef, sign) for s in (1, 2, 3)
    ]
    product = jnp.dot(
        own, jnp.concatenate(nexts, axis=1),
        precision=lax.Precision.HIGHEST, preferred_element_type=F32,
    )

    rolls = (7, 1)
    sums_in, sums_out = [], []
    half_sign = 0.5 * sign
    for h in every:
        totals = [tile(h, SUM_IN), tile(h, SUM_OUT)]
        if width == LB:
            packed = tile(h, SHARED)

            def shared(kind, k):
                at = 3 * kind + k
                return jnp.broadcast_to(packed[:, at : at + 1], (8, width))

            kinds = [0, 0, 1, 2, 3, 3, 4, 4]
        else:

            def shared(kind, k):
                return tile(h, SHARED + 3 * kind + k)

            kinds = range(8)
        for v, factor in enumerate(first[h]):
            high, low = shift_lanes(factor, 1), shift_lanes(factor, -1)
            up, down = (pltpu.roll(factor, r, 0) for r in rolls)
            up_high, down_high = (pltpu.roll(high, r, 0) for r in rolls)
            up_low, down_low = (pltpu.roll(low, r, 0) for r in rolls)
            for g in range(2):
                k = v + g
                spread = (
                    shared(kinds[2], k) * up
                    + shared(kinds[3], k) * down
                )
                if width == LB:
                    spread = spread + shared(0, k) * (high + low)
                    spread = spread + half_sign * (
                        shared(3, k) * (up_high - up_low) - shared(4, k) * (down_high - down_low)
                    )
                else:
                    spread = spread + shared(0, k) * high + shared(1, k) * low
                    spread = spread + half_sign * (
                        shared(4, k) * up_high - shared(5, k) * up_low
                        - shared(6, k) * down_high + shared(7, k) * down_low
                    )
                totals[g] = totals[g] + tile(h, WEIGHTS + k) * factor + TIME_STEP * spread
        bridge = inverse[h // 2, HB - 1 : HB][:, HB : HB + 1]
        sums_in.append(bridge * totals[0])
        sums_out.append(totals[1])
    alpha, beta = pick(edge_couplings(sums_in, sums_out, inverse, rate))
    final = [None] * SLOTS
    for s in (1, 2, 3):
        final[s] = (
            product[:, (s - 1) * width : s * width]
            + inner_plane * alpha[s : s + 1]
            + outer_plane * beta[s : s + 1]
        )
    tissue = coef[3](2)
    v_late, v_early = fwd_v[1].astype(F32), fwd_v[0].astype(F32)
    w = tissue * (
        (1.0 - TIME_STEP * RECOVERY_RATE) * w_in[...]
        - TIME_STEP * v_late * (solved[2] + added[2])
    )
    center = centre(gain(v_early, fwd_g[0].astype(F32)), 2, coef)
    out_v[...] = (
        stencil(2, final, center, coef, sign)
        + (TIME_STEP * RECOVERY_RATE * EXCITATION) * (tissue * w)
    )
    out_w[...] = tissue * (
        (1.0 - TIME_STEP * RECOVERY_RATE) * w - TIME_STEP * v_early * final[2]
    )


def swaps(lines, lanes, partner):
    found = []
    for i in range(lines):
        for j in range(lanes):
            k, m = partner(i, j)
            found.append((i * lanes + j, k * lanes + m))
    return found


def per_device(
    adj_voltage,
    adj_gating,
    fwd_voltage,
    fwd_gating,
    region_labels,
    region_axial,
    region_shear,
    block_rate,
    block_inverse,
):
    lanes, lines = lax.axis_size("gy"), lax.axis_size("gx")
    _, depth, width = adj_voltage.shape
    label_blocks = region_labels.shape[2]
    assert depth == HB and block_inverse.shape[1] == ZB and lines % 4 == 0
    shape = jax.ShapeDtypeStruct
    room = pltpu.CompilerParams(vmem_limit_bytes=(8 << 20) * (width // LB))
    near, far, fwd_v, fwd_g, w, inverse, axial, shear, rate = pl.pallas_call(
        first_kernel,
        out_shape=(
            shape((3 * HB + 8, width), F32), shape((HB + 8, width), F32),
            shape((2, HB, width), fwd_voltage.dtype), shape((2, HB, width), fwd_gating.dtype),
            shape((HB, width), F32), shape(block_inverse.shape, F32),
            shape(region_axial.shape, F32),
            shape((1,) + region_shear.shape, F32), shape((1,) + block_rate.shape, F32),
        ),
        in_specs=[HBM] * 9,
        out_specs=(VMEM,) * 9,
        scratch_shapes=[pltpu.VMEM((label_blocks, HB), jnp.int32), pltpu.SemaphoreType.DMA((10,))],
        compiler_params=room,
    )(
        *[
            pltpu.with_memory_space_constraint(x, pltpu.HBM)
            for x in (
                adj_voltage[0], adj_gating[0], fwd_voltage[:, 0], fwd_gating[:, 0],
                region_labels[0].T, region_axial, region_shear[None], block_rate[None],
                block_inverse,
            )
        ]
    )
    ends = (0, lines - 1)
    wide = ends + (1, lines - 2)
    pair = lax.ppermute(near, BOTH, swaps(lines, lanes, lambda i, j: (i ^ 1, j)))
    after = lax.ppermute(
        near, BOTH,
        swaps(lines, lanes, lambda i, j: (i, j ^ 1) if i in ends else (i - 1 + 2 * (i % 2), j)),
    )
    two_a = lax.ppermute(far, BOTH, swaps(lines, lanes, lambda i, j: (i ^ 2, j)))
    two_b = lax.ppermute(
        far, BOTH,
        swaps(lines, lanes, lambda i, j: (i ^ 1, j) if i in wide else (((i - 2) ^ 2) + 2, j)),
    )
    count = -(-SLOTS * label_blocks // 8) * 8
    share_shape = (share_tiles(width), 8, width)
    share, solved, centres, partial, planes = pl.pallas_call(
        gather_kernel,
        out_shape=(
            shape(share_shape, F32), shape((SLOTS, HB, width), F32), shape((3, HB, width), F32),
            shape((3, HB, width), F32), shape((4 * SLOTS, HB, width), F32),
        ),
        in_specs=[VMEM] * 8,
        out_specs=(VMEM,) * 5,
        scratch_shapes=[pltpu.VMEM((count, LB), F32)],
        compiler_params=room,
    )(near, pair, after, two_a, two_b, inverse, axial, shear)
    shares = [share] + [
        lax.ppermute(share, BOTH, swaps(lines, lanes, lambda i, j: (i, j ^ d)))
        for d in range(1, lanes)
    ]
    out_v, out_w = pl.pallas_call(
        lambda *refs: finish_kernel(lanes, *refs),
        out_shape=(shape((HB, width), F32),) * 2,
        in_specs=[VMEM] * (lanes + 9),
        out_specs=(VMEM,) * 2,
        scratch_shapes=[pltpu.VMEM((lanes,) + share_shape, F32)],
        compiler_params=room,
    )(*shares, solved, centres, partial, planes, inverse, rate, fwd_v, fwd_g, w)
    return (out_v[None], out_w[None])


def solution(mesh):
    return jax.shard_map(
        per_device,
        mesh=mesh,
        in_specs=(
            P("gx", "gy", None),
            P("gx", "gy", None),
            P(None, "gx", "gy", None),
            P(None, "gx", "gy", None),
            P("gx", "gy", None),
            P(),
            P(),
            P(),
            P(),
        ),
        out_specs=(P("gx", "gy", None), P("gx", "gy", None)),
        check_vma=False,
    )
```

time: 80.4 us -> 19.2 us (0.24)
  the two profiles are of different devices: /device:TPU:1 before, /device:TPU:0 now
where the time goes in v3:
time: 19.2 us; the launch traced here: 19 us
  starting transfers between devices  9.91 us (52%)
  waiting for transfers between devices  5.33 us (28%)
  Pallas kernels  3.14 us (16%)
  between operations  0.66 us (3%)
    ppermute x3, starting transfers between devices, per_device(): lax.ppermute(share, BOTH, swaps(lines, lanes, lambda i, j: (i, j ^ d)))  3.55 us
    ppermute x3, waiting for transfers between devices, per_device(): lax.ppermute(share, BOTH, swaps(lines, lanes, lambda i, j: (i, j ^ d)))  3.39 us
    ppermute x1, starting transfers between devices, per_device(): lax.ppermute(near, BOTH, swaps(lines, lanes, lambda i, j: (i, j ^ 1) if i...  3 us
    ppermute x1, starting transfers between devices, per_device(): lax.ppermute(far, BOTH, swaps(lines, lanes, lambda i, j: (i ^ 2, j)))  2.84 us
    ppermute x1, waiting for transfers between devices, per_device(): lax.ppermute(far, BOTH, swaps(lines, lanes, lambda i, j: (i ^ 2, j)))  1.93 us
    pallas_call x1, Pallas kernels, per_device(): pl.pallas_call(lambda *refs: finish_kernel(lanes, *refs), out_shape=(shap...  1.3 us
    pallas_call x1, Pallas kernels, per_device(): pl.pallas_call(first_kernel, out_shape=(shape((3 * HB + 8, width), F32),...  1.12 us
    pallas_call x1, Pallas kernels, per_device(): pl.pallas_call(gather_kernel, out_shape=(shape(share_shape, F32), shape((...  0.73 us
  transfers between devices with their start and end apart: 7, of which 4 were waited for; matrix products, arithmetic and copies ran while one was open for 0% of the time, Pallas kernels for 0%

profile of v3, /device:TPU:0, one launch (start us, length us, event | category | flops | bytes accessed | tf_op | source)
XLA Modules:
  0.0 19.0 jit_solution(14104334326485074767)
XLA Ops:
  0.6 1.1 %shard_map.104 = (f32[200,128]{1,0:T(8,128)S(1)}, f32[72,128]{1,0:T(8,128)S(1)}, bf16[2,64,128]{2,1,0:T(8,128)(2,1)S(1)}, bf16[2,64,128]{2,1,0:T(8,128)(2,1)S(1)...) custom-call(f32[64,128]{1,0:T(8,128)} %bitcast.9, ...), custom_call_target="tpu_custom_call" | custom-call | tf_op jit(solution)/shard_map/pallas_call | solution.py:423
  1.8 3.0 %collective-permute-start.1 = (f32[200,128]{1,0:T(8,128)S(1)}, f32[200,128]{1,0:T(8,128)S(1)}, u32[]{:S(2)}, u32[]{:S(2)}) collective-permute-start(f32[200,128]{1,0:T(8,128)S(1)} %get-tuple-element.18.near), channel_id=1, source_target_pairs={{0,1},{1,0},{2,3},{3,2},{4,8},{5,9},{6,10},{7,11},{8,4},{9,5},{10,... | collective-permute-start | bytes 307208 | tf_op jit(solution)/shard_map/ppermute | solution.py:449
  4.8 0.2 %collective-permute-start = (f32[200,128]{1,0:T(8,128)S(1)}, f32[200,128]{1,0:T(8,128)S(1)}, u32[]{:S(2)}, u32[]{:S(2)}) collective-permute-start(f32[200,128]{1,0:T(8,128)S(1)} %get-tuple-element.18.near), channel_id=1, source_target_pairs={{0,4},{1,5},{2,6},{3,7},{4,0},{5,1},{6,2},{7,3},{8,12},{9,13},{10,... | collective-permute-start | bytes 307208 | tf_op jit(solution)/shard_map/ppermute | solution.py:448
  5.0 0.3 %collective-permute-start.3 = (f32[72,128]{1,0:T(8,128)S(1)}, f32[72,128]{1,0:T(8,128)S(1)}, u32[]{:S(2)}, u32[]{:S(2)}) collective-permute-start(f32[72,128]{1,0:T(8,128)S(1)} %get-tuple-element.19), channel_id=1, source_target_pairs={{0,4},{1,5},{2,6},{3,7},{4,0},{5,1},{6,2},{7,3},{8,16},{9,17},{10,... | collective-permute-start | bytes 110600 | tf_op jit(solution)/shard_map/ppermute | solution.py:454
  5.3 2.8 %collective-permute-start.2 = (f32[72,128]{1,0:T(8,128)S(1)}, f32[72,128]{1,0:T(8,128)S(1)}, u32[]{:S(2)}, u32[]{:S(2)}) collective-permute-start(f32[72,128]{1,0:T(8,128)S(1)} %get-tuple-element.19), channel_id=1, source_target_pairs={{0,8},{1,9},{2,10},{3,11},{4,12},{5,13},{6,14},{7,15},{8,0},{9,1},... | collective-permute-start | bytes 110600 | tf_op jit(solution)/shard_map/ppermute | solution.py:453
  8.1 0.0 collective-permute-done.3.two_b
  8.1 1.9 %collective-permute-done.2.two_a = f32[72,128]{1,0:T(8,128)S(1)} collective-permute-done((f32[72,128]{1,0:T(8,128)S(1)}, f32[72,128]{1,0:T(8,128)S(1)}, u32[]{:S(2)}, u32[]{:S(2)}) %collective-permute-start.2) | collective-permute-done | bytes 36896 | tf_op jit(solution)/shard_map/ppermute | solution.py:453
  10.1 0.0 collective-permute-done.1.after
  10.1 0.0 collective-permute-done.pair
  10.1 0.7 %shard_map.105 = (f32[8,8,128]{2,1,0:T(8,128)S(1)}, f32[5,64,128]{2,1,0:T(8,128)S(1)}, f32[3,64,128]{2,1,0:T(8,128)S(1)}, f32[3,64,128]{2,1,0:T(8,128)S(1)}, f32[20,64,128]{2,1,0:T(8,128)S(1)}) custom-call(f32[200,128]{1,0:T(8,128)S(1)} %get-tuple-element.18.near, f32[200,128]{1,0:T(8,128)S(1)} %collective-permute-done.pair, ...), custom_call_target="tpu_custom_call" | custom-call | tf_op jit(solution)/shard_map/pallas_call | solution.py:460
  10.8 2.5 %collective-permute-start.6 = (f32[8,8,128]{2,1,0:T(8,128)S(1)}, f32[8,8,128]{2,1,0:T(8,128)S(1)}, u32[]{:S(2)}, u32[]{:S(2)}) collective-permute-start(f32[8,8,128]{2,1,0:T(8,128)S(1)} %get-tuple-element.23.refs_0_), channel_id=1, source_target_pairs={{0,3},{1,2},{2,1},{3,0},{4,7},{5,6},{6,5},{7,4},{8,11},{9,10},{10,... | collective-permute-start | bytes 98312 | tf_op jit(solution)/shard_map/ppermute | solution.py:472
  13.3 0.5 %collective-permute-start.5 = (f32[8,8,128]{2,1,0:T(8,128)S(1)}, f32[8,8,128]{2,1,0:T(8,128)S(1)}, u32[]{:S(2)}, u32[]{:S(2)}) collective-permute-start(f32[8,8,128]{2,1,0:T(8,128)S(1)} %get-tuple-element.23.refs_0_), channel_id=1, source_target_pairs={{0,2},{1,3},{2,0},{3,1},{4,6},{5,7},{6,4},{7,5},{8,10},{9,11},{10,... | collective-permute-start | bytes 98312 | tf_op jit(solution)/shard_map/ppermute | solution.py:472
  13.8 0.5 %collective-permute-start.4 = (f32[8,8,128]{2,1,0:T(8,128)S(1)}, f32[8,8,128]{2,1,0:T(8,128)S(1)}, u32[]{:S(2)}, u32[]{:S(2)}) collective-permute-start(f32[8,8,128]{2,1,0:T(8,128)S(1)} %get-tuple-element.23.refs_0_), channel_id=1, source_target_pairs={{0,1},{1,0},{2,3},{3,2},{4,5},{5,4},{6,7},{7,6},{8,9},{9,8},{10,11... | collective-permute-start | bytes 98312 | tf_op jit(solution)/shard_map/ppermute | solution.py:472
  14.3 1.3 %collective-permute-done.6.refs_3_ = f32[8,8,128]{2,1,0:T(8,128)S(1)} collective-permute-done((f32[8,8,128]{2,1,0:T(8,128)S(1)}, f32[8,8,128]{2,1,0:T(8,128)S(1)}, u32[]{:S(2)}, u32[]{:S(2)}) %collective-permute-start.6) | collective-permute-done | bytes 32800 | tf_op jit(solution)/shard_map/ppermute | solution.py:472
  15.7 1.6 %collective-permute-done.5.refs_2_ = f32[8,8,128]{2,1,0:T(8,128)S(1)} collective-permute-done((f32[8,8,128]{2,1,0:T(8,128)S(1)}, f32[8,8,128]{2,1,0:T(8,128)S(1)}, u32[]{:S(2)}, u32[]{:S(2)}) %collective-permute-start.5) | collective-permute-done | bytes 32800 | tf_op jit(solution)/shard_map/ppermute | solution.py:472
  17.2 0.5 %collective-permute-done.4.refs_1_ = f32[8,8,128]{2,1,0:T(8,128)S(1)} collective-permute-done((f32[8,8,128]{2,1,0:T(8,128)S(1)}, f32[8,8,128]{2,1,0:T(8,128)S(1)}, u32[]{:S(2)}, u32[]{:S(2)}) %collective-permute-start.4) | collective-permute-done | bytes 32800 | tf_op jit(solution)/shard_map/ppermute | solution.py:472
  17.7 1.3 %shard_map.106 = (f32[64,128]{1,0:T(8,128)}, f32[64,128]{1,0:T(8,128)}) custom-call(f32[8,8,128]{2,1,0:T(8,128)S(1)} %get-tuple-element.23.refs_0_, f32[8,8,128]{2,1,0:T(8,128)S(1)} %collective-permute-done.4.refs_1_, f32[8,8,128]{2,1,0:T(8,128)S(1)} %collective-permute-done.5.refs_2_, f32[8,8,128]{2,1,0:T(8,128)S(1)} %collective-permute-done.6.refs_3_, ...), custom_call_target="tpu_custom_call" | custom-call | tf_op jit(solution)/shard_map/pallas_call | solution.py:475
Async XLA Ops:
  1.8 8.3 %collective-permute-start.1 = (f32[200,128]{1,0:T(8,128)S(1)}, f32[200,128]{1,0:T(8,128)S(1)}, u32[]{:S(2)}, u32[]{:S(2)}) collective-permute-start(f32[200,128]{1,0:T(8,128)S(1)} %get-tuple-element.18.near), channel_id=1, source_target_pairs={{0,1},{1,0},{2,3},{3,2},{4,8},{5,9},{6,10},{7,11},{8,4},{9,5},{10,... | collective-permute-start | bytes 307208 | tf_op jit(solution)/shard_map/ppermute | solution.py:449
  4.8 5.3 %collective-permute-start = (f32[200,128]{1,0:T(8,128)S(1)}, f32[200,128]{1,0:T(8,128)S(1)}, u32[]{:S(2)}, u32[]{:S(2)}) collective-permute-start(f32[200,128]{1,0:T(8,128)S(1)} %get-tuple-element.18.near), channel_id=1, source_target_pairs={{0,4},{1,5},{2,6},{3,7},{4,0},{5,1},{6,2},{7,3},{8,12},{9,13},{10,... | collective-permute-start | bytes 307208 | tf_op jit(solution)/shard_map/ppermute | solution.py:448
  5.0 3.2 %collective-permute-start.3 = (f32[72,128]{1,0:T(8,128)S(1)}, f32[72,128]{1,0:T(8,128)S(1)}, u32[]{:S(2)}, u32[]{:S(2)}) collective-permute-start(f32[72,128]{1,0:T(8,128)S(1)} %get-tuple-element.19), channel_id=1, source_target_pairs={{0,4},{1,5},{2,6},{3,7},{4,0},{5,1},{6,2},{7,3},{8,16},{9,17},{10,... | collective-permute-start | bytes 110600 | tf_op jit(solution)/shard_map/ppermute | solution.py:454
  5.3 4.8 %collective-permute-start.2 = (f32[72,128]{1,0:T(8,128)S(1)}, f32[72,128]{1,0:T(8,128)S(1)}, u32[]{:S(2)}, u32[]{:S(2)}) collective-permute-start(f32[72,128]{1,0:T(8,128)S(1)} %get-tuple-element.19), channel_id=1, source_target_pairs={{0,8},{1,9},{2,10},{3,11},{4,12},{5,13},{6,14},{7,15},{8,0},{9,1},... | collective-permute-start | bytes 110600 | tf_op jit(solution)/shard_map/ppermute | solution.py:453
  10.8 4.9 %collective-permute-start.6 = (f32[8,8,128]{2,1,0:T(8,128)S(1)}, f32[8,8,128]{2,1,0:T(8,128)S(1)}, u32[]{:S(2)}, u32[]{:S(2)}) collective-permute-start(f32[8,8,128]{2,1,0:T(8,128)S(1)} %get-tuple-element.23.refs_0_), channel_id=1, source_target_pairs={{0,3},{1,2},{2,1},{3,0},{4,7},{5,6},{6,5},{7,4},{8,11},{9,10},{10,... | collective-permute-start | bytes 98312 | tf_op jit(solution)/shard_map/ppermute | solution.py:472
  13.3 3.9 %collective-permute-start.5 = (f32[8,8,128]{2,1,0:T(8,128)S(1)}, f32[8,8,128]{2,1,0:T(8,128)S(1)}, u32[]{:S(2)}, u32[]{:S(2)}) collective-permute-start(f32[8,8,128]{2,1,0:T(8,128)S(1)} %get-tuple-element.23.refs_0_), channel_id=1, source_target_pairs={{0,2},{1,3},{2,0},{3,1},{4,6},{5,7},{6,4},{7,5},{8,10},{9,11},{10,... | collective-permute-start | bytes 98312 | tf_op jit(solution)/shard_map/ppermute | solution.py:472
  13.8 3.9 %collective-permute-start.4 = (f32[8,8,128]{2,1,0:T(8,128)S(1)}, f32[8,8,128]{2,1,0:T(8,128)S(1)}, u32[]{:S(2)}, u32[]{:S(2)}) collective-permute-start(f32[8,8,128]{2,1,0:T(8,128)S(1)} %get-tuple-element.23.refs_0_), channel_id=1, source_target_pairs={{0,1},{1,0},{2,3},{3,2},{4,5},{5,4},{6,7},{7,6},{8,9},{9,8},{10,11... | collective-permute-start | bytes 98312 | tf_op jit(solution)/shard_map/ppermute | solution.py:472

commit v4 on v3

--- a/solution.py
+++ b/solution.py
@@ -20,7 +20,9 @@
 VMEM = pl.BlockSpec(memory_space=pltpu.VMEM)
 HBM = pl.BlockSpec(memory_space=pltpu.HBM)
 F32 = jnp.float32
-EDGE_IN, EDGE_OUT, SUM_IN, SUM_OUT, WEIGHTS, SHARED = 0, 1, 2, 3, 4, 7
+FAR = HB + 8
+GAIN, LEAD = slice(FAR, FAR + HB), slice(FAR + HB, FAR + 2 * HB)
+EDGE_IN, SUM_IN, EDGE_OUT, SUM_OUT, WEIGHTS, SHARED = 0, 1, 2, 3, 4, 7
 
 
 def gain(voltage, gating):
@@ -33,13 +35,13 @@
 
 
 def first_kernel(
-    voltage_in, gating_in, fwd_v_in, fwd_g_in, label_in, axial_in, shear_in, rate_in, inverse_in,
-    near, far, fwd_v, fwd_g, w, inverse, axial, shear, rate, label, sems,
+    voltage_in, gating_in, fwd_v_in, fwd_g_in, label_in, axial_in, shear_in, rate_in,
+    near, fwd_v, fwd_g, w, axial, shear, rate, label, sems,
 ):
     pairs = [
         (fwd_v_in, fwd_v), (fwd_g_in, fwd_g), (gating_in, w), (label_in, label),
-        (voltage_in, near.at[pl.ds(0, HB)]), (voltage_in, far.at[pl.ds(0, HB)]),
-        (inverse_in, inverse), (axial_in, axial), (shear_in, shear), (rate_in, rate),
+        (voltage_in, near.at[pl.ds(0, HB)]),
+        (axial_in, axial), (shear_in, shear), (rate_in, rate),
     ]
     copies = [pltpu.make_async_copy(a, b, sems.at[n]) for n, (a, b) in enumerate(pairs)]
     for copy in copies:
@@ -47,12 +49,11 @@
     for copy in copies[:4]:
         copy.wait()
     later = fwd_v.shape[0] - 1
-    near[HB : 2 * HB] = gain(fwd_v[later].astype(F32), fwd_g[later].astype(F32))
-    near[2 * HB : 3 * HB] = TIME_STEP * RECOVERY_RATE * EXCITATION * w[...]
+    near[GAIN] = gain(fwd_v[later].astype(F32), fwd_g[later].astype(F32))
+    near[LEAD] = TIME_STEP * RECOVERY_RATE * EXCITATION * w[...]
     blocks = label.shape[0]
-    near[3 * HB :] = jnp.zeros((8, near.shape[1]), F32)
-    near[3 * HB : 3 * HB + blocks, 0:HB] = label[...].astype(F32)
-    far[HB:] = near[3 * HB :]
+    near[HB : FAR] = jnp.zeros((8, near.shape[1]), F32)
+    near[HB : HB + blocks, 0:HB] = label[...].astype(F32)
     for copy in copies[4:]:
         copy.wait()
 
@@ -106,7 +107,7 @@
 
 
 def gather_kernel(
-    near, pair, after, two_a, two_b, inverse, axial, shear,
+    near, pair, after, before, beyond, inverse, axial, shear,
     share, solved, centres, partial, planes, rows,
 ):
     width = near.shape[1]
@@ -115,25 +116,17 @@
     me = lax.axis_index("gy")
     upper, mine = lax.rem(me, 2) == 1, lax.div(me, 2)
     even = lax.rem(line, 2) == 0
-    ahead = jnp.logical_or(lax.rem(line, 4) == 0, lax.rem(line, 4) == 3)
     inside = {
         1: jnp.logical_and(line > 0, line < last),
         4: jnp.where(even, line + 2 <= last, line >= 2),
         0: jnp.where(even, line >= 2, line + 2 <= last),
     }
 
-    def two(first, part):
-        a, b = two_a[part], two_b[part]
-        return jnp.where(ahead, a, b) if first else jnp.where(ahead, b, a)
-
-    body, tail = pl.ds(0, HB), pl.ds(HB, 8)
-    fields = [two(False, body), after[0:HB], near[0:HB], pair[0:HB], two(True, body)]
-    labels = [
-        two(False, tail), after[3 * HB :], near[3 * HB :], pair[3 * HB :], two(True, tail),
-    ]
+    given = (before, after, near, pair, beyond)
+    fields = [ref[0:HB] for ref in given]
     rows[...] = jnp.zeros(rows.shape, F32)
     for slot in range(SLOTS):
-        label = labels[slot][:label_blocks, :LB]
+        label = given[slot][HB : HB + label_blocks, :LB]
         if slot in inside:
             label = jnp.where(inside[slot], label, 0.0)
         rows[slot * label_blocks : (slot + 1) * label_blocks] = label
@@ -169,18 +162,18 @@
     parts = [product[:, slot * width : (slot + 1) * width] for slot in range(SLOTS)]
     share[...] = jnp.zeros(share.shape, F32)
 
-    def total(tile, slot, value):
-        share[tile, slot : slot + 1, :] = jnp.sum(value, axis=0, keepdims=True)
+    def total(kind, slot, value):
+        row = slot + 4 * (kind % 2)
+        share[kind // 2, row : row + 1, :] = jnp.sum(value, axis=0, keepdims=True)
 
     for slot in range(SLOTS):
         solved[slot] = parts[slot]
         total(EDGE_IN, slot, bridge * (inner_plane * fields[slot]))
         total(EDGE_OUT, slot, outer_plane * fields[slot])
     weights = (inner_plane * inner_plane, inner_plane * outer_plane, outer_plane * outer_plane)
-    sources = {1: after, 2: near, 3: pair}
     for slot in (1, 2, 3):
-        gains = sources[slot][HB : 2 * HB]
-        lead = sources[slot][2 * HB : 3 * HB]
+        gains = given[slot][GAIN]
+        lead = given[slot][LEAD]
         center = centre(gains, slot, coef)
         part = stencil(slot, parts, center, coef, sign) + coef[3](slot) * lead
         centres[slot - 1] = center
@@ -209,7 +202,7 @@
             for k, vector in enumerate(vectors):
                 value = jnp.sum(kind * vector, axis=1, keepdims=True)
                 packed = jnp.where(lanes == 3 * n + k, value, packed)
-        share[SHARED] = packed
+        share[SHARED // 2, 5:8] = packed[1:4]
     else:
         ones = jnp.ones((HB, width), F32)
         none = jnp.zeros((HB, width), F32)
@@ -231,7 +224,7 @@
 
 
 def share_tiles(width):
-    return SHARED + (1 if width == LB else 24)
+    return -(-(SHARED + (1 if width == LB else 24)) // 2)
 
 
 def edge_couplings(edge_in, edge_out, inverse, rate, only=None):
@@ -295,8 +288,9 @@
     for d in range(halves):
         board[d] = shares[d][...]
 
-    def tile(half, which):
-        return board[lax.bitwise_xor(half, me), which]
+    def tile(half, kind):
+        found = board[lax.bitwise_xor(half, me), kind // 2]
+        return pltpu.roll(found, 4, 0) if kind % 2 else found
 
     every = range(halves)
     first = edge_couplings(
@@ -420,18 +414,17 @@
     assert depth == HB and block_inverse.shape[1] == ZB and lines % 4 == 0
     shape = jax.ShapeDtypeStruct
     room = pltpu.CompilerParams(vmem_limit_bytes=(8 << 20) * (width // LB))
-    near, far, fwd_v, fwd_g, w, inverse, axial, shear, rate = pl.pallas_call(
+    near, fwd_v, fwd_g, w, axial, shear, rate = pl.pallas_call(
         first_kernel,
         out_shape=(
-            shape((3 * HB + 8, width), F32), shape((HB + 8, width), F32),
+            shape((3 * HB + 8, width), F32),
             shape((2, HB, width), fwd_voltage.dtype), shape((2, HB, width), fwd_gating.dtype),
-            shape((HB, width), F32), shape(block_inverse.shape, F32),
-            shape(region_axial.shape, F32),
+            shape((HB, width), F32), shape(region_axial.shape, F32),
             shape((1,) + region_shear.shape, F32), shape((1,) + block_rate.shape, F32),
         ),
-        in_specs=[HBM] * 9,
-        out_specs=(VMEM,) * 9,
-        scratch_shapes=[pltpu.VMEM((label_blocks, HB), jnp.int32), pltpu.SemaphoreType.DMA((10,))],
+        in_specs=[HBM] * 8,
+        out_specs=(VMEM,) * 7,
+        scratch_shapes=[pltpu.VMEM((label_blocks, HB), jnp.int32), pltpu.SemaphoreType.DMA((8,))],
         compiler_params=room,
     )(
         *[
@@ -439,22 +432,20 @@
             for x in (
                 adj_voltage[0], adj_gating[0], fwd_voltage[:, 0], fwd_gating[:, 0],
                 region_labels[0].T, region_axial, region_shear[None], block_rate[None],
-                block_inverse,
             )
         ]
     )
     ends = (0, lines - 1)
-    wide = ends + (1, lines - 2)
-    pair = lax.ppermute(near, BOTH, swaps(lines, lanes, lambda i, j: (i ^ 1, j)))
+    cycle = list(range(0, lines, 2)) + list(range(lines - 1, 0, -2))
+    onward = {i: cycle[(n + 1) % lines] for n, i in enumerate(cycle)}
+    pairing = swaps(lines, lanes, lambda i, j: (i ^ 1, j))
     after = lax.ppermute(
         near, BOTH,
         swaps(lines, lanes, lambda i, j: (i, j ^ 1) if i in ends else (i - 1 + 2 * (i % 2), j)),
     )
-    two_a = lax.ppermute(far, BOTH, swaps(lines, lanes, lambda i, j: (i ^ 2, j)))
-    two_b = lax.ppermute(
-        far, BOTH,
-        swaps(lines, lanes, lambda i, j: (i ^ 1, j) if i in wide else (((i - 2) ^ 2) + 2, j)),
-    )
+    before = lax.ppermute(near, BOTH, swaps(lines, lanes, lambda i, j: (onward[i], j)))
+    pair = lax.ppermute(near, BOTH, pairing)
+    beyond = lax.ppermute(after[:FAR], BOTH, pairing)
     count = -(-SLOTS * label_blocks // 8) * 8
     share_shape = (share_tiles(width), 8, width)
     share, solved, centres, partial, planes = pl.pallas_call(
@@ -467,7 +458,7 @@
         out_specs=(VMEM,) * 5,
         scratch_shapes=[pltpu.VMEM((count, LB), F32)],
         compiler_params=room,
-    )(near, pair, after, two_a, two_b, inverse, axial, shear)
+    )(near, pair, after, before, beyond, block_inverse, axial, shear)
     shares = [share] + [
         lax.ppermute(share, BOTH, swaps(lines, lanes, lambda i, j: (i, j ^ d)))
         for d in range(1, lanes)
@@ -479,7 +470,9 @@
         out_specs=(VMEM,) * 2,
         scratch_shapes=[pltpu.VMEM((lanes,) + share_shape, F32)],
         compiler_params=room,
-    )(*shares, solved, centres, partial, planes, inverse, rate, fwd_v, fwd_g, w)
+    )(
+        *shares, solved, centres, partial, planes, block_inverse, rate, fwd_v, fwd_g, w
+    )
     return (out_v[None], out_w[None])
 
 

time: 19.2 us -> 17.9 us (0.932)
  starting transfers between devices: 9.91 us -> 7.31 us
  waiting for transfers between devices: 5.33 us -> 6.83 us
    ppermute x3, starting transfers between devices: 3.35 us -> 0.63 us  [the longest x1 0.38 us: per_device(): pair = lax.ppermute(near, BOTH, pairing)]
    ppermute x1, waiting for transfers between devices: 0.01 us -> 2.13 us  [per_device(): lax.ppermute(near, BOTH, swaps(lines, lanes, lambda i, j: (i, j ^ 1) if i...]
    ppermute x3, waiting for transfers between devices: 1.94 us -> 1.1 us  [the longest x1 1.07 us: per_device(): beyond = lax.ppermute(after[:FAR], BOTH, pairing)]
    ppermute x3, waiting for transfers between devices: 3.39 us -> 3.6 us  [per_device(): lax.ppermute(share, BOTH, swaps(lines, lanes, lambda i, j: (i, j ^ d)))]
  transfers between devices with their start and end apart: 7 -> 7, of which waited for: 4 -> 5; matrix products, arithmetic and copies ran while one was open for 0% -> 0% of each run, Pallas kernels for 0% -> 0%
where the time goes in v4:
time: 17.9 us; the launch traced here: 17.8 us
  starting transfers between devices  7.31 us (41%)
  waiting for transfers between devices  6.83 us (38%)
  Pallas kernels  2.96 us (17%)
  between operations  0.67 us (4%)
    ppermute x3, starting transfers between devices, per_device(): lax.ppermute(share, BOTH, swaps(lines, lanes, lambda i, j: (i, j ^ d)))  3.68 us
    ppermute x3, waiting for transfers between devices, per_device(): lax.ppermute(share, BOTH, swaps(lines, lanes, lambda i, j: (i, j ^ d)))  3.6 us
    ppermute x1, starting transfers between devices, per_device(): lax.ppermute(near, BOTH, swaps(lines, lanes, lambda i, j: (i, j ^ 1) if i...  3 us
    ppermute x1, waiting for transfers between devices, per_device(): lax.ppermute(near, BOTH, swaps(lines, lanes, lambda i, j: (i, j ^ 1) if i...  2.13 us
    pallas_call x1, Pallas kernels, per_device(): pl.pallas_call(lambda *refs: finish_kernel(lanes, *refs), out_shape=(shap...  1.3 us
    ppermute x1, waiting for transfers between devices, per_device(): beyond = lax.ppermute(after[:FAR], BOTH, pairing)  1.07 us
    pallas_call x1, Pallas kernels, per_device(): pl.pallas_call(first_kernel, out_shape=(shape((3 * HB + 8, width), F32),...  0.93 us
    pallas_call x1, Pallas kernels, per_device(): pl.pallas_call(gather_kernel, out_shape=(shape(share_shape, F32), shape((...  0.72 us
  transfers between devices with their start and end apart: 7, of which 5 were waited for; matrix products, arithmetic and copies ran while one was open for 0% of the time, Pallas kernels for 0%

profile of v4, /device:TPU:0, one launch (start us, length us, event | category | flops | bytes accessed | tf_op | source)
XLA Modules:
  0.0 17.8 jit_solution(477582823688172116)
XLA Ops:
  0.6 0.0 copy-start
  0.6 0.9 %shard_map.104 = (f32[200,128]{1,0:T(8,128)S(1)}, bf16[2,64,128]{2,1,0:T(8,128)(2,1)S(1)}, bf16[2,64,128]{2,1,0:T(8,128)(2,1)S(1)}, f32[64,128]{1,0:T(8,128)S(1)...) custom-call(f32[64,128]{1,0:T(8,128)} %bitcast.9, f32[64,128]{1,0:T(8,128)} %bitcast.10, ...), custom_call_target="tpu_custom_call" | custom-call | tf_op jit(solution)/shard_map/pallas_call | solution.py:417
  1.6 3.0 %collective-permute-start.1 = (f32[200,128]{1,0:T(8,128)S(1)}, f32[200,128]{1,0:T(8,128)S(1)}, u32[]{:S(2)}, u32[]{:S(2)}) collective-permute-start(f32[200,128]{1,0:T(8,128)S(1)} %get-tuple-element.16.near), channel_id=1, source_target_pairs={{0,1},{1,0},{2,3},{3,2},{4,8},{5,9},{6,10},{7,11},{8,4},{9,5},{10,... | collective-permute-start | bytes 307208 | tf_op jit(solution)/shard_map/ppermute | solution.py:442
  4.6 0.1 collective-permute-start.2
  4.7 0.4 %collective-permute-start = (f32[200,128]{1,0:T(8,128)S(1)}, f32[200,128]{1,0:T(8,128)S(1)}, u32[]{:S(2)}, u32[]{:S(2)}) collective-permute-start(f32[200,128]{1,0:T(8,128)S(1)} %get-tuple-element.16.near), channel_id=1, source_target_pairs={{0,4},{1,5},{2,6},{3,7},{4,0},{5,1},{6,2},{7,3},{8,12},{9,13},{10,... | collective-permute-start | bytes 307208 | tf_op jit(solution)/shard_map/ppermute | solution.py:447
  5.1 2.1 %collective-permute-done.1.after = f32[200,128]{1,0:T(8,128)S(1)} collective-permute-done((f32[200,128]{1,0:T(8,128)S(1)}, f32[200,128]{1,0:T(8,128)S(1)}, u32[]{:S(2)}, u32[]{:S(2)}) %collective-permute-start.1) | collective-permute-done | bytes 102432 | tf_op jit(solution)/shard_map/ppermute | solution.py:442
  7.2 0.1 collective-permute-start.3
  7.3 0.0 collective-permute-done.2.before
  7.4 0.0 collective-permute-done.pair
  7.4 1.1 %collective-permute-done.3.beyond = f32[72,128]{1,0:T(8,128)S(1)} collective-permute-done((f32[72,128]{1,0:T(8,128)S(1)}, f32[72,128]{1,0:T(8,128)S(1)}, u32[]{:S(2)}, u32[]{:S(2)}) %collective-permute-start.3) | collective-permute-done | bytes 36896 | tf_op jit(solution)/shard_map/ppermute | solution.py:448
  8.4 0.0 copy-done
  8.4 0.7 %shard_map.105 = (f32[4,8,128]{2,1,0:T(8,128)S(1)}, f32[5,64,128]{2,1,0:T(8,128)S(1)}, f32[3,64,128]{2,1,0:T(8,128)S(1)}, f32[3,64,128]{2,1,0:T(8,128)S(1)}, f32[20,64,128]{2,1,0:T(8,128)S(1)}) custom-call(f32[200,128]{1,0:T(8,128)S(1)} %get-tuple-element.16.near, f32[200,128]{1,0:T(8,128)S(1)} %collective-permute-done.pair, ...), custom_call_target="tpu_custom_call" | custom-call | tf_op jit(solution)/shard_map/pallas_call | solution.py:451
  9.2 3.0 %collective-permute-start.6 = (f32[4,8,128]{2,1,0:T(8,128)S(1)}, f32[4,8,128]{2,1,0:T(8,128)S(1)}, u32[]{:S(2)}, u32[]{:S(2)}) collective-permute-start(f32[4,8,128]{2,1,0:T(8,128)S(1)} %get-tuple-element.19.refs_0_), channel_id=1, source_target_pairs={{0,3},{1,2},{2,1},{3,0},{4,7},{5,6},{6,5},{7,4},{8,11},{9,10},{10,... | collective-permute-start | bytes 49160 | tf_op jit(solution)/shard_map/ppermute | solution.py:463
  12.2 0.5 %collective-permute-start.5 = (f32[4,8,128]{2,1,0:T(8,128)S(1)}, f32[4,8,128]{2,1,0:T(8,128)S(1)}, u32[]{:S(2)}, u32[]{:S(2)}) collective-permute-start(f32[4,8,128]{2,1,0:T(8,128)S(1)} %get-tuple-element.19.refs_0_), channel_id=1, source_target_pairs={{0,2},{1,3},{2,0},{3,1},{4,6},{5,7},{6,4},{7,5},{8,10},{9,11},{10,... | collective-permute-start | bytes 49160 | tf_op jit(solution)/shard_map/ppermute | solution.py:463
  12.7 0.1 collective-permute-start.4
  12.9 1.1 %collective-permute-done.6.refs_3_ = f32[4,8,128]{2,1,0:T(8,128)S(1)} collective-permute-done((f32[4,8,128]{2,1,0:T(8,128)S(1)}, f32[4,8,128]{2,1,0:T(8,128)S(1)}, u32[]{:S(2)}, u32[]{:S(2)}) %collective-permute-start.6) | collective-permute-done | bytes 16416 | tf_op jit(solution)/shard_map/ppermute | solution.py:463
  13.9 2.0 %collective-permute-done.5.refs_2_ = f32[4,8,128]{2,1,0:T(8,128)S(1)} collective-permute-done((f32[4,8,128]{2,1,0:T(8,128)S(1)}, f32[4,8,128]{2,1,0:T(8,128)S(1)}, u32[]{:S(2)}, u32[]{:S(2)}) %collective-permute-start.5) | collective-permute-done | bytes 16416 | tf_op jit(solution)/shard_map/ppermute | solution.py:463
  16.0 0.5 %collective-permute-done.4.refs_1_ = f32[4,8,128]{2,1,0:T(8,128)S(1)} collective-permute-done((f32[4,8,128]{2,1,0:T(8,128)S(1)}, f32[4,8,128]{2,1,0:T(8,128)S(1)}, u32[]{:S(2)}, u32[]{:S(2)}) %collective-permute-start.4) | collective-permute-done | bytes 16416 | tf_op jit(solution)/shard_map/ppermute | solution.py:463
  16.5 1.3 %shard_map.106 = (f32[64,128]{1,0:T(8,128)}, f32[64,128]{1,0:T(8,128)}) custom-call(f32[4,8,128]{2,1,0:T(8,128)S(1)} %get-tuple-element.19.refs_0_, f32[4,8,128]{2,1,0:T(8,128)S(1)} %collective-permute-done.4.refs_1_, f32[4,8,128]{2,1,0:T(8,128)S(1)} %collective-permute-done.5.refs_2_, f32[4,8,128]{2,1,0:T(8,128)S(1)} %collective-permute-done.6.refs_3_, ...), custom_call_target="tpu_custom_call" | custom-call | tf_op jit(solution)/shard_map/pallas_call | solution.py:466
  (1 shorter events, 0.0 us)
Async XLA Ops:
  0.6 7.8 %copy-start = (f32[2,128,128]{2,1,0:T(8,128)S(1)}, f32[2,128,128]{2,1,0:T(8,128)}, u32[]{:S(2)}) copy-start(f32[2,128,128]{2,1,0:T(8,128)} %refs_8_.1) | copy-start | bytes 393220
  1.6 5.6 %collective-permute-start.1 = (f32[200,128]{1,0:T(8,128)S(1)}, f32[200,128]{1,0:T(8,128)S(1)}, u32[]{:S(2)}, u32[]{:S(2)}) collective-permute-start(f32[200,128]{1,0:T(8,128)S(1)} %get-tuple-element.16.near), channel_id=1, source_target_pairs={{0,1},{1,0},{2,3},{3,2},{4,8},{5,9},{6,10},{7,11},{8,4},{9,5},{10,... | collective-permute-start | bytes 307208 | tf_op jit(solution)/shard_map/ppermute | solution.py:442
  4.6 2.8 %collective-permute-start.2 = (f32[200,128]{1,0:T(8,128)S(1)}, f32[200,128]{1,0:T(8,128)S(1)}, u32[]{:S(2)}, u32[]{:S(2)}) collective-permute-start(f32[200,128]{1,0:T(8,128)S(1)} %get-tuple-element.16.near), channel_id=1, source_target_pairs={{0,8},{1,9},{2,10},{3,11},{4,0},{5,1},{6,2},{7,3},{8,16},{9,17},{1... | collective-permute-start | bytes 307208 | tf_op jit(solution)/shard_map/ppermute | solution.py:446
  4.7 2.7 %collective-permute-start = (f32[200,128]{1,0:T(8,128)S(1)}, f32[200,128]{1,0:T(8,128)S(1)}, u32[]{:S(2)}, u32[]{:S(2)}) collective-permute-start(f32[200,128]{1,0:T(8,128)S(1)} %get-tuple-element.16.near), channel_id=1, source_target_pairs={{0,4},{1,5},{2,6},{3,7},{4,0},{5,1},{6,2},{7,3},{8,12},{9,13},{10,... | collective-permute-start | bytes 307208 | tf_op jit(solution)/shard_map/ppermute | solution.py:447
  7.2 1.2 %collective-permute-start.3 = (f32[72,128]{1,0:T(8,128)S(1)}, f32[72,128]{1,0:T(8,128)S(1)}, u32[]{:S(2)}, u32[]{:S(2)}) collective-permute-start(f32[72,128]{1,0:T(8,128)S(1)} %slice.4), channel_id=1, source_target_pairs={{0,4},{1,5},{2,6},{3,7},{4,0},{5,1},{6,2},{7,3},{8,12},{9,13},{10,... | collective-permute-start | bytes 110600 | tf_op jit(solution)/shard_map/ppermute | solution.py:448
  9.2 4.8 %collective-permute-start.6 = (f32[4,8,128]{2,1,0:T(8,128)S(1)}, f32[4,8,128]{2,1,0:T(8,128)S(1)}, u32[]{:S(2)}, u32[]{:S(2)}) collective-permute-start(f32[4,8,128]{2,1,0:T(8,128)S(1)} %get-tuple-element.19.refs_0_), channel_id=1, source_target_pairs={{0,3},{1,2},{2,1},{3,0},{4,7},{5,6},{6,5},{7,4},{8,11},{9,10},{10,... | collective-permute-start | bytes 49160 | tf_op jit(solution)/shard_map/ppermute | solution.py:463
  12.2 3.7 %collective-permute-start.5 = (f32[4,8,128]{2,1,0:T(8,128)S(1)}, f32[4,8,128]{2,1,0:T(8,128)S(1)}, u32[]{:S(2)}, u32[]{:S(2)}) collective-permute-start(f32[4,8,128]{2,1,0:T(8,128)S(1)} %get-tuple-element.19.refs_0_), channel_id=1, source_target_pairs={{0,2},{1,3},{2,0},{3,1},{4,6},{5,7},{6,4},{7,5},{8,10},{9,11},{10,... | collective-permute-start | bytes 49160 | tf_op jit(solution)/shard_map/ppermute | solution.py:463
  12.7 3.7 %collective-permute-start.4 = (f32[4,8,128]{2,1,0:T(8,128)S(1)}, f32[4,8,128]{2,1,0:T(8,128)S(1)}, u32[]{:S(2)}, u32[]{:S(2)}) collective-permute-start(f32[4,8,128]{2,1,0:T(8,128)S(1)} %get-tuple-element.19.refs_0_), channel_id=1, source_target_pairs={{0,1},{1,0},{2,3},{3,2},{4,5},{5,4},{6,7},{7,6},{8,9},{9,8},{10,11... | collective-permute-start | bytes 49160 | tf_op jit(solution)/shard_map/ppermute | solution.py:463

commit v5 on v4

--- a/solution.py
+++ b/solution.py
@@ -21,7 +21,7 @@
 HBM = pl.BlockSpec(memory_space=pltpu.HBM)
 F32 = jnp.float32
 FAR = HB + 8
-GAIN, LEAD = slice(FAR, FAR + HB), slice(FAR + HB, FAR + 2 * HB)
+GAIN, LEAD = pl.ds(FAR, HB), pl.ds(FAR + HB, HB)
 EDGE_IN, SUM_IN, EDGE_OUT, SUM_OUT, WEIGHTS, SHARED = 0, 1, 2, 3, 4, 7
 
 
@@ -34,103 +34,33 @@
     return 1.0 + TIME_STEP * slope
 
 
-def first_kernel(
-    voltage_in, gating_in, fwd_v_in, fwd_g_in, label_in, axial_in, shear_in, rate_in,
-    near, fwd_v, fwd_g, w, axial, shear, rate, label, sems,
-):
-    pairs = [
-        (fwd_v_in, fwd_v), (fwd_g_in, fwd_g), (gating_in, w), (label_in, label),
-        (voltage_in, near.at[pl.ds(0, HB)]),
-        (axial_in, axial), (shear_in, shear), (rate_in, rate),
-    ]
+def start_copies(pairs, sems):
     copies = [pltpu.make_async_copy(a, b, sems.at[n]) for n, (a, b) in enumerate(pairs)]
     for copy in copies:
         copy.start()
-    for copy in copies[:4]:
+    return copies
+
+
+def first_kernel(voltage_in, gating_in, fwd_v_in, fwd_g_in, label_in, near, v, g, label, sems):
+    later = fwd_v_in.shape[0] - 1
+    copies = start_copies(
+        [
+            (fwd_v_in.at[later], v), (fwd_g_in.at[later], g), (label_in, label),
+            (gating_in, near.at[LEAD]), (voltage_in, near.at[pl.ds(0, HB)]),
+        ],
+        sems,
+    )
+    for copy in copies[:3]:
         copy.wait()
-    later = fwd_v.shape[0] - 1
-    near[GAIN] = gain(fwd_v[later].astype(F32), fwd_g[later].astype(F32))
-    near[LEAD] = TIME_STEP * RECOVERY_RATE * EXCITATION * w[...]
+    near[GAIN] = gain(v[...].astype(F32), g[...].astype(F32))
     blocks = label.shape[0]
-    near[HB : FAR] = jnp.zeros((8, near.shape[1]), F32)
+    near[HB:FAR] = jnp.zeros((8, near.shape[1]), F32)
     near[HB : HB + blocks, 0:HB] = label[...].astype(F32)
-    for copy in copies[4:]:
+    for copy in copies[3:]:
         copy.wait()
 
 
-def half_vectors(inverse, mine, upper):
-    def row(index):
-        return inverse[mine, index : index + 1, :]
-
-    bridge = row(HB - 1)[:, HB : HB + 1]
-    inner = jnp.where(upper, pltpu.roll(row(HB - 1), HB, 1), row(HB)) / bridge
-    outer = jnp.where(upper, pltpu.roll(row(ZB - 1), HB, 1), row(0))
-    rows = inverse[mine, pl.ds(pl.multiple_of(jnp.where(upper, HB, 0), HB), HB), :]
-    swapped = jnp.where(upper, pltpu.roll(rows, HB, 1), rows)
-    inner_column = jnp.where(upper, swapped[:, ZB - 1 :], swapped[:, HB : HB + 1]) / bridge
-    outer_column = jnp.where(upper, swapped[:, HB - 1 : HB], swapped[:, 0:1])
-    return inner, outer, inner_column, outer_column, bridge, swapped[:, :HB]
-
-
-def y_shifts(plus, minus):
-    width = plus.shape[1]
-    lane = lax.broadcasted_iota(jnp.int32, plus.shape, 1)
-    return jnp.where(lane == width - 1, 0.0, pltpu.roll(plus, width - 1, 1)) + jnp.where(
-        lane == 0, 0.0, pltpu.roll(minus, 1, 1)
-    )
-
-
-def stencil(slot, field, center, coef, sign):
-    along, across, shear, tissue = coef
-    level = TIME_STEP * (across(slot) * field[slot])
-    twist = (0.5 * TIME_STEP * sign) * (
-        shear(slot + 1) * field[slot + 1] - shear(slot - 1) * field[slot - 1]
-    )
-    beside = TIME_STEP * (
-        along(slot + 1) * field[slot + 1] + along(slot - 1) * field[slot - 1]
-    )
-    return center * field[slot] + tissue(slot) * (y_shifts(level + twist, level - twist) + beside)
-
-
-def centre(gains, slot, coef):
-    along, across, _, tissue = coef
-    return tissue(slot) * gains - (2.0 * TIME_STEP) * (along(slot) + across(slot))
-
-
-def coefficients(planes):
-    return [lambda slot, k=k: planes[k * SLOTS + slot] for k in range(4)]
-
-
-def orientation():
-    line = lax.axis_index("gx")
-    return jnp.where(lax.rem(line, 2) == 0, 1.0, -1.0)
-
-
-def gather_kernel(
-    near, pair, after, before, beyond, inverse, axial, shear,
-    share, solved, centres, partial, planes, rows,
-):
-    width = near.shape[1]
-    label_blocks = width // LB
-    line, last = lax.axis_index("gx"), lax.axis_size("gx") - 1
-    me = lax.axis_index("gy")
-    upper, mine = lax.rem(me, 2) == 1, lax.div(me, 2)
-    even = lax.rem(line, 2) == 0
-    inside = {
-        1: jnp.logical_and(line > 0, line < last),
-        4: jnp.where(even, line + 2 <= last, line >= 2),
-        0: jnp.where(even, line >= 2, line + 2 <= last),
-    }
-
-    given = (before, after, near, pair, beyond)
-    fields = [ref[0:HB] for ref in given]
-    rows[...] = jnp.zeros(rows.shape, F32)
-    for slot in range(SLOTS):
-        label = given[slot][HB : HB + label_blocks, :LB]
-        if slot in inside:
-            label = jnp.where(inside[slot], label, 0.0)
-        rows[slot * label_blocks : (slot + 1) * label_blocks] = label
-    label = rows[...]
+def lookup(label, axial, shear):
     zero = jnp.zeros(label.shape, F32)
     tables = [zero, zero, zero]
     for region in range(1, axial.shape[1]):
@@ -141,22 +71,140 @@
         ):
             tables[k] = jnp.where(here, value, tables[k])
     tables.append((label > 0.0).astype(F32))
+    return tables
+
+
+def fill_plane(plane, columns, at, label_blocks):
+    for block in range(label_blocks):
+        plane[:, block * LB : (block + 1) * LB] = jnp.broadcast_to(
+            columns[:, at + block : at + block + 1], (HB, LB)
+        )
+
+
+def aside_kernel(
+    near, gating_in, fwd_v_in, fwd_g_in, axial_in, shear_in, rate_in, inverse_in,
+    axial, shear, rate, inverse, vectors, own, lines, planes, early, w, v, g, label, sems,
+):
+    width = w.shape[1]
+    label_blocks = width // LB
+    me = lax.axis_index("gy")
+    upper, mine = lax.rem(me, 2) == 1, lax.div(me, 2)
+    for copy in start_copies(
+        [
+            (inverse_in, inverse), (axial_in, axial), (shear_in, shear), (rate_in, rate),
+            (gating_in, w), (fwd_v_in, v), (fwd_g_in, g),
+        ],
+        sems,
+    ):
+        copy.wait()
+    inner, outer, inner_column, outer_column, bridge, square = half_vectors(inverse, mine, upper)
+    vectors[0] = jnp.broadcast_to(inner_column, (HB, width))
+    vectors[1] = jnp.broadcast_to(outer_column, (HB, width))
+    own[...] = square
+    lines[0:1] = inner
+    lines[1:2] = outer
+    lines[2:3] = jnp.broadcast_to(bridge, (1, ZB))
+    label[...] = jnp.zeros(label.shape, F32)
+    label[0:label_blocks] = near[HB : HB + label_blocks, :LB]
+    columns = jnp.concatenate(lookup(label[...], axial, shear), axis=0).T[:HB]
+    for k in range(4):
+        fill_plane(planes.at[k], columns, 8 * k, label_blocks)
+    tissue = planes[3]
+    late_v, early_v = v[1].astype(F32), v[0].astype(F32)
+    early[0] = (1.0 - TIME_STEP * RECOVERY_RATE) * (tissue * w[...])
+    early[1] = TIME_STEP * (tissue * late_v)
+    early[2] = TIME_STEP * (tissue * early_v)
+    early[3] = tissue * gain(early_v, g[0].astype(F32)) - (2.0 * TIME_STEP) * (
+        planes[0] + planes[1]
+    )
+
+
+def half_vectors(inverse, mine, upper):
+    def row(index):
+        return inverse[mine, index : index + 1, :]
+
+    bridge = row(HB - 1)[:, HB : HB + 1]
+    inner = jnp.where(upper, pltpu.roll(row(HB - 1), HB, 1), row(HB)) / bridge
+    outer = jnp.where(upper, pltpu.roll(row(ZB - 1), HB, 1), row(0))
+    rows = inverse[mine, pl.ds(pl.multiple_of(jnp.where(upper, HB, 0), HB), HB), :]
+    swapped = jnp.where(upper, pltpu.roll(rows, HB, 1), rows)
+    inner_column = jnp.where(upper, swapped[:, ZB - 1 :], swapped[:, HB : HB + 1]) / bridge
+    outer_column = jnp.where(upper, swapped[:, HB - 1 : HB], swapped[:, 0:1])
+    return inner, outer, inner_column, outer_column, bridge, swapped[:, :HB]
+
+
+def y_shifts(plus, minus):
+    width = plus.shape[1]
+    lane = lax.broadcasted_iota(jnp.int32, plus.shape, 1)
+    return jnp.where(lane == width - 1, 0.0, pltpu.roll(plus, width - 1, 1)) + jnp.where(
+        lane == 0, 0.0, pltpu.roll(minus, 1, 1)
+    )
+
+
+def stencil(slot, field, center, coef, sign):
+    along, across, shear, tissue = coef
+    level = TIME_STEP * (across(slot) * field[slot])
+    twist = (0.5 * TIME_STEP * sign) * (
+        shear(slot + 1) * field[slot + 1] - shear(slot - 1) * field[slot - 1]
+    )
+    beside = TIME_STEP * (
+        along(slot + 1) * field[slot + 1] + along(slot - 1) * field[slot - 1]
+    )
+    return center * field[slot] + tissue(slot) * (y_shifts(level + twist, level - twist) + beside)
+
+
+def centre(gains, slot, coef):
+    along, across, _, tissue = coef
+    return tissue(slot) * gains - (2.0 * TIME_STEP) * (along(slot) + across(slot))
+
+
+def coefficients(planes, here):
+    return [
+        lambda slot, k=k: here[k] if slot == 2 else planes[k * SLOTS + slot] for k in range(4)
+    ]
+
+
+def orientation():
+    line = lax.axis_index("gx")
+    return jnp.where(lax.rem(line, 2) == 0, 1.0, -1.0)
+
+
+def gather_kernel(
+    near, pair, after, before, beyond, axial, shear, vectors, own, lines, here,
+    share, solved, centres, partial, planes, rows,
+):
+    width = near.shape[1]
+    label_blocks = width // LB
+    line, last = lax.axis_index("gx"), lax.axis_size("gx") - 1
+    even = lax.rem(line, 2) == 0
+    inside = {
+        1: jnp.logical_and(line > 0, line < last),
+        4: jnp.where(even, line + 2 <= last, line >= 2),
+        0: jnp.where(even, line >= 2, line + 2 <= last),
+    }
+
+    given = (before, after, near, pair, beyond)
+    fields = [ref[0:HB] for ref in given]
+    rows[...] = jnp.zeros(rows.shape, F32)
+    for slot in range(SLOTS):
+        label = given[slot][HB : HB + label_blocks, :LB]
+        if slot in inside:
+            label = jnp.where(inside[slot], label, 0.0)
+        rows[slot * label_blocks : (slot + 1) * label_blocks] = label
+    tables = lookup(rows[...], axial, shear)
     columns = jnp.concatenate(tables, axis=0).T[:HB]
-    count = label.shape[0]
+    count = rows.shape[0]
     for k in range(4):
         for slot in range(SLOTS):
-            for block in range(label_blocks):
-                at = k * count + slot * label_blocks + block
-                planes[k * SLOTS + slot, :, block * LB : (block + 1) * LB] = jnp.broadcast_to(
-                    columns[:, at : at + 1], (HB, LB)
-                )
-    coef = coefficients(planes)
+            if slot == 2 or (slot in (0, 4) and k in (1, 3)):
+                continue
+            fill_plane(planes.at[k * SLOTS + slot], columns, k * count + slot * label_blocks, label_blocks)
+    coef = coefficients(planes, here)
     sign = orientation()
-    inner, outer, inner_column, outer_column, bridge, own = half_vectors(inverse, mine, upper)
-    inner_plane = jnp.broadcast_to(inner_column, (HB, width))
-    outer_plane = jnp.broadcast_to(outer_column, (HB, width))
+    inner, outer, bridge = lines[0:1], lines[1:2], lines[2:3, 0:1]
+    inner_plane, outer_plane = vectors[0], vectors[1]
     product = jnp.dot(
-        own, jnp.concatenate(fields, axis=1),
+        own[...], jnp.concatenate(fields, axis=1),
         precision=lax.Precision.HIGHEST, preferred_element_type=F32,
     )
     parts = [product[:, slot * width : (slot + 1) * width] for slot in range(SLOTS)]
@@ -175,7 +223,7 @@
         gains = given[slot][GAIN]
         lead = given[slot][LEAD]
         center = centre(gains, slot, coef)
-        part = stencil(slot, parts, center, coef, sign) + coef[3](slot) * lead
+        part = stencil(slot, parts, center, coef, sign) + coef[3](slot) * ((TIME_STEP * RECOVERY_RATE * EXCITATION) * lead)
         centres[slot - 1] = center
         partial[slot - 1] = part
         total(SUM_IN, slot, inner_plane * part)
@@ -186,7 +234,7 @@
         lane = lax.broadcasted_iota(jnp.int32, (1, ZB), 1)
         inner = jnp.where(lane < HB, inner, 0.0)
         outer = jnp.where(lane < HB, outer, 0.0)
-        vectors = (inner * inner, inner * outer, outer * outer)
+        pairs = (inner * inner, inner * outer, outer * outer)
         along, across, shears, tissue = tables
         up, down = count - 1, 1
         kinds = (
@@ -199,7 +247,7 @@
         lanes = lax.broadcasted_iota(jnp.int32, (8, ZB), 1)
         packed = jnp.zeros((8, ZB), F32)
         for n, kind in enumerate(kinds):
-            for k, vector in enumerate(vectors):
+            for k, vector in enumerate(pairs):
                 value = jnp.sum(kind * vector, axis=1, keepdims=True)
                 packed = jnp.where(lanes == 3 * n + k, value, packed)
         share[SHARED // 2, 5:8] = packed[1:4]
@@ -279,11 +327,12 @@
 
 def finish_kernel(halves, *refs):
     shares = refs[:halves]
-    (solved, centres, partial, planes, inverse, rate, fwd_v, fwd_g, w_in) = refs[halves : halves + 9]
-    out_v, out_w, board = refs[halves + 9 :]
+    (solved, centres, partial, planes, here, vectors, own, early, inverse, rate) = refs[
+        halves : halves + 10
+    ]
+    out_v, out_w, board = refs[halves + 10 :]
     width = out_v.shape[1]
     me = lax.axis_index("gy")
-    upper, mine = lax.rem(me, 2) == 1, lax.div(me, 2)
     sign = orientation()
     for d in range(halves):
         board[d] = shares[d][...]
@@ -296,10 +345,8 @@
     first = edge_couplings(
         [tile(h, EDGE_IN) for h in every], [tile(h, EDGE_OUT) for h in every], inverse, rate
     )
-    _, _, inner_column, outer_column, _, own = half_vectors(inverse, mine, upper)
-    inner_plane = jnp.broadcast_to(inner_column, (HB, width))
-    outer_plane = jnp.broadcast_to(outer_column, (HB, width))
-    coef = coefficients(planes)
+    inner_plane, outer_plane = vectors[0], vectors[1]
+    coef = coefficients(planes, here)
 
     def pick(factors):
         chosen = factors[0]
@@ -315,7 +362,7 @@
         partial[s - 1] + stencil(s, added, centres[s - 1], coef, sign) for s in (1, 2, 3)
     ]
     product = jnp.dot(
-        own, jnp.concatenate(nexts, axis=1),
+        own[...], jnp.concatenate(nexts, axis=1),
         precision=lax.Precision.HIGHEST, preferred_element_type=F32,
     )
 
@@ -372,20 +419,11 @@
             + inner_plane * alpha[s : s + 1]
             + outer_plane * beta[s : s + 1]
         )
-    tissue = coef[3](2)
-    v_late, v_early = fwd_v[1].astype(F32), fwd_v[0].astype(F32)
-    w = tissue * (
-        (1.0 - TIME_STEP * RECOVERY_RATE) * w_in[...]
-        - TIME_STEP * v_late * (solved[2] + added[2])
-    )
-    center = centre(gain(v_early, fwd_g[0].astype(F32)), 2, coef)
-    out_v[...] = (
-        stencil(2, final, center, coef, sign)
-        + (TIME_STEP * RECOVERY_RATE * EXCITATION) * (tissue * w)
-    )
-    out_w[...] = tissue * (
-        (1.0 - TIME_STEP * RECOVERY_RATE) * w - TIME_STEP * v_early * final[2]
-    )
+    w = early[0] - early[1] * (solved[2] + added[2])
+    out_w[...] = (1.0 - TIME_STEP * RECOVERY_RATE) * w - early[2] * final[2]
+    out_v[...] = stencil(2, final, early[3], coef, sign) + (
+        TIME_STEP * RECOVERY_RATE * EXCITATION
+    ) * w
 
 
 def swaps(lines, lanes, partner):
@@ -414,26 +452,42 @@
     assert depth == HB and block_inverse.shape[1] == ZB and lines % 4 == 0
     shape = jax.ShapeDtypeStruct
     room = pltpu.CompilerParams(vmem_limit_bytes=(8 << 20) * (width // LB))
-    near, fwd_v, fwd_g, w, axial, shear, rate = pl.pallas_call(
+    in_hbm = lambda *arrays: [pltpu.with_memory_space_constraint(x, pltpu.HBM) for x in arrays]
+    voltages, gatings = fwd_voltage[:, 0], fwd_gating[:, 0]
+    late = pltpu.VMEM((HB, width), fwd_voltage.dtype)
+    near = pl.pallas_call(
         first_kernel,
+        out_shape=shape((3 * HB + 8, width), F32),
+        in_specs=[HBM] * 5,
+        out_specs=VMEM,
+        scratch_shapes=[
+            late, late, pltpu.VMEM((label_blocks, HB), jnp.int32), pltpu.SemaphoreType.DMA((5,)),
+        ],
+        compiler_params=room,
+    )(*in_hbm(adj_voltage[0], adj_gating[0], voltages, gatings, region_labels[0].T))
+    both = pltpu.VMEM((2, HB, width), fwd_voltage.dtype)
+    axial, shear, rate, inverse, vectors, own, own_rows, here, early = pl.pallas_call(
+        aside_kernel,
         out_shape=(
-            shape((3 * HB + 8, width), F32),
-            shape((2, HB, width), fwd_voltage.dtype), shape((2, HB, width), fwd_gating.dtype),
-            shape((HB, width), F32), shape(region_axial.shape, F32),
-            shape((1,) + region_shear.shape, F32), shape((1,) + block_rate.shape, F32),
+            shape(region_axial.shape, F32), shape((1,) + region_shear.shape, F32),
+            shape((1,) + block_rate.shape, F32), shape(block_inverse.shape, F32),
+            shape((2, HB, width), F32), shape((HB, HB), F32), shape((8, ZB), F32),
+            shape((4, HB, width), F32), shape((4, HB, width), F32),
         ),
-        in_specs=[HBM] * 8,
-        out_specs=(VMEM,) * 7,
-        scratch_shapes=[pltpu.VMEM((label_blocks, HB), jnp.int32), pltpu.SemaphoreType.DMA((8,))],
+        in_specs=[VMEM] + [HBM] * 7,
+        out_specs=(VMEM,) * 9,
+        scratch_shapes=[
+            pltpu.VMEM((HB, width), F32), both, both, pltpu.VMEM((8, LB), F32),
+            pltpu.SemaphoreType.DMA((7,)),
+        ],
         compiler_params=room,
+        cost_estimate=pl.CostEstimate(flops=1 << 20, bytes_accessed=1 << 20, transcendentals=0),
     )(
-        *[
-            pltpu.with_memory_space_constraint(x, pltpu.HBM)
-            for x in (
-                adj_voltage[0], adj_gating[0], fwd_voltage[:, 0], fwd_gating[:, 0],
-                region_labels[0].T, region_axial, region_shear[None], block_rate[None],
-            )
-        ]
+        near,
+        *in_hbm(
+            adj_gating[0], voltages, gatings, region_axial, region_shear[None], block_rate[None],
+            block_inverse,
+        ),
     )
     ends = (0, lines - 1)
     cycle = list(range(0, lines, 2)) + list(range(lines - 1, 0, -2))
@@ -445,7 +499,8 @@
     )
     before = lax.ppermute(near, BOTH, swaps(lines, lanes, lambda i, j: (onward[i], j)))
     pair = lax.ppermute(near, BOTH, pairing)
-    beyond = lax.ppermute(after[:FAR], BOTH, pairing)
+    relayed, own_rows = lax.optimization_barrier((after[:FAR], own_rows))
+    beyond = lax.ppermute(relayed, BOTH, pairing)
     count = -(-SLOTS * label_blocks // 8) * 8
     share_shape = (share_tiles(width), 8, width)
     share, solved, centres, partial, planes = pl.pallas_call(
@@ -454,11 +509,11 @@
             shape(share_shape, F32), shape((SLOTS, HB, width), F32), shape((3, HB, width), F32),
             shape((3, HB, width), F32), shape((4 * SLOTS, HB, width), F32),
         ),
-        in_specs=[VMEM] * 8,
+        in_specs=[VMEM] * 11,
         out_specs=(VMEM,) * 5,
         scratch_shapes=[pltpu.VMEM((count, LB), F32)],
         compiler_params=room,
-    )(near, pair, after, before, beyond, block_inverse, axial, shear)
+    )(near, pair, after, before, beyond, axial, shear, vectors, own, own_rows, here)
     shares = [share] + [
         lax.ppermute(share, BOTH, swaps(lines, lanes, lambda i, j: (i, j ^ d)))
         for d in range(1, lanes)
@@ -466,12 +521,12 @@
     out_v, out_w = pl.pallas_call(
         lambda *refs: finish_kernel(lanes, *refs),
         out_shape=(shape((HB, width), F32),) * 2,
-        in_specs=[VMEM] * (lanes + 9),
+        in_specs=[VMEM] * (lanes + 10),
         out_specs=(VMEM,) * 2,
         scratch_shapes=[pltpu.VMEM((lanes,) + share_shape, F32)],
         compiler_params=room,
     )(
-        *shares, solved, centres, partial, planes, block_inverse, rate, fwd_v, fwd_g, w
+        *shares, solved, centres, partial, planes, here, vectors, own, early, inverse, rate
     )
     return (out_v[None], out_w[None])
 

time: 17.9 us -> 17.8 us (level)
  waiting for transfers between devices: 6.83 us -> 5.5 us
  Pallas kernels: 2.96 us -> 4.04 us
    ppermute x1, waiting for transfers between devices: 2.13 us -> 0.8 us  [per_device(): lax.ppermute(near, BOTH, swaps(lines, lanes, lambda i, j: (i, j ^ 1) if i...]
    pallas_call x1 -> x2, Pallas kernels: 0.93 us -> 2.19 us  [the longest x1 1.32 us: per_device(): pl.pallas_call(aside_kernel, out_shape=(shape(region_axial.shape, F32), s...]
  transfers between devices with their start and end apart: 7 -> 7, of which waited for: 5 -> 5; matrix products, arithmetic and copies ran while one was open for 0% -> 0% of each run, Pallas kernels for 0% -> 8%
where the time goes in v5:
time: 17.8 us; the launch traced here: 17.5 us
  starting transfers between devices  7.31 us (41%)
  waiting for transfers between devices  5.5 us (31%)
  Pallas kernels  4.04 us (23%)
  between operations  0.65 us (4%)
    ppermute x3, starting transfers between devices, per_device(): lax.ppermute(share, BOTH, swaps(lines, lanes, lambda i, j: (i, j ^ d)))  3.68 us
    ppermute x3, waiting for transfers between devices, per_device(): lax.ppermute(share, BOTH, swaps(lines, lanes, lambda i, j: (i, j ^ d)))  3.6 us
    ppermute x1, starting transfers between devices, per_device(): lax.ppermute(near, BOTH, swaps(lines, lanes, lambda i, j: (i, j ^ 1) if i...  3 us
    pallas_call x1, Pallas kernels, per_device(): pl.pallas_call(aside_kernel, out_shape=(shape(region_axial.shape, F32), s...  1.32 us
    pallas_call x1, Pallas kernels, per_device(): pl.pallas_call(lambda *refs: finish_kernel(lanes, *refs), out_shape=(shap...  1.28 us
    ppermute x1, waiting for transfers between devices, per_device(): beyond = lax.ppermute(relayed, BOTH, pairing)  1.07 us
    pallas_call x1, Pallas kernels, per_device(): pl.pallas_call(first_kernel, out_shape=shape((3 * HB + 8, width), F32), i...  0.87 us
    ppermute x1, waiting for transfers between devices, per_device(): lax.ppermute(near, BOTH, swaps(lines, lanes, lambda i, j: (i, j ^ 1) if i...  0.8 us
  transfers between devices with their start and end apart: 7, of which 5 were waited for; matrix products, arithmetic and copies ran while one was open for 0% of the time, Pallas kernels for 8%

profile of v5, /device:TPU:0, one launch (start us, length us, event | category | flops | bytes accessed | tf_op | source)
XLA Modules:
  0.0 17.5 jit_solution(4450747166203890173)
XLA Ops:
  0.6 0.9 %shard_map.104.near = f32[200,128]{1,0:T(8,128)S(1)} custom-call(f32[64,128]{1,0:T(8,128)} %bitcast.15, f32[64,128]{1,0:T(8,128)} %bitcast.9, bf16[2,64,128]{2,1,0:T(8,128)(2,1)} %bitcast.11, bf16[2,64,128]{2,1,0:T(8,128)(2,1)} %bitcast.13, s32[1,64]{1,0:T(1,128)} %bitcast.16), custom_call_target="tpu_custom_call" | custom-call | tf_op jit(solution)/shard_map/pallas_call | solution.py:458
  1.5 3.0 %collective-permute-start.1 = (f32[200,128]{1,0:T(8,128)S(1)}, f32[200,128]{1,0:T(8,128)S(1)}, u32[]{:S(2)}, u32[]{:S(2)}) collective-permute-start(f32[200,128]{1,0:T(8,128)S(1)} %shard_map.104.near), channel_id=1, source_target_pairs={{0,1},{1,0},{2,3},{3,2},{4,8},{5,9},{6,10},{7,11},{8,4},{9,5},{10,... | collective-permute-start | bytes 307208 | tf_op jit(solution)/shard_map/ppermute | solution.py:496
  4.5 0.1 collective-permute-start.2
  4.6 0.4 %collective-permute-start = (f32[200,128]{1,0:T(8,128)S(1)}, f32[200,128]{1,0:T(8,128)S(1)}, u32[]{:S(2)}, u32[]{:S(2)}) collective-permute-start(f32[200,128]{1,0:T(8,128)S(1)} %shard_map.104.near), channel_id=1, source_target_pairs={{0,4},{1,5},{2,6},{3,7},{4,0},{5,1},{6,2},{7,3},{8,12},{9,13},{10,... | collective-permute-start | bytes 307208 | tf_op jit(solution)/shard_map/ppermute | solution.py:501
  5.0 1.3 %shard_map.105 = (f32[2,8]{1,0:T(2,128)S(1)}, f32[1,8]{1,0:T(1,128)S(1)}, f32[1,2]{1,0:T(1,128)S(1)}, f32[2,128,128]{2,1,0:T(8,128)S(1)}, f32[2,64,128]{2,1,0:T(...) custom-call(f32[200,128]{1,0:T(8,128)S(1)} %shard_map.104.near, ...), custom_call_target="tpu_custom_call" | custom-call | flops 1048576 | bytes 1048576 | tf_op jit(solution)/shard_map/pallas_call | solution.py:469
  6.3 0.8 %collective-permute-done.1.after = f32[200,128]{1,0:T(8,128)S(1)} collective-permute-done((f32[200,128]{1,0:T(8,128)S(1)}, f32[200,128]{1,0:T(8,128)S(1)}, u32[]{:S(2)}, u32[]{:S(2)}) %collective-permute-start.1) | collective-permute-done | bytes 102432 | tf_op jit(solution)/shard_map/ppermute | solution.py:496
  7.2 0.1 collective-permute-start.3
  7.3 0.0 collective-permute-done.2.before
  7.3 0.0 collective-permute-done.pair
  7.3 1.1 %collective-permute-done.3.beyond = f32[72,128]{1,0:T(8,128)S(1)} collective-permute-done((f32[72,128]{1,0:T(8,128)S(1)}, f32[72,128]{1,0:T(8,128)S(1)}, u32[]{:S(2)}, u32[]{:S(2)}) %collective-permute-start.3) | collective-permute-done | bytes 36896 | tf_op jit(solution)/shard_map/ppermute | solution.py:503
  8.4 0.6 %shard_map.106 = (f32[4,8,128]{2,1,0:T(8,128)S(1)}, f32[5,64,128]{2,1,0:T(8,128)S(1)}, f32[3,64,128]{2,1,0:T(8,128)S(1)}, f32[3,64,128]{2,1,0:T(8,128)S(1)}, f32[20,64,128]{2,1,0:T(8,128)S(1)}) custom-call(f32[200,128]{1,0:T(8,128)S(1)} %shard_map.104.near, f32[200,128]{1,0:T(8,128)S(1)} %collective-permute-done.pair, ...), custom_call_target="tpu_custom_call" | custom-call | tf_op jit(solution)/shard_map/pallas_call | solution.py:506
  8.9 3.0 %collective-permute-start.6 = (f32[4,8,128]{2,1,0:T(8,128)S(1)}, f32[4,8,128]{2,1,0:T(8,128)S(1)}, u32[]{:S(2)}, u32[]{:S(2)}) collective-permute-start(f32[4,8,128]{2,1,0:T(8,128)S(1)} %get-tuple-element.28.refs_0_), channel_id=1, source_target_pairs={{0,3},{1,2},{2,1},{3,0},{4,7},{5,6},{6,5},{7,4},{8,11},{9,10},{10,... | collective-permute-start | bytes 49160 | tf_op jit(solution)/shard_map/ppermute | solution.py:518
  12.0 0.5 %collective-permute-start.5 = (f32[4,8,128]{2,1,0:T(8,128)S(1)}, f32[4,8,128]{2,1,0:T(8,128)S(1)}, u32[]{:S(2)}, u32[]{:S(2)}) collective-permute-start(f32[4,8,128]{2,1,0:T(8,128)S(1)} %get-tuple-element.28.refs_0_), channel_id=1, source_target_pairs={{0,2},{1,3},{2,0},{3,1},{4,6},{5,7},{6,4},{7,5},{8,10},{9,11},{10,... | collective-permute-start | bytes 49160 | tf_op jit(solution)/shard_map/ppermute | solution.py:518
  12.5 0.1 collective-permute-start.4
  12.6 1.1 %collective-permute-done.6.refs_3_ = f32[4,8,128]{2,1,0:T(8,128)S(1)} collective-permute-done((f32[4,8,128]{2,1,0:T(8,128)S(1)}, f32[4,8,128]{2,1,0:T(8,128)S(1)}, u32[]{:S(2)}, u32[]{:S(2)}) %collective-permute-start.6) | collective-permute-done | bytes 16416 | tf_op jit(solution)/shard_map/ppermute | solution.py:518
  13.7 2.0 %collective-permute-done.5.refs_2_ = f32[4,8,128]{2,1,0:T(8,128)S(1)} collective-permute-done((f32[4,8,128]{2,1,0:T(8,128)S(1)}, f32[4,8,128]{2,1,0:T(8,128)S(1)}, u32[]{:S(2)}, u32[]{:S(2)}) %collective-permute-start.5) | collective-permute-done | bytes 16416 | tf_op jit(solution)/shard_map/ppermute | solution.py:518
  15.7 0.5 %collective-permute-done.4.refs_1_ = f32[4,8,128]{2,1,0:T(8,128)S(1)} collective-permute-done((f32[4,8,128]{2,1,0:T(8,128)S(1)}, f32[4,8,128]{2,1,0:T(8,128)S(1)}, u32[]{:S(2)}, u32[]{:S(2)}) %collective-permute-start.4) | collective-permute-done | bytes 16416 | tf_op jit(solution)/shard_map/ppermute | solution.py:518
  16.2 1.3 %shard_map.107 = (f32[64,128]{1,0:T(8,128)}, f32[64,128]{1,0:T(8,128)}) custom-call(f32[4,8,128]{2,1,0:T(8,128)S(1)} %get-tuple-element.28.refs_0_, f32[4,8,128]{2,1,0:T(8,128)S(1)} %collective-permute-done.4.refs_1_, f32[4,8,128]{2,1,0:T(8,128)S(1)} %collective-permute-done.5.refs_2_, f32[4,8,128]{2,1,0:T(8,128)S(1)} %collective-permute-done.6.refs_3_, ...), custom_call_target="tpu_custom_call" | custom-call | tf_op jit(solution)/shard_map/pallas_call | solution.py:521
  (1 shorter events, 0.0 us)
Async XLA Ops:
  1.5 5.6 %collective-permute-start.1 = (f32[200,128]{1,0:T(8,128)S(1)}, f32[200,128]{1,0:T(8,128)S(1)}, u32[]{:S(2)}, u32[]{:S(2)}) collective-permute-start(f32[200,128]{1,0:T(8,128)S(1)} %shard_map.104.near), channel_id=1, source_target_pairs={{0,1},{1,0},{2,3},{3,2},{4,8},{5,9},{6,10},{7,11},{8,4},{9,5},{10,... | collective-permute-start | bytes 307208 | tf_op jit(solution)/shard_map/ppermute | solution.py:496
  4.5 2.8 %collective-permute-start.2 = (f32[200,128]{1,0:T(8,128)S(1)}, f32[200,128]{1,0:T(8,128)S(1)}, u32[]{:S(2)}, u32[]{:S(2)}) collective-permute-start(f32[200,128]{1,0:T(8,128)S(1)} %shard_map.104.near), channel_id=1, source_target_pairs={{0,8},{1,9},{2,10},{3,11},{4,0},{5,1},{6,2},{7,3},{8,16},{9,17},{1... | collective-permute-start | bytes 307208 | tf_op jit(solution)/shard_map/ppermute | solution.py:500
  4.6 2.7 %collective-permute-start = (f32[200,128]{1,0:T(8,128)S(1)}, f32[200,128]{1,0:T(8,128)S(1)}, u32[]{:S(2)}, u32[]{:S(2)}) collective-permute-start(f32[200,128]{1,0:T(8,128)S(1)} %shard_map.104.near), channel_id=1, source_target_pairs={{0,4},{1,5},{2,6},{3,7},{4,0},{5,1},{6,2},{7,3},{8,12},{9,13},{10,... | collective-permute-start | bytes 307208 | tf_op jit(solution)/shard_map/ppermute | solution.py:501
  7.2 1.2 %collective-permute-start.3 = (f32[72,128]{1,0:T(8,128)S(1)}, f32[72,128]{1,0:T(8,128)S(1)}, u32[]{:S(2)}, u32[]{:S(2)}) collective-permute-start(f32[72,128]{1,0:T(8,128)S(1)} %slice.4), channel_id=1, source_target_pairs={{0,4},{1,5},{2,6},{3,7},{4,0},{5,1},{6,2},{7,3},{8,12},{9,13},{10,... | collective-permute-start | bytes 110600 | tf_op jit(solution)/shard_map/ppermute | solution.py:503
  8.9 4.8 %collective-permute-start.6 = (f32[4,8,128]{2,1,0:T(8,128)S(1)}, f32[4,8,128]{2,1,0:T(8,128)S(1)}, u32[]{:S(2)}, u32[]{:S(2)}) collective-permute-start(f32[4,8,128]{2,1,0:T(8,128)S(1)} %get-tuple-element.28.refs_0_), channel_id=1, source_target_pairs={{0,3},{1,2},{2,1},{3,0},{4,7},{5,6},{6,5},{7,4},{8,11},{9,10},{10,... | collective-permute-start | bytes 49160 | tf_op jit(solution)/shard_map/ppermute | solution.py:518
  12.0 3.7 %collective-permute-start.5 = (f32[4,8,128]{2,1,0:T(8,128)S(1)}, f32[4,8,128]{2,1,0:T(8,128)S(1)}, u32[]{:S(2)}, u32[]{:S(2)}) collective-permute-start(f32[4,8,128]{2,1,0:T(8,128)S(1)} %get-tuple-element.28.refs_0_), channel_id=1, source_target_pairs={{0,2},{1,3},{2,0},{3,1},{4,6},{5,7},{6,4},{7,5},{8,10},{9,11},{10,... | collective-permute-start | bytes 49160 | tf_op jit(solution)/shard_map/ppermute | solution.py:518
  12.5 3.7 %collective-permute-start.4 = (f32[4,8,128]{2,1,0:T(8,128)S(1)}, f32[4,8,128]{2,1,0:T(8,128)S(1)}, u32[]{:S(2)}, u32[]{:S(2)}) collective-permute-start(f32[4,8,128]{2,1,0:T(8,128)S(1)} %get-tuple-element.28.refs_0_), channel_id=1, source_target_pairs={{0,1},{1,0},{2,3},{3,2},{4,5},{5,4},{6,7},{7,6},{8,9},{9,8},{10,11... | collective-permute-start | bytes 49160 | tf_op jit(solution)/shard_map/ppermute | solution.py:518

commit v6 on v5

--- a/solution.py
+++ b/solution.py
@@ -144,13 +144,18 @@
 def stencil(slot, field, center, coef, sign):
     along, across, shear, tissue = coef
     level = TIME_STEP * (across(slot) * field[slot])
-    twist = (0.5 * TIME_STEP * sign) * (
-        shear(slot + 1) * field[slot + 1] - shear(slot - 1) * field[slot - 1]
-    )
-    beside = TIME_STEP * (
-        along(slot + 1) * field[slot + 1] + along(slot - 1) * field[slot - 1]
-    )
+    twist, beside = 0.0, 0.0
+    for step in (1, -1):
+        other = slot + step
+        if field[other] is not None:
+            twist = twist + (step * 0.5 * TIME_STEP * sign) * (shear(other) * field[other])
+            beside = beside + TIME_STEP * (along(other) * field[other])
     return center * field[slot] + tissue(slot) * (y_shifts(level + twist, level - twist) + beside)
+
+
+def reach(slot, other, field, coef, sign):
+    twist = ((other - slot) * 0.5 * TIME_STEP * sign) * (coef[2](other) * field)
+    return coef[3](slot) * (y_shifts(twist, -twist) + TIME_STEP * (coef[0](other) * field))
 
 
 def centre(gains, slot, coef):
@@ -158,10 +163,18 @@
     return tissue(slot) * gains - (2.0 * TIME_STEP) * (along(slot) + across(slot))
 
 
-def coefficients(planes, here):
-    return [
-        lambda slot, k=k: here[k] if slot == 2 else planes[k * SLOTS + slot] for k in range(4)
-    ]
+def coefficients(here, beside, beyond):
+    def reader(k):
+        def read(slot):
+            if slot == 2:
+                return here[k]
+            if slot in (1, 3):
+                return beside[2 * k + slot // 2]
+            return beyond[k + slot // 4]
+
+        return read
+
+    return [reader(k) for k in range(4)]
 
 
 def orientation():
@@ -169,12 +182,19 @@
     return jnp.where(lax.rem(line, 2) == 0, 1.0, -1.0)
 
 
-def gather_kernel(
-    near, pair, after, before, beyond, axial, shear, vectors, own, lines, here,
-    share, solved, centres, partial, planes, rows,
-):
-    width = near.shape[1]
-    label_blocks = width // LB
+def upright(row):
+    z = lax.broadcasted_iota(jnp.int32, (HB, LB), 0)
+    lane = lax.broadcasted_iota(jnp.int32, (HB, LB), 1)
+    column = jnp.sum(jnp.where(z == lane, row, 0.0), axis=1, keepdims=True)
+    return jnp.broadcast_to(column, (HB, LB))
+
+
+def put_total(share, kind, slot, value):
+    row = slot + 4 * (kind % 2)
+    share[kind // 2, row : row + 1, :] = jnp.sum(value, axis=0, keepdims=True)
+
+
+def label_rows(rows, given, label_blocks):
     line, last = lax.axis_index("gx"), lax.axis_size("gx") - 1
     even = lax.rem(line, 2) == 0
     inside = {
@@ -182,61 +202,104 @@
         4: jnp.where(even, line + 2 <= last, line >= 2),
         0: jnp.where(even, line >= 2, line + 2 <= last),
     }
-
-    given = (before, after, near, pair, beyond)
-    fields = [ref[0:HB] for ref in given]
     rows[...] = jnp.zeros(rows.shape, F32)
-    for slot in range(SLOTS):
-        label = given[slot][HB : HB + label_blocks, :LB]
+    for slot, ref in given.items():
+        label = ref[HB : HB + label_blocks, :LB]
         if slot in inside:
             label = jnp.where(inside[slot], label, 0.0)
         rows[slot * label_blocks : (slot + 1) * label_blocks] = label
-    tables = lookup(rows[...], axial, shear)
+    return rows[...]
+
+
+def solve_planes(own, fields, width):
+    product = jnp.dot(
+        own[...], jnp.concatenate(fields, axis=1),
+        precision=lax.Precision.HIGHEST, preferred_element_type=F32,
+    )
+    return [product[:, n * width : (n + 1) * width] for n in range(len(fields))]
+
+
+def gather_kernel(
+    near, pair, after, axial, shear, vectors, own, lines, here,
+    share, solved, centres, partial, beside, rows,
+):
+    width = near.shape[1]
+    label_blocks = width // LB
+    given = {1: after, 2: near, 3: pair}
+    tables = lookup(label_rows(rows, {1: after, 3: pair}, label_blocks), axial, shear)
     columns = jnp.concatenate(tables, axis=0).T[:HB]
-    count = rows.shape[0]
     for k in range(4):
-        for slot in range(SLOTS):
-            if slot == 2 or (slot in (0, 4) and k in (1, 3)):
-                continue
-            fill_plane(planes.at[k * SLOTS + slot], columns, k * count + slot * label_blocks, label_blocks)
-    coef = coefficients(planes, here)
+        for slot in (1, 3):
+            fill_plane(
+                beside.at[2 * k + slot // 2], columns,
+                k * rows.shape[0] + slot * label_blocks, label_blocks,
+            )
+    coef = coefficients(here, beside, None)
+    sign = orientation()
+    bridge = lines[2:3, 0:1]
+    inner_plane, outer_plane = vectors[0], vectors[1]
+    fields = [given[slot][0:HB] for slot in (1, 2, 3)]
+    parts = [None] + solve_planes(own, fields, width) + [None]
+    solved[...] = parts[2]
+    share[...] = jnp.zeros(share.shape, F32)
+    for slot in (1, 2, 3):
+        put_total(share, EDGE_IN, slot, bridge * (inner_plane * fields[slot - 1]))
+        put_total(share, EDGE_OUT, slot, outer_plane * fields[slot - 1])
+    weights = (inner_plane * inner_plane, inner_plane * outer_plane, outer_plane * outer_plane)
+    for slot in (1, 2, 3):
+        center = centre(given[slot][GAIN], slot, coef)
+        lead = (TIME_STEP * RECOVERY_RATE * EXCITATION) * given[slot][LEAD]
+        part = stencil(slot, parts, center, coef, sign) + coef[3](slot) * lead
+        centres[slot - 1] = center
+        partial[slot - 1] = part
+        if slot == 2:
+            put_total(share, SUM_IN, slot, inner_plane * part)
+            put_total(share, SUM_OUT, slot, outer_plane * part)
+        for k, weight in enumerate(weights):
+            put_total(share, WEIGHTS + k, slot, weight * center)
+
+
+def complete_kernel(
+    near, pair, after, before, beyond, axial, shear, vectors, own, lines, here,
+    begun, most, beside, share, outside, distant, rows,
+):
+    width = near.shape[1]
+    label_blocks = width // LB
+    given = {0: before, 1: after, 2: near, 3: pair, 4: beyond}
+    tables = lookup(label_rows(rows, given, label_blocks), axial, shear)
+    for k in range(2):
+        for slot in (0, 4):
+            for block in range(label_blocks):
+                at = slot * label_blocks + block
+                distant[2 * k + slot // 4, :, block * LB : (block + 1) * LB] = upright(
+                    tables[2 * k][at : at + 1]
+                )
+    coef = coefficients(here, beside, distant)
     sign = orientation()
     inner, outer, bridge = lines[0:1], lines[1:2], lines[2:3, 0:1]
     inner_plane, outer_plane = vectors[0], vectors[1]
-    product = jnp.dot(
-        own[...], jnp.concatenate(fields, axis=1),
-        precision=lax.Precision.HIGHEST, preferred_element_type=F32,
-    )
-    parts = [product[:, slot * width : (slot + 1) * width] for slot in range(SLOTS)]
-    share[...] = jnp.zeros(share.shape, F32)
+    share[...] = begun[...]
 
     def total(kind, slot, value):
-        row = slot + 4 * (kind % 2)
-        share[kind // 2, row : row + 1, :] = jnp.sum(value, axis=0, keepdims=True)
-
-    for slot in range(SLOTS):
-        solved[slot] = parts[slot]
-        total(EDGE_IN, slot, bridge * (inner_plane * fields[slot]))
-        total(EDGE_OUT, slot, outer_plane * fields[slot])
-    weights = (inner_plane * inner_plane, inner_plane * outer_plane, outer_plane * outer_plane)
-    for slot in (1, 2, 3):
-        gains = given[slot][GAIN]
-        lead = given[slot][LEAD]
-        center = centre(gains, slot, coef)
-        part = stencil(slot, parts, center, coef, sign) + coef[3](slot) * ((TIME_STEP * RECOVERY_RATE * EXCITATION) * lead)
-        centres[slot - 1] = center
-        partial[slot - 1] = part
-        total(SUM_IN, slot, inner_plane * part)
-        total(SUM_OUT, slot, outer_plane * part)
-        for k, weight in enumerate(weights):
-            total(WEIGHTS + k, slot, weight * center)
+        put_total(share, kind, slot, value)
+
+    fields = [before[0:HB], beyond[0:HB]]
+    parts = solve_planes(own, fields, width)
+    for n, slot in enumerate((0, 4)):
+        total(EDGE_IN, slot, bridge * (inner_plane * fields[n]))
+        total(EDGE_OUT, slot, outer_plane * fields[n])
+        middle = 1 + 2 * n
+        part = most[middle - 1] + reach(middle, slot, parts[n], coef, sign)
+        outside[n] = part
+        total(SUM_IN, middle, inner_plane * part)
+        total(SUM_OUT, middle, outer_plane * part)
     if label_blocks == 1:
         lane = lax.broadcasted_iota(jnp.int32, (1, ZB), 1)
         inner = jnp.where(lane < HB, inner, 0.0)
         outer = jnp.where(lane < HB, outer, 0.0)
         pairs = (inner * inner, inner * outer, outer * outer)
         along, across, shears, tissue = tables
-        up, down = count - 1, 1
+        up, down = rows.shape[0] - 1, 1
         kinds = (
             across,
             tissue * pltpu.roll(along, up, 0),
@@ -252,8 +315,10 @@
                 packed = jnp.where(lanes == 3 * n + k, value, packed)
         share[SHARED // 2, 5:8] = packed[1:4]
     else:
-        ones = jnp.ones((HB, width), F32)
         none = jnp.zeros((HB, width), F32)
+        weights = (
+            inner_plane * inner_plane, inner_plane * outer_plane, outer_plane * outer_plane
+        )
         for slot in (1, 2, 3):
             here = coef[3](slot)
             kinds = (
@@ -327,10 +392,10 @@
 
 def finish_kernel(halves, *refs):
     shares = refs[:halves]
-    (solved, centres, partial, planes, here, vectors, own, early, inverse, rate) = refs[
-        halves : halves + 10
-    ]
-    out_v, out_w, board = refs[halves + 10 :]
+    (
+        solved, centres, partial, outside, here, beside, distant, vectors, own, early, inverse, rate,
+    ) = refs[halves : halves + 12]
+    out_v, out_w, board = refs[halves + 12 :]
     width = out_v.shape[1]
     me = lax.axis_index("gy")
     sign = orientation()
@@ -346,7 +411,7 @@
         [tile(h, EDGE_IN) for h in every], [tile(h, EDGE_OUT) for h in every], inverse, rate
     )
     inner_plane, outer_plane = vectors[0], vectors[1]
-    coef = coefficients(planes, here)
+    coef = coefficients(here, beside, distant)
 
     def pick(factors):
         chosen = factors[0]
@@ -359,7 +424,9 @@
         inner_plane * alpha[s : s + 1] + outer_plane * beta[s : s + 1] for s in range(SLOTS)
     ]
     nexts = [
-        partial[s - 1] + stencil(s, added, centres[s - 1], coef, sign) for s in (1, 2, 3)
+        (partial[1] if s == 2 else outside[s // 2])
+        + stencil(s, added, centres[s - 1], coef, sign)
+        for s in (1, 2, 3)
     ]
     product = jnp.dot(
         own[...], jnp.concatenate(nexts, axis=1),
@@ -419,7 +486,7 @@
             + inner_plane * alpha[s : s + 1]
             + outer_plane * beta[s : s + 1]
         )
-    w = early[0] - early[1] * (solved[2] + added[2])
+    w = early[0] - early[1] * (solved[...] + added[2])
     out_w[...] = (1.0 - TIME_STEP * RECOVERY_RATE) * w - early[2] * final[2]
     out_v[...] = stencil(2, final, early[3], coef, sign) + (
         TIME_STEP * RECOVERY_RATE * EXCITATION
@@ -497,23 +564,38 @@
         near, BOTH,
         swaps(lines, lanes, lambda i, j: (i, j ^ 1) if i in ends else (i - 1 + 2 * (i % 2), j)),
     )
-    before = lax.ppermute(near, BOTH, swaps(lines, lanes, lambda i, j: (onward[i], j)))
+    before = lax.ppermute(near[:FAR], BOTH, swaps(lines, lanes, lambda i, j: (onward[i], j)))
     pair = lax.ppermute(near, BOTH, pairing)
     relayed, own_rows = lax.optimization_barrier((after[:FAR], own_rows))
     beyond = lax.ppermute(relayed, BOTH, pairing)
     count = -(-SLOTS * label_blocks // 8) * 8
     share_shape = (share_tiles(width), 8, width)
-    share, solved, centres, partial, planes = pl.pallas_call(
+    label_scratch = [pltpu.VMEM((count, LB), F32)]
+    begun, solved, centres, partial, beside = pl.pallas_call(
         gather_kernel,
         out_shape=(
-            shape(share_shape, F32), shape((SLOTS, HB, width), F32), shape((3, HB, width), F32),
-            shape((3, HB, width), F32), shape((4 * SLOTS, HB, width), F32),
+            shape(share_shape, F32), shape((HB, width), F32), shape((3, HB, width), F32),
+            shape((3, HB, width), F32), shape((8, HB, width), F32),
         ),
-        in_specs=[VMEM] * 11,
+        in_specs=[VMEM] * 9,
         out_specs=(VMEM,) * 5,
-        scratch_shapes=[pltpu.VMEM((count, LB), F32)],
+        scratch_shapes=label_scratch,
         compiler_params=room,
-    )(near, pair, after, before, beyond, axial, shear, vectors, own, own_rows, here)
+        cost_estimate=pl.CostEstimate(flops=1 << 20, bytes_accessed=1 << 20, transcendentals=0),
+    )(near, pair, after, axial, shear, vectors, own, own_rows, here)
+    share, outside, distant = pl.pallas_call(
+        complete_kernel,
+        out_shape=(
+            shape(share_shape, F32), shape((2, HB, width), F32), shape((4, HB, width), F32),
+        ),
+        in_specs=[VMEM] * 14,
+        out_specs=(VMEM,) * 3,
+        scratch_shapes=label_scratch,
+        compiler_params=room,
+    )(
+        near, pair, after, before, beyond, axial, shear, vectors, own, own_rows, here, begun,
+        partial, beside,
+    )
     shares = [share] + [
         lax.ppermute(share, BOTH, swaps(lines, lanes, lambda i, j: (i, j ^ d)))
         for d in range(1, lanes)
@@ -521,12 +603,13 @@
     out_v, out_w = pl.pallas_call(
         lambda *refs: finish_kernel(lanes, *refs),
         out_shape=(shape((HB, width), F32),) * 2,
-        in_specs=[VMEM] * (lanes + 10),
+        in_specs=[VMEM] * (lanes + 12),
         out_specs=(VMEM,) * 2,
         scratch_shapes=[pltpu.VMEM((lanes,) + share_shape, F32)],
         compiler_params=room,
     )(
-        *shares, solved, centres, partial, planes, here, vectors, own, early, inverse, rate
+        *shares, solved, centres, partial, outside, here, beside, distant, vectors, own, early,
+        inverse, rate,
     )
     return (out_v[None], out_w[None])
 

time: 17.8 us -> 17.5 us (0.983)
  waiting for transfers between devices: 5.5 us -> 3.89 us
  starting transfers between devices: 7.31 us -> 8.4 us
  Pallas kernels: 4.04 us -> 4.28 us
    ppermute x1, starting transfers between devices: 0.13 us -> 1.58 us  [per_device(): lax.ppermute(near[:FAR], BOTH, swaps(lines, lanes, lambda i, j: (onward[i...]
    ppermute x1, waiting for transfers between devices: 0.8 us -> 0.01 us  [per_device(): lax.ppermute(near, BOTH, swaps(lines, lanes, lambda i, j: (i, j ^ 1) if i...]
    ppermute x3, waiting for transfers between devices: 3.6 us -> 3.2 us  [per_device(): lax.ppermute(share, BOTH, swaps(lines, lanes, lambda i, j: (i, j ^ d)))]
    ppermute x1, waiting for transfers between devices: 1.07 us -> 0.68 us  [per_device(): beyond = lax.ppermute(relayed, BOTH, pairing)]
    pallas_call x0 -> x1, Pallas kernels: none -> 0.32 us  [per_device(): pl.pallas_call(complete_kernel, out_shape=(shape(share_shape, F32), shape...]
    ppermute x1, starting transfers between devices: 0.38 us -> 0.2 us  [per_device(): pair = lax.ppermute(near, BOTH, pairing)]
  transfers between devices with their start and end apart: 7 -> 7, of which waited for: 5 -> 4; matrix products, arithmetic and copies ran while one was open for 0% -> 0% of each run, Pallas kernels for 8% -> 10%
where the time goes in v6:
time: 17.5 us; the launch traced here: 17.3 us
  starting transfers between devices  8.4 us (48%)
  Pallas kernels  4.28 us (24%)
  waiting for transfers between devices  3.89 us (22%)
  between operations  0.69 us (4%)
    ppermute x3, starting transfers between devices, per_device(): lax.ppermute(share, BOTH, swaps(lines, lanes, lambda i, j: (i, j ^ d)))  3.55 us
    ppermute x3, waiting for transfers between devices, per_device(): lax.ppermute(share, BOTH, swaps(lines, lanes, lambda i, j: (i, j ^ d)))  3.2 us
    ppermute x1, starting transfers between devices, per_device(): lax.ppermute(near, BOTH, swaps(lines, lanes, lambda i, j: (i, j ^ 1) if i...  3 us
    ppermute x1, starting transfers between devices, per_device(): lax.ppermute(near[:FAR], BOTH, swaps(lines, lanes, lambda i, j: (onward[i...  1.58 us
    pallas_call x1, Pallas kernels, per_device(): pl.pallas_call(aside_kernel, out_shape=(shape(region_axial.shape, F32), s...  1.32 us
    pallas_call x1, Pallas kernels, per_device(): pl.pallas_call(lambda *refs: finish_kernel(lanes, *refs), out_shape=(shap...  1.28 us
    pallas_call x1, Pallas kernels, per_device(): pl.pallas_call(first_kernel, out_shape=shape((3 * HB + 8, width), F32), i...  0.87 us
    ppermute x1, waiting for transfers between devices, per_device(): beyond = lax.ppermute(relayed, BOTH, pairing)  0.68 us
  transfers between devices with their start and end apart: 7, of which 4 were waited for; matrix products, arithmetic and copies ran while one was open for 0% of the time, Pallas kernels for 10%

profile of v6, /device:TPU:0, one launch (start us, length us, event | category | flops | bytes accessed | tf_op | source)
XLA Modules:
  0.0 17.3 jit_solution(14541298638918965470)
XLA Ops:
  0.6 0.9 %shard_map.104.near = f32[200,128]{1,0:T(8,128)S(1)} custom-call(f32[64,128]{1,0:T(8,128)} %bitcast.15, f32[64,128]{1,0:T(8,128)} %bitcast.9, bf16[2,64,128]{2,1,0:T(8,128)(2,1)} %bitcast.11, bf16[2,64,128]{2,1,0:T(8,128)(2,1)} %bitcast.13, s32[1,64]{1,0:T(1,128)} %bitcast.16), custom_call_target="tpu_custom_call" | custom-call | tf_op jit(solution)/shard_map/pallas_call | solution.py:525
  1.5 3.0 %collective-permute-start.1 = (f32[200,128]{1,0:T(8,128)S(1)}, f32[200,128]{1,0:T(8,128)S(1)}, u32[]{:S(2)}, u32[]{:S(2)}) collective-permute-start(f32[200,128]{1,0:T(8,128)S(1)} %shard_map.104.near), channel_id=1, source_target_pairs={{0,1},{1,0},{2,3},{3,2},{4,8},{5,9},{6,10},{7,11},{8,4},{9,5},{10,... | collective-permute-start | bytes 307208 | tf_op jit(solution)/shard_map/ppermute | solution.py:563
  4.5 0.2 %collective-permute-start = (f32[200,128]{1,0:T(8,128)S(1)}, f32[200,128]{1,0:T(8,128)S(1)}, u32[]{:S(2)}, u32[]{:S(2)}) collective-permute-start(f32[200,128]{1,0:T(8,128)S(1)} %shard_map.104.near), channel_id=1, source_target_pairs={{0,4},{1,5},{2,6},{3,7},{4,0},{5,1},{6,2},{7,3},{8,12},{9,13},{10,... | collective-permute-start | bytes 307208 | tf_op jit(solution)/shard_map/ppermute | solution.py:568
  4.7 1.6 %collective-permute-start.2 = (f32[72,128]{1,0:T(8,128)S(1)}, f32[72,128]{1,0:T(8,128)S(1)}, u32[]{:S(2)}, u32[]{:S(2)}) collective-permute-start(f32[72,128]{1,0:T(8,128)S(1)} %slice.8), channel_id=1, source_target_pairs={{0,8},{1,9},{2,10},{3,11},{4,0},{5,1},{6,2},{7,3},{8,16},{9,17},{1... | collective-permute-start | bytes 110600 | tf_op jit(solution)/shard_map/ppermute | solution.py:567
  6.3 1.3 %shard_map.105 = (f32[2,8]{1,0:T(2,128)S(1)}, f32[1,8]{1,0:T(1,128)S(1)}, f32[1,2]{1,0:T(1,128)S(1)}, f32[2,128,128]{2,1,0:T(8,128)S(1)}, f32[2,64,128]{2,1,0:T(...) custom-call(f32[200,128]{1,0:T(8,128)S(1)} %shard_map.104.near, ...), custom_call_target="tpu_custom_call" | custom-call | flops 1048576 | bytes 1048576 | tf_op jit(solution)/shard_map/pallas_call | solution.py:536
  7.6 0.0 collective-permute-done.1.after
  7.6 0.1 collective-permute-start.3
  7.7 0.0 collective-permute-done.pair
  7.7 0.5 %shard_map.106 = (f32[4,8,128]{2,1,0:T(8,128)S(1)}, f32[64,128]{1,0:T(8,128)S(1)}, f32[3,64,128]{2,1,0:T(8,128)S(1)}, f32[3,64,128]{2,1,0:T(8,128)S(1)}, f32[8,64,128]{2,1,0:T(8,128)S(1)}) custom-call(f32[200,128]{1,0:T(8,128)S(1)} %shard_map.104.near, f32[200,128]{1,0:T(8,128)S(1)} %collective-permute-done.pair, ...), custom_call_target="tpu_custom_call" | custom-call | flops 1048576 | bytes 1048576 | tf_op jit(solution)/shard_map/pallas_call | solution.py:574
  8.2 0.0 collective-permute-done.2.before
  8.2 0.7 %collective-permute-done.3.beyond = f32[72,128]{1,0:T(8,128)S(1)} collective-permute-done((f32[72,128]{1,0:T(8,128)S(1)}, f32[72,128]{1,0:T(8,128)S(1)}, u32[]{:S(2)}, u32[]{:S(2)}) %collective-permute-start.3) | collective-permute-done | bytes 36896 | tf_op jit(solution)/shard_map/ppermute | solution.py:570
  8.9 0.3 %shard_map.107 = (f32[4,8,128]{2,1,0:T(8,128)S(1)}, f32[2,64,128]{2,1,0:T(8,128)S(1)}, f32[4,64,128]{2,1,0:T(8,128)S(1)}) custom-call(f32[200,128]{1,0:T(8,128)S(1)} %shard_map.104.near, f32[200,128]{1,0:T(8,128)S(1)} %collective-permute-done.pair, f32[200,128]{1,0:T(8,128)S(1)} %collective-permute-done.1.after, ...), custom_call_target="tpu_custom_call" | custom-call | tf_op jit(solution)/shard_map/pallas_call | solution.py:586
  9.2 2.5 %collective-permute-start.6 = (f32[4,8,128]{2,1,0:T(8,128)S(1)}, f32[4,8,128]{2,1,0:T(8,128)S(1)}, u32[]{:S(2)}, u32[]{:S(2)}) collective-permute-start(f32[4,8,128]{2,1,0:T(8,128)S(1)} %get-tuple-element.34.refs_0_), channel_id=1, source_target_pairs={{0,3},{1,2},{2,1},{3,0},{4,7},{5,6},{6,5},{7,4},{8,11},{9,10},{10,... | collective-permute-start | bytes 49160 | tf_op jit(solution)/shard_map/ppermute | solution.py:600
  11.7 0.5 %collective-permute-start.5 = (f32[4,8,128]{2,1,0:T(8,128)S(1)}, f32[4,8,128]{2,1,0:T(8,128)S(1)}, u32[]{:S(2)}, u32[]{:S(2)}) collective-permute-start(f32[4,8,128]{2,1,0:T(8,128)S(1)} %get-tuple-element.34.refs_0_), channel_id=1, source_target_pairs={{0,2},{1,3},{2,0},{3,1},{4,6},{5,7},{6,4},{7,5},{8,10},{9,11},{10,... | collective-permute-start | bytes 49160 | tf_op jit(solution)/shard_map/ppermute | solution.py:600
  12.3 0.5 %collective-permute-start.4 = (f32[4,8,128]{2,1,0:T(8,128)S(1)}, f32[4,8,128]{2,1,0:T(8,128)S(1)}, u32[]{:S(2)}, u32[]{:S(2)}) collective-permute-start(f32[4,8,128]{2,1,0:T(8,128)S(1)} %get-tuple-element.34.refs_0_), channel_id=1, source_target_pairs={{0,1},{1,0},{2,3},{3,2},{4,5},{5,4},{6,7},{7,6},{8,9},{9,8},{10,11... | collective-permute-start | bytes 49160 | tf_op jit(solution)/shard_map/ppermute | solution.py:600
  12.8 1.1 %collective-permute-done.6.refs_3_ = f32[4,8,128]{2,1,0:T(8,128)S(1)} collective-permute-done((f32[4,8,128]{2,1,0:T(8,128)S(1)}, f32[4,8,128]{2,1,0:T(8,128)S(1)}, u32[]{:S(2)}, u32[]{:S(2)}) %collective-permute-start.6) | collective-permute-done | bytes 16416 | tf_op jit(solution)/shard_map/ppermute | solution.py:600
  13.9 1.5 %collective-permute-done.5.refs_2_ = f32[4,8,128]{2,1,0:T(8,128)S(1)} collective-permute-done((f32[4,8,128]{2,1,0:T(8,128)S(1)}, f32[4,8,128]{2,1,0:T(8,128)S(1)}, u32[]{:S(2)}, u32[]{:S(2)}) %collective-permute-start.5) | collective-permute-done | bytes 16416 | tf_op jit(solution)/shard_map/ppermute | solution.py:600
  15.5 0.5 %collective-permute-done.4.refs_1_ = f32[4,8,128]{2,1,0:T(8,128)S(1)} collective-permute-done((f32[4,8,128]{2,1,0:T(8,128)S(1)}, f32[4,8,128]{2,1,0:T(8,128)S(1)}, u32[]{:S(2)}, u32[]{:S(2)}) %collective-permute-start.4) | collective-permute-done | bytes 16416 | tf_op jit(solution)/shard_map/ppermute | solution.py:600
  16.0 1.3 %shard_map.108 = (f32[64,128]{1,0:T(8,128)}, f32[64,128]{1,0:T(8,128)}) custom-call(f32[4,8,128]{2,1,0:T(8,128)S(1)} %get-tuple-element.34.refs_0_, f32[4,8,128]{2,1,0:T(8,128)S(1)} %collective-permute-done.4.refs_1_, f32[4,8,128]{2,1,0:T(8,128)S(1)} %collective-permute-done.5.refs_2_, f32[4,8,128]{2,1,0:T(8,128)S(1)} %collective-permute-done.6.refs_3_, ...), custom_call_target="tpu_custom_call" | custom-call | tf_op jit(solution)/shard_map/pallas_call | solution.py:603
  (2 shorter events, 0.0 us)
Async XLA Ops:
  1.5 6.1 %collective-permute-start.1 = (f32[200,128]{1,0:T(8,128)S(1)}, f32[200,128]{1,0:T(8,128)S(1)}, u32[]{:S(2)}, u32[]{:S(2)}) collective-permute-start(f32[200,128]{1,0:T(8,128)S(1)} %shard_map.104.near), channel_id=1, source_target_pairs={{0,1},{1,0},{2,3},{3,2},{4,8},{5,9},{6,10},{7,11},{8,4},{9,5},{10,... | collective-permute-start | bytes 307208 | tf_op jit(solution)/shard_map/ppermute | solution.py:563
  4.5 3.2 %collective-permute-start = (f32[200,128]{1,0:T(8,128)S(1)}, f32[200,128]{1,0:T(8,128)S(1)}, u32[]{:S(2)}, u32[]{:S(2)}) collective-permute-start(f32[200,128]{1,0:T(8,128)S(1)} %shard_map.104.near), channel_id=1, source_target_pairs={{0,4},{1,5},{2,6},{3,7},{4,0},{5,1},{6,2},{7,3},{8,12},{9,13},{10,... | collective-permute-start | bytes 307208 | tf_op jit(solution)/shard_map/ppermute | solution.py:568
  4.7 3.5 %collective-permute-start.2 = (f32[72,128]{1,0:T(8,128)S(1)}, f32[72,128]{1,0:T(8,128)S(1)}, u32[]{:S(2)}, u32[]{:S(2)}) collective-permute-start(f32[72,128]{1,0:T(8,128)S(1)} %slice.8), channel_id=1, source_target_pairs={{0,8},{1,9},{2,10},{3,11},{4,0},{5,1},{6,2},{7,3},{8,16},{9,17},{1... | collective-permute-start | bytes 110600 | tf_op jit(solution)/shard_map/ppermute | solution.py:567
  7.6 1.3 %collective-permute-start.3 = (f32[72,128]{1,0:T(8,128)S(1)}, f32[72,128]{1,0:T(8,128)S(1)}, u32[]{:S(2)}, u32[]{:S(2)}) collective-permute-start(f32[72,128]{1,0:T(8,128)S(1)} %slice.9), channel_id=1, source_target_pairs={{0,4},{1,5},{2,6},{3,7},{4,0},{5,1},{6,2},{7,3},{8,12},{9,13},{10,... | collective-permute-start | bytes 110600 | tf_op jit(solution)/shard_map/ppermute | solution.py:570
  9.2 4.7 %collective-permute-start.6 = (f32[4,8,128]{2,1,0:T(8,128)S(1)}, f32[4,8,128]{2,1,0:T(8,128)S(1)}, u32[]{:S(2)}, u32[]{:S(2)}) collective-permute-start(f32[4,8,128]{2,1,0:T(8,128)S(1)} %get-tuple-element.34.refs_0_), channel_id=1, source_target_pairs={{0,3},{1,2},{2,1},{3,0},{4,7},{5,6},{6,5},{7,4},{8,11},{9,10},{10,... | collective-permute-start | bytes 49160 | tf_op jit(solution)/shard_map/ppermute | solution.py:600
  11.7 3.7 %collective-permute-start.5 = (f32[4,8,128]{2,1,0:T(8,128)S(1)}, f32[4,8,128]{2,1,0:T(8,128)S(1)}, u32[]{:S(2)}, u32[]{:S(2)}) collective-permute-start(f32[4,8,128]{2,1,0:T(8,128)S(1)} %get-tuple-element.34.refs_0_), channel_id=1, source_target_pairs={{0,2},{1,3},{2,0},{3,1},{4,6},{5,7},{6,4},{7,5},{8,10},{9,11},{10,... | collective-permute-start | bytes 49160 | tf_op jit(solution)/shard_map/ppermute | solution.py:600
  12.3 3.7 %collective-permute-start.4 = (f32[4,8,128]{2,1,0:T(8,128)S(1)}, f32[4,8,128]{2,1,0:T(8,128)S(1)}, u32[]{:S(2)}, u32[]{:S(2)}) collective-permute-start(f32[4,8,128]{2,1,0:T(8,128)S(1)} %get-tuple-element.34.refs_0_), channel_id=1, source_target_pairs={{0,1},{1,0},{2,3},{3,2},{4,5},{5,4},{6,7},{7,6},{8,9},{9,8},{10,11... | collective-permute-start | bytes 49160 | tf_op jit(solution)/shard_map/ppermute | solution.py:600

commit v7 on v6

--- a/solution.py
+++ b/solution.py
@@ -74,16 +74,21 @@
     return tables
 
 
-def fill_plane(plane, columns, at, label_blocks):
+def upright(row):
+    z = lax.broadcasted_iota(jnp.int32, (HB, LB), 0)
+    lane = lax.broadcasted_iota(jnp.int32, (HB, LB), 1)
+    column = jnp.sum(jnp.where(z == lane, row, 0.0), axis=1, keepdims=True)
+    return jnp.broadcast_to(column, (HB, LB))
+
+
+def fill_plane(plane, table, at, label_blocks):
     for block in range(label_blocks):
-        plane[:, block * LB : (block + 1) * LB] = jnp.broadcast_to(
-            columns[:, at + block : at + block + 1], (HB, LB)
-        )
+        plane[:, block * LB : (block + 1) * LB] = upright(table[at + block : at + block + 1])
 
 
 def aside_kernel(
     near, gating_in, fwd_v_in, fwd_g_in, axial_in, shear_in, rate_in, inverse_in,
-    axial, shear, rate, inverse, vectors, own, lines, planes, early, w, v, g, label, sems,
+    axial, shear, numbers, vectors, own, lines, planes, early, w, v, g, label, inverse, rate, sems,
 ):
     width = w.shape[1]
     label_blocks = width // LB
@@ -101,14 +106,15 @@
     vectors[0] = jnp.broadcast_to(inner_column, (HB, width))
     vectors[1] = jnp.broadcast_to(outer_column, (HB, width))
     own[...] = square
+    for n, value in enumerate(edge_constants(inverse, rate)):
+        numbers[n : n + 1] = jnp.broadcast_to(value, (1, width))
     lines[0:1] = inner
     lines[1:2] = outer
     lines[2:3] = jnp.broadcast_to(bridge, (1, ZB))
     label[...] = jnp.zeros(label.shape, F32)
     label[0:label_blocks] = near[HB : HB + label_blocks, :LB]
-    columns = jnp.concatenate(lookup(label[...], axial, shear), axis=0).T[:HB]
-    for k in range(4):
-        fill_plane(planes.at[k], columns, 8 * k, label_blocks)
+    for k, table in enumerate(lookup(label[...], axial, shear)):
+        fill_plane(planes.at[k], table, 0, label_blocks)
     tissue = planes[3]
     late_v, early_v = v[1].astype(F32), v[0].astype(F32)
     early[0] = (1.0 - TIME_STEP * RECOVERY_RATE) * (tissue * w[...])
@@ -180,13 +186,6 @@
 def orientation():
     line = lax.axis_index("gx")
     return jnp.where(lax.rem(line, 2) == 0, 1.0, -1.0)
-
-
-def upright(row):
-    z = lax.broadcasted_iota(jnp.int32, (HB, LB), 0)
-    lane = lax.broadcasted_iota(jnp.int32, (HB, LB), 1)
-    column = jnp.sum(jnp.where(z == lane, row, 0.0), axis=1, keepdims=True)
-    return jnp.broadcast_to(column, (HB, LB))
 
 
 def put_total(share, kind, slot, value):
@@ -227,13 +226,9 @@
     label_blocks = width // LB
     given = {1: after, 2: near, 3: pair}
     tables = lookup(label_rows(rows, {1: after, 3: pair}, label_blocks), axial, shear)
-    columns = jnp.concatenate(tables, axis=0).T[:HB]
     for k in range(4):
         for slot in (1, 3):
-            fill_plane(
-                beside.at[2 * k + slot // 2], columns,
-                k * rows.shape[0] + slot * label_blocks, label_blocks,
-            )
+            fill_plane(beside.at[2 * k + slot // 2], tables[k], slot * label_blocks, label_blocks)
     coef = coefficients(here, beside, None)
     sign = orientation()
     bridge = lines[2:3, 0:1]
@@ -269,11 +264,9 @@
     tables = lookup(label_rows(rows, given, label_blocks), axial, shear)
     for k in range(2):
         for slot in (0, 4):
-            for block in range(label_blocks):
-                at = slot * label_blocks + block
-                distant[2 * k + slot // 4, :, block * LB : (block + 1) * LB] = upright(
-                    tables[2 * k][at : at + 1]
-                )
+            fill_plane(
+                distant.at[2 * k + slot // 4], tables[2 * k], slot * label_blocks, label_blocks
+            )
     coef = coefficients(here, beside, distant)
     sign = orientation()
     inner, outer, bridge = lines[0:1], lines[1:2], lines[2:3, 0:1]
@@ -340,26 +333,42 @@
     return -(-(SHARED + (1 if width == LB else 24)) // 2)
 
 
-def edge_couplings(edge_in, edge_out, inverse, rate, only=None):
+def edge_constants(inverse, rate):
     blocks = inverse.shape[0]
-    first, last, corner, reach = [], [], [], []
+    links = [jnp.minimum(rate[:, b : b + 1], rate[:, b + 1 : b + 2]) for b in range(blocks - 1)]
+    none = jnp.zeros((1, 1), F32)
+    links = [none] + links + [none]
+    found = []
     for b in range(blocks):
         top, bottom = inverse[b, 0:1], inverse[b, ZB - 1 : ZB]
         middle = inverse[b, HB - 1 : HB]
         bridge = middle[:, HB : HB + 1]
-        first.append(edge_out[2 * b] + (top[:, HB : HB + 1] / bridge) * edge_in[2 * b + 1])
-        last.append(edge_out[2 * b + 1] + (bottom[:, HB - 1 : HB] / bridge) * edge_in[2 * b])
-        corner.append((top[:, 0:1], top[:, ZB - 1 :], bottom[:, 0:1], bottom[:, ZB - 1 :]))
-        reach.append((middle[:, ZB - 1 :], inverse[b, HB : HB + 1][:, 0:1]))
-    links = [jnp.minimum(rate[:, b : b + 1], rate[:, b + 1 : b + 2]) for b in range(blocks - 1)]
+        below, above = links[b], links[b + 1]
+        found += [
+            top[:, HB : HB + 1] / bridge, bottom[:, HB - 1 : HB] / bridge,
+            below * top[:, 0:1], above * top[:, ZB - 1 :],
+            below * bottom[:, 0:1], above * bottom[:, ZB - 1 :],
+            middle[:, ZB - 1 :], inverse[b, HB : HB + 1][:, 0:1],
+            below, above, bridge,
+        ]
+    return found
+
+
+KINDS = 11
+
+
+def edge_couplings(edge_in, edge_out, numbers):
+    blocks = numbers.shape[0] // KINDS
+
+    def number(b, kind):
+        return numbers[KINDS * b + kind : KINDS * b + kind + 1]
+
+    first = [edge_out[2 * b] + number(b, 0) * edge_in[2 * b + 1] for b in range(blocks)]
+    last = [edge_out[2 * b + 1] + number(b, 1) * edge_in[2 * b] for b in range(blocks)]
     down = [None] + [
-        (links[b - 1] * corner[b][0], links[b] * corner[b][1] if b < blocks - 1 else None)
-        for b in range(1, blocks)
+        (number(b, 2), number(b, 3) if b < blocks - 1 else None) for b in range(1, blocks)
     ]
-    ups = [
-        (links[b - 1] * corner[b][2] if b else None, links[b] * corner[b][3])
-        for b in range(blocks - 1)
-    ]
+    ups = [(number(b, 4) if b else None, number(b, 5)) for b in range(blocks - 1)]
     u_first, u_last = list(first), list(last)
     for _ in range(SWEEPS - 1):
         n_first, n_last = list(first), list(last)
@@ -375,10 +384,10 @@
     factors = []
     zero = jnp.zeros_like(first[0])
     for b in range(blocks):
-        below = links[b - 1] * u_last[b - 1] if b else zero
-        above = links[b] * u_first[b + 1] if b < blocks - 1 else zero
-        factors.append((edge_in[2 * b + 1] + reach[b][0] * above, below))
-        factors.append((edge_in[2 * b] + reach[b][1] * below, above))
+        below = number(b, 8) * u_last[b - 1] if b else zero
+        above = number(b, 9) * u_first[b + 1] if b < blocks - 1 else zero
+        factors.append((edge_in[2 * b + 1] + number(b, 6) * above, below))
+        factors.append((edge_in[2 * b] + number(b, 7) * below, above))
     return factors
 
 
@@ -393,9 +402,9 @@
 def finish_kernel(halves, *refs):
     shares = refs[:halves]
     (
-        solved, centres, partial, outside, here, beside, distant, vectors, own, early, inverse, rate,
-    ) = refs[halves : halves + 12]
-    out_v, out_w, board = refs[halves + 12 :]
+        solved, centres, partial, outside, here, beside, distant, vectors, own, early, numbers,
+    ) = refs[halves : halves + 11]
+    out_v, out_w, board = refs[halves + 11 :]
     width = out_v.shape[1]
     me = lax.axis_index("gy")
     sign = orientation()
@@ -408,7 +417,7 @@
 
     every = range(halves)
     first = edge_couplings(
-        [tile(h, EDGE_IN) for h in every], [tile(h, EDGE_OUT) for h in every], inverse, rate
+        [tile(h, EDGE_IN) for h in every], [tile(h, EDGE_OUT) for h in every], numbers
     )
     inner_plane, outer_plane = vectors[0], vectors[1]
     coef = coefficients(here, beside, distant)
@@ -475,10 +484,10 @@
                         - shared(6, k) * down_high + shared(7, k) * down_low
                     )
                 totals[g] = totals[g] + tile(h, WEIGHTS + k) * factor + TIME_STEP * spread
-        bridge = inverse[h // 2, HB - 1 : HB][:, HB : HB + 1]
-        sums_in.append(bridge * totals[0])
+        at = KINDS * (h // 2) + 10
+        sums_in.append(numbers[at : at + 1] * totals[0])
         sums_out.append(totals[1])
-    alpha, beta = pick(edge_couplings(sums_in, sums_out, inverse, rate))
+    alpha, beta = pick(edge_couplings(sums_in, sums_out, numbers))
     final = [None] * SLOTS
     for s in (1, 2, 3):
         final[s] = (
@@ -533,18 +542,19 @@
         compiler_params=room,
     )(*in_hbm(adj_voltage[0], adj_gating[0], voltages, gatings, region_labels[0].T))
     both = pltpu.VMEM((2, HB, width), fwd_voltage.dtype)
-    axial, shear, rate, inverse, vectors, own, own_rows, here, early = pl.pallas_call(
+    axial, shear, numbers, vectors, own, own_rows, here, early = pl.pallas_call(
         aside_kernel,
         out_shape=(
             shape(region_axial.shape, F32), shape((1,) + region_shear.shape, F32),
-            shape((1,) + block_rate.shape, F32), shape(block_inverse.shape, F32),
+            shape((KINDS * block_inverse.shape[0], width), F32),
             shape((2, HB, width), F32), shape((HB, HB), F32), shape((8, ZB), F32),
             shape((4, HB, width), F32), shape((4, HB, width), F32),
         ),
         in_specs=[VMEM] + [HBM] * 7,
-        out_specs=(VMEM,) * 9,
+        out_specs=(VMEM,) * 8,
         scratch_shapes=[
             pltpu.VMEM((HB, width), F32), both, both, pltpu.VMEM((8, LB), F32),
+            pltpu.VMEM(block_inverse.shape, F32), pltpu.VMEM((1,) + block_rate.shape, F32),
             pltpu.SemaphoreType.DMA((7,)),
         ],
         compiler_params=room,
@@ -603,13 +613,13 @@
     out_v, out_w = pl.pallas_call(
         lambda *refs: finish_kernel(lanes, *refs),
         out_shape=(shape((HB, width), F32),) * 2,
-        in_specs=[VMEM] * (lanes + 12),
+        in_specs=[VMEM] * (lanes + 11),
         out_specs=(VMEM,) * 2,
         scratch_shapes=[pltpu.VMEM((lanes,) + share_shape, F32)],
         compiler_params=room,
     )(
         *shares, solved, centres, partial, outside, here, beside, distant, vectors, own, early,
-        inverse, rate,
+        numbers,
     )
     return (out_v[None], out_w[None])
 

time: 17.5 us -> 17.3 us (0.989)
  Pallas kernels: 4.28 us -> 3.93 us
where the time goes in v7:
time: 17.3 us; the launch traced here: 17.1 us
  starting transfers between devices  8.4 us (49%)
  waiting for transfers between devices  4.04 us (23%)
  Pallas kernels  3.93 us (23%)
  between operations  0.69 us (4%)
    ppermute x3, starting transfers between devices, per_device(): lax.ppermute(share, BOTH, swaps(lines, lanes, lambda i, j: (i, j ^ d)))  3.55 us
    ppermute x3, waiting for transfers between devices, per_device(): lax.ppermute(share, BOTH, swaps(lines, lanes, lambda i, j: (i, j ^ d)))  3.25 us
    ppermute x1, starting transfers between devices, per_device(): lax.ppermute(near, BOTH, swaps(lines, lanes, lambda i, j: (i, j ^ 1) if i...  3 us
    ppermute x1, starting transfers between devices, per_device(): lax.ppermute(near[:FAR], BOTH, swaps(lines, lanes, lambda i, j: (onward[i...  1.58 us
    pallas_call x1, Pallas kernels, per_device(): pl.pallas_call(aside_kernel, out_shape=(shape(region_axial.shape, F32), s...  1.24 us
    pallas_call x1, Pallas kernels, per_device(): pl.pallas_call(lambda *refs: finish_kernel(lanes, *refs), out_shape=(shap...  1.1 us
    pallas_call x1, Pallas kernels, per_device(): pl.pallas_call(first_kernel, out_shape=shape((3 * HB + 8, width), F32), i...  0.87 us
    ppermute x1, waiting for transfers between devices, per_device(): beyond = lax.ppermute(relayed, BOTH, pairing)  0.78 us
  transfers between devices with their start and end apart: 7, of which 4 were waited for; matrix products, arithmetic and copies ran while one was open for 0% of the time, Pallas kernels for 10%

profile of v7, /device:TPU:0, one launch (start us, length us, event | category | flops | bytes accessed | tf_op | source)
XLA Modules:
  0.0 17.1 jit_solution(7505791300784271279)
XLA Ops:
  0.6 0.9 %shard_map.104.near = f32[200,128]{1,0:T(8,128)S(1)} custom-call(f32[64,128]{1,0:T(8,128)} %bitcast.15, f32[64,128]{1,0:T(8,128)} %bitcast.9, bf16[2,64,128]{2,1,0:T(8,128)(2,1)} %bitcast.11, bf16[2,64,128]{2,1,0:T(8,128)(2,1)} %bitcast.13, s32[1,64]{1,0:T(1,128)} %bitcast.16), custom_call_target="tpu_custom_call" | custom-call | tf_op jit(solution)/shard_map/pallas_call | solution.py:534
  1.5 3.0 %collective-permute-start.1 = (f32[200,128]{1,0:T(8,128)S(1)}, f32[200,128]{1,0:T(8,128)S(1)}, u32[]{:S(2)}, u32[]{:S(2)}) collective-permute-start(f32[200,128]{1,0:T(8,128)S(1)} %shard_map.104.near), channel_id=1, source_target_pairs={{0,1},{1,0},{2,3},{3,2},{4,8},{5,9},{6,10},{7,11},{8,4},{9,5},{10,... | collective-permute-start | bytes 307208 | tf_op jit(solution)/shard_map/ppermute | solution.py:573
  4.5 0.2 %collective-permute-start = (f32[200,128]{1,0:T(8,128)S(1)}, f32[200,128]{1,0:T(8,128)S(1)}, u32[]{:S(2)}, u32[]{:S(2)}) collective-permute-start(f32[200,128]{1,0:T(8,128)S(1)} %shard_map.104.near), channel_id=1, source_target_pairs={{0,4},{1,5},{2,6},{3,7},{4,0},{5,1},{6,2},{7,3},{8,12},{9,13},{10,... | collective-permute-start | bytes 307208 | tf_op jit(solution)/shard_map/ppermute | solution.py:578
  4.7 1.6 %collective-permute-start.2 = (f32[72,128]{1,0:T(8,128)S(1)}, f32[72,128]{1,0:T(8,128)S(1)}, u32[]{:S(2)}, u32[]{:S(2)}) collective-permute-start(f32[72,128]{1,0:T(8,128)S(1)} %slice.8), channel_id=1, source_target_pairs={{0,8},{1,9},{2,10},{3,11},{4,0},{5,1},{6,2},{7,3},{8,16},{9,17},{1... | collective-permute-start | bytes 110600 | tf_op jit(solution)/shard_map/ppermute | solution.py:577
  6.3 1.2 %shard_map.105 = (f32[2,8]{1,0:T(2,128)S(1)}, f32[1,8]{1,0:T(1,128)S(1)}, f32[22,128]{1,0:T(8,128)S(1)}, f32[2,64,128]{2,1,0:T(8,128)S(1)}, f32[64,64]{1,0:T(8,1...) custom-call(f32[200,128]{1,0:T(8,128)S(1)} %shard_map.104.near, ...), custom_call_target="tpu_custom_call" | custom-call | flops 1048576 | bytes 1048576 | tf_op jit(solution)/shard_map/pallas_call | solution.py:545
  7.5 0.0 collective-permute-done.1.after
  7.6 0.1 collective-permute-start.3
  7.6 0.0 collective-permute-done.pair
  7.7 0.4 %shard_map.106 = (f32[4,8,128]{2,1,0:T(8,128)S(1)}, f32[64,128]{1,0:T(8,128)S(1)}, f32[3,64,128]{2,1,0:T(8,128)S(1)}, f32[3,64,128]{2,1,0:T(8,128)S(1)}, f32[8,64,128]{2,1,0:T(8,128)S(1)}) custom-call(f32[200,128]{1,0:T(8,128)S(1)} %shard_map.104.near, f32[200,128]{1,0:T(8,128)S(1)} %collective-permute-done.pair, ...), custom_call_target="tpu_custom_call" | custom-call | flops 1048576 | bytes 1048576 | tf_op jit(solution)/shard_map/pallas_call | solution.py:584
  8.1 0.0 collective-permute-done.2.before
  8.1 0.8 %collective-permute-done.3.beyond = f32[72,128]{1,0:T(8,128)S(1)} collective-permute-done((f32[72,128]{1,0:T(8,128)S(1)}, f32[72,128]{1,0:T(8,128)S(1)}, u32[]{:S(2)}, u32[]{:S(2)}) %collective-permute-start.3) | collective-permute-done | bytes 36896 | tf_op jit(solution)/shard_map/ppermute | solution.py:580
  8.8 0.3 %shard_map.107 = (f32[4,8,128]{2,1,0:T(8,128)S(1)}, f32[2,64,128]{2,1,0:T(8,128)S(1)}, f32[4,64,128]{2,1,0:T(8,128)S(1)}) custom-call(f32[200,128]{1,0:T(8,128)S(1)} %shard_map.104.near, f32[200,128]{1,0:T(8,128)S(1)} %collective-permute-done.pair, f32[200,128]{1,0:T(8,128)S(1)} %collective-permute-done.1.after, ...), custom_call_target="tpu_custom_call" | custom-call | tf_op jit(solution)/shard_map/pallas_call | solution.py:596
  9.2 2.6 %collective-permute-start.6 = (f32[4,8,128]{2,1,0:T(8,128)S(1)}, f32[4,8,128]{2,1,0:T(8,128)S(1)}, u32[]{:S(2)}, u32[]{:S(2)}) collective-permute-start(f32[4,8,128]{2,1,0:T(8,128)S(1)} %get-tuple-element.33.refs_0_), channel_id=1, source_target_pairs={{0,3},{1,2},{2,1},{3,0},{4,7},{5,6},{6,5},{7,4},{8,11},{9,10},{10,... | collective-permute-start | bytes 49160 | tf_op jit(solution)/shard_map/ppermute | solution.py:610
  11.7 0.5 %collective-permute-start.5 = (f32[4,8,128]{2,1,0:T(8,128)S(1)}, f32[4,8,128]{2,1,0:T(8,128)S(1)}, u32[]{:S(2)}, u32[]{:S(2)}) collective-permute-start(f32[4,8,128]{2,1,0:T(8,128)S(1)} %get-tuple-element.33.refs_0_), channel_id=1, source_target_pairs={{0,2},{1,3},{2,0},{3,1},{4,6},{5,7},{6,4},{7,5},{8,10},{9,11},{10,... | collective-permute-start | bytes 49160 | tf_op jit(solution)/shard_map/ppermute | solution.py:610
  12.2 0.5 %collective-permute-start.4 = (f32[4,8,128]{2,1,0:T(8,128)S(1)}, f32[4,8,128]{2,1,0:T(8,128)S(1)}, u32[]{:S(2)}, u32[]{:S(2)}) collective-permute-start(f32[4,8,128]{2,1,0:T(8,128)S(1)} %get-tuple-element.33.refs_0_), channel_id=1, source_target_pairs={{0,1},{1,0},{2,3},{3,2},{4,5},{5,4},{6,7},{7,6},{8,9},{9,8},{10,11... | collective-permute-start | bytes 49160 | tf_op jit(solution)/shard_map/ppermute | solution.py:610
  12.7 1.1 %collective-permute-done.6.refs_3_ = f32[4,8,128]{2,1,0:T(8,128)S(1)} collective-permute-done((f32[4,8,128]{2,1,0:T(8,128)S(1)}, f32[4,8,128]{2,1,0:T(8,128)S(1)}, u32[]{:S(2)}, u32[]{:S(2)}) %collective-permute-start.6) | collective-permute-done | bytes 16416 | tf_op jit(solution)/shard_map/ppermute | solution.py:610
  13.9 1.6 %collective-permute-done.5.refs_2_ = f32[4,8,128]{2,1,0:T(8,128)S(1)} collective-permute-done((f32[4,8,128]{2,1,0:T(8,128)S(1)}, f32[4,8,128]{2,1,0:T(8,128)S(1)}, u32[]{:S(2)}, u32[]{:S(2)}) %collective-permute-start.5) | collective-permute-done | bytes 16416 | tf_op jit(solution)/shard_map/ppermute | solution.py:610
  15.5 0.5 %collective-permute-done.4.refs_1_ = f32[4,8,128]{2,1,0:T(8,128)S(1)} collective-permute-done((f32[4,8,128]{2,1,0:T(8,128)S(1)}, f32[4,8,128]{2,1,0:T(8,128)S(1)}, u32[]{:S(2)}, u32[]{:S(2)}) %collective-permute-start.4) | collective-permute-done | bytes 16416 | tf_op jit(solution)/shard_map/ppermute | solution.py:610
  16.0 1.1 %shard_map.108 = (f32[64,128]{1,0:T(8,128)}, f32[64,128]{1,0:T(8,128)}) custom-call(f32[4,8,128]{2,1,0:T(8,128)S(1)} %get-tuple-element.33.refs_0_, f32[4,8,128]{2,1,0:T(8,128)S(1)} %collective-permute-done.4.refs_1_, f32[4,8,128]{2,1,0:T(8,128)S(1)} %collective-permute-done.5.refs_2_, f32[4,8,128]{2,1,0:T(8,128)S(1)} %collective-permute-done.6.refs_3_, ...), custom_call_target="tpu_custom_call" | custom-call | tf_op jit(solution)/shard_map/pallas_call | solution.py:613
  (2 shorter events, 0.0 us)
Async XLA Ops:
  1.5 6.0 %collective-permute-start.1 = (f32[200,128]{1,0:T(8,128)S(1)}, f32[200,128]{1,0:T(8,128)S(1)}, u32[]{:S(2)}, u32[]{:S(2)}) collective-permute-start(f32[200,128]{1,0:T(8,128)S(1)} %shard_map.104.near), channel_id=1, source_target_pairs={{0,1},{1,0},{2,3},{3,2},{4,8},{5,9},{6,10},{7,11},{8,4},{9,5},{10,... | collective-permute-start | bytes 307208 | tf_op jit(solution)/shard_map/ppermute | solution.py:573
  4.5 3.1 %collective-permute-start = (f32[200,128]{1,0:T(8,128)S(1)}, f32[200,128]{1,0:T(8,128)S(1)}, u32[]{:S(2)}, u32[]{:S(2)}) collective-permute-start(f32[200,128]{1,0:T(8,128)S(1)} %shard_map.104.near), channel_id=1, source_target_pairs={{0,4},{1,5},{2,6},{3,7},{4,0},{5,1},{6,2},{7,3},{8,12},{9,13},{10,... | collective-permute-start | bytes 307208 | tf_op jit(solution)/shard_map/ppermute | solution.py:578
  4.7 3.3 %collective-permute-start.2 = (f32[72,128]{1,0:T(8,128)S(1)}, f32[72,128]{1,0:T(8,128)S(1)}, u32[]{:S(2)}, u32[]{:S(2)}) collective-permute-start(f32[72,128]{1,0:T(8,128)S(1)} %slice.8), channel_id=1, source_target_pairs={{0,8},{1,9},{2,10},{3,11},{4,0},{5,1},{6,2},{7,3},{8,16},{9,17},{1... | collective-permute-start | bytes 110600 | tf_op jit(solution)/shard_map/ppermute | solution.py:577
  7.6 1.3 %collective-permute-start.3 = (f32[72,128]{1,0:T(8,128)S(1)}, f32[72,128]{1,0:T(8,128)S(1)}, u32[]{:S(2)}, u32[]{:S(2)}) collective-permute-start(f32[72,128]{1,0:T(8,128)S(1)} %slice.9), channel_id=1, source_target_pairs={{0,4},{1,5},{2,6},{3,7},{4,0},{5,1},{6,2},{7,3},{8,12},{9,13},{10,... | collective-permute-start | bytes 110600 | tf_op jit(solution)/shard_map/ppermute | solution.py:580
  9.2 4.7 %collective-permute-start.6 = (f32[4,8,128]{2,1,0:T(8,128)S(1)}, f32[4,8,128]{2,1,0:T(8,128)S(1)}, u32[]{:S(2)}, u32[]{:S(2)}) collective-permute-start(f32[4,8,128]{2,1,0:T(8,128)S(1)} %get-tuple-element.33.refs_0_), channel_id=1, source_target_pairs={{0,3},{1,2},{2,1},{3,0},{4,7},{5,6},{6,5},{7,4},{8,11},{9,10},{10,... | collective-permute-start | bytes 49160 | tf_op jit(solution)/shard_map/ppermute | solution.py:610
  11.7 3.7 %collective-permute-start.5 = (f32[4,8,128]{2,1,0:T(8,128)S(1)}, f32[4,8,128]{2,1,0:T(8,128)S(1)}, u32[]{:S(2)}, u32[]{:S(2)}) collective-permute-start(f32[4,8,128]{2,1,0:T(8,128)S(1)} %get-tuple-element.33.refs_0_), channel_id=1, source_target_pairs={{0,2},{1,3},{2,0},{3,1},{4,6},{5,7},{6,4},{7,5},{8,10},{9,11},{10,... | collective-permute-start | bytes 49160 | tf_op jit(solution)/shard_map/ppermute | solution.py:610
  12.2 3.7 %collective-permute-start.4 = (f32[4,8,128]{2,1,0:T(8,128)S(1)}, f32[4,8,128]{2,1,0:T(8,128)S(1)}, u32[]{:S(2)}, u32[]{:S(2)}) collective-permute-start(f32[4,8,128]{2,1,0:T(8,128)S(1)} %get-tuple-element.33.refs_0_), channel_id=1, source_target_pairs={{0,1},{1,0},{2,3},{3,2},{4,5},{5,4},{6,7},{7,6},{8,9},{9,8},{10,11... | collective-permute-start | bytes 49160 | tf_op jit(solution)/shard_map/ppermute | solution.py:610

commit v8 on v7

--- a/solution.py
+++ b/solution.py
@@ -105,7 +105,7 @@
     inner, outer, inner_column, outer_column, bridge, square = half_vectors(inverse, mine, upper)
     vectors[0] = jnp.broadcast_to(inner_column, (HB, width))
     vectors[1] = jnp.broadcast_to(outer_column, (HB, width))
-    own[...] = square
+    own[...] = left_parts(square)
     for n, value in enumerate(edge_constants(inverse, rate)):
         numbers[n : n + 1] = jnp.broadcast_to(value, (1, width))
     lines[0:1] = inner
@@ -125,6 +125,23 @@
     )
 
 
+def two_parts(value):
+    high = value.astype(jnp.bfloat16)
+    return high, (value - high.astype(F32)).astype(jnp.bfloat16)
+
+
+def left_parts(matrix):
+    high, low = two_parts(matrix)
+    return jnp.concatenate([high, high, low, low], axis=1)
+
+
+def times(parts, field):
+    high, low = two_parts(field)
+    return jnp.dot(
+        parts, jnp.concatenate([high, low, high, low], axis=0), preferred_element_type=F32
+    )
+
+
 def half_vectors(inverse, mine, upper):
     def row(index):
         return inverse[mine, index : index + 1, :]
@@ -211,10 +228,7 @@
 
 
 def solve_planes(own, fields, width):
-    product = jnp.dot(
-        own[...], jnp.concatenate(fields, axis=1),
-        precision=lax.Precision.HIGHEST, preferred_element_type=F32,
-    )
+    product = times(own[...], jnp.concatenate(fields, axis=1))
     return [product[:, n * width : (n + 1) * width] for n in range(len(fields))]
 
 
@@ -437,10 +451,7 @@
         + stencil(s, added, centres[s - 1], coef, sign)
         for s in (1, 2, 3)
     ]
-    product = jnp.dot(
-        own[...], jnp.concatenate(nexts, axis=1),
-        precision=lax.Precision.HIGHEST, preferred_element_type=F32,
-    )
+    product = times(own[...], jnp.concatenate(nexts, axis=1))
 
     rolls = (7, 1)
     sums_in, sums_out = [], []
@@ -547,7 +558,7 @@
         out_shape=(
             shape(region_axial.shape, F32), shape((1,) + region_shear.shape, F32),
             shape((KINDS * block_inverse.shape[0], width), F32),
-            shape((2, HB, width), F32), shape((HB, HB), F32), shape((8, ZB), F32),
+            shape((2, HB, width), F32), shape((HB, 4 * HB), jnp.bfloat16), shape((8, ZB), F32),
             shape((4, HB, width), F32), shape((4, HB, width), F32),
         ),
         in_specs=[VMEM] + [HBM] * 7,

time: 17.3 us -> 17.3 us (level)
  no operation moved by 1% of the time
where the time goes in v8:
time: 17.3 us; the launch traced here: 17 us
  starting transfers between devices  8.4 us (49%)
  waiting for transfers between devices  4.05 us (23%)
  Pallas kernels  3.87 us (22%)
  between operations  0.7 us (4%)
    ppermute x3, starting transfers between devices, per_device(): lax.ppermute(share, BOTH, swaps(lines, lanes, lambda i, j: (i, j ^ d)))  3.55 us
    ppermute x3, waiting for transfers between devices, per_device(): lax.ppermute(share, BOTH, swaps(lines, lanes, lambda i, j: (i, j ^ d)))  3.21 us
    ppermute x1, starting transfers between devices, per_device(): lax.ppermute(near, BOTH, swaps(lines, lanes, lambda i, j: (i, j ^ 1) if i...  3 us
    ppermute x1, starting transfers between devices, per_device(): lax.ppermute(near[:FAR], BOTH, swaps(lines, lanes, lambda i, j: (onward[i...  1.58 us
    pallas_call x1, Pallas kernels, per_device(): pl.pallas_call(aside_kernel, out_shape=(shape(region_axial.shape, F32), s...  1.28 us
    pallas_call x1, Pallas kernels, per_device(): pl.pallas_call(lambda *refs: finish_kernel(lanes, *refs), out_shape=(shap...  1.05 us
    pallas_call x1, Pallas kernels, per_device(): pl.pallas_call(first_kernel, out_shape=shape((3 * HB + 8, width), F32), i...  0.87 us
    ppermute x1, waiting for transfers between devices, per_device(): beyond = lax.ppermute(relayed, BOTH, pairing)  0.83 us
  transfers between devices with their start and end apart: 7, of which 4 were waited for; matrix products, arithmetic and copies ran while one was open for 0% of the time, Pallas kernels for 10%

profile of v8, /device:TPU:0, one launch (start us, length us, event | category | flops | bytes accessed | tf_op | source)
XLA Modules:
  0.0 17.0 jit_solution(3301781833805572805)
XLA Ops:
  0.6 0.9 %shard_map.104.near = f32[200,128]{1,0:T(8,128)S(1)} custom-call(f32[64,128]{1,0:T(8,128)} %bitcast.15, f32[64,128]{1,0:T(8,128)} %bitcast.9, bf16[2,64,128]{2,1,0:T(8,128)(2,1)} %bitcast.11, bf16[2,64,128]{2,1,0:T(8,128)(2,1)} %bitcast.13, s32[1,64]{1,0:T(1,128)} %bitcast.16), custom_call_target="tpu_custom_call" | custom-call | tf_op jit(solution)/shard_map/pallas_call | solution.py:545
  1.5 3.0 %collective-permute-start.1 = (f32[200,128]{1,0:T(8,128)S(1)}, f32[200,128]{1,0:T(8,128)S(1)}, u32[]{:S(2)}, u32[]{:S(2)}) collective-permute-start(f32[200,128]{1,0:T(8,128)S(1)} %shard_map.104.near), channel_id=1, source_target_pairs={{0,1},{1,0},{2,3},{3,2},{4,8},{5,9},{6,10},{7,11},{8,4},{9,5},{10,... | collective-permute-start | bytes 307208 | tf_op jit(solution)/shard_map/ppermute | solution.py:584
  4.5 0.2 %collective-permute-start = (f32[200,128]{1,0:T(8,128)S(1)}, f32[200,128]{1,0:T(8,128)S(1)}, u32[]{:S(2)}, u32[]{:S(2)}) collective-permute-start(f32[200,128]{1,0:T(8,128)S(1)} %shard_map.104.near), channel_id=1, source_target_pairs={{0,4},{1,5},{2,6},{3,7},{4,0},{5,1},{6,2},{7,3},{8,12},{9,13},{10,... | collective-permute-start | bytes 307208 | tf_op jit(solution)/shard_map/ppermute | solution.py:589
  4.7 1.6 %collective-permute-start.2 = (f32[72,128]{1,0:T(8,128)S(1)}, f32[72,128]{1,0:T(8,128)S(1)}, u32[]{:S(2)}, u32[]{:S(2)}) collective-permute-start(f32[72,128]{1,0:T(8,128)S(1)} %slice.8), channel_id=1, source_target_pairs={{0,8},{1,9},{2,10},{3,11},{4,0},{5,1},{6,2},{7,3},{8,16},{9,17},{1... | collective-permute-start | bytes 110600 | tf_op jit(solution)/shard_map/ppermute | solution.py:588
  6.3 1.3 %shard_map.105 = (f32[2,8]{1,0:T(2,128)S(1)}, f32[1,8]{1,0:T(1,128)S(1)}, f32[22,128]{1,0:T(8,128)S(1)}, f32[2,64,128]{2,1,0:T(8,128)S(1)}, bf16[64,256]{1,0:T(8...) custom-call(f32[200,128]{1,0:T(8,128)S(1)} %shard_map.104.near, ...), custom_call_target="tpu_custom_call" | custom-call | flops 1048576 | bytes 1048576 | tf_op jit(solution)/shard_map/pallas_call | solution.py:556
  7.6 0.0 collective-permute-done.1.after
  7.6 0.1 collective-permute-start.3
  7.7 0.0 collective-permute-done.pair
  7.7 0.3 %shard_map.106 = (f32[4,8,128]{2,1,0:T(8,128)S(1)}, f32[64,128]{1,0:T(8,128)S(1)}, f32[3,64,128]{2,1,0:T(8,128)S(1)}, f32[3,64,128]{2,1,0:T(8,128)S(1)}, f32[8,64,128]{2,1,0:T(8,128)S(1)}) custom-call(f32[200,128]{1,0:T(8,128)S(1)} %shard_map.104.near, f32[200,128]{1,0:T(8,128)S(1)} %collective-permute-done.pair, ...), custom_call_target="tpu_custom_call" | custom-call | flops 1048576 | bytes 1048576 | tf_op jit(solution)/shard_map/pallas_call | solution.py:595
  8.0 0.0 collective-permute-done.2.before
  8.1 0.8 %collective-permute-done.3.beyond = f32[72,128]{1,0:T(8,128)S(1)} collective-permute-done((f32[72,128]{1,0:T(8,128)S(1)}, f32[72,128]{1,0:T(8,128)S(1)}, u32[]{:S(2)}, u32[]{:S(2)}) %collective-permute-start.3) | collective-permute-done | bytes 36896 | tf_op jit(solution)/shard_map/ppermute | solution.py:591
  8.9 0.3 %shard_map.107 = (f32[4,8,128]{2,1,0:T(8,128)S(1)}, f32[2,64,128]{2,1,0:T(8,128)S(1)}, f32[4,64,128]{2,1,0:T(8,128)S(1)}) custom-call(f32[200,128]{1,0:T(8,128)S(1)} %shard_map.104.near, f32[200,128]{1,0:T(8,128)S(1)} %collective-permute-done.pair, f32[200,128]{1,0:T(8,128)S(1)} %collective-permute-done.1.after, ...), custom_call_target="tpu_custom_call" | custom-call | tf_op jit(solution)/shard_map/pallas_call | solution.py:607
  9.2 2.5 %collective-permute-start.6 = (f32[4,8,128]{2,1,0:T(8,128)S(1)}, f32[4,8,128]{2,1,0:T(8,128)S(1)}, u32[]{:S(2)}, u32[]{:S(2)}) collective-permute-start(f32[4,8,128]{2,1,0:T(8,128)S(1)} %get-tuple-element.33.refs_0_), channel_id=1, source_target_pairs={{0,3},{1,2},{2,1},{3,0},{4,7},{5,6},{6,5},{7,4},{8,11},{9,10},{10,... | collective-permute-start | bytes 49160 | tf_op jit(solution)/shard_map/ppermute | solution.py:621
  11.7 0.5 %collective-permute-start.5 = (f32[4,8,128]{2,1,0:T(8,128)S(1)}, f32[4,8,128]{2,1,0:T(8,128)S(1)}, u32[]{:S(2)}, u32[]{:S(2)}) collective-permute-start(f32[4,8,128]{2,1,0:T(8,128)S(1)} %get-tuple-element.33.refs_0_), channel_id=1, source_target_pairs={{0,2},{1,3},{2,0},{3,1},{4,6},{5,7},{6,4},{7,5},{8,10},{9,11},{10,... | collective-permute-start | bytes 49160 | tf_op jit(solution)/shard_map/ppermute | solution.py:621
  12.2 0.5 %collective-permute-start.4 = (f32[4,8,128]{2,1,0:T(8,128)S(1)}, f32[4,8,128]{2,1,0:T(8,128)S(1)}, u32[]{:S(2)}, u32[]{:S(2)}) collective-permute-start(f32[4,8,128]{2,1,0:T(8,128)S(1)} %get-tuple-element.33.refs_0_), channel_id=1, source_target_pairs={{0,1},{1,0},{2,3},{3,2},{4,5},{5,4},{6,7},{7,6},{8,9},{9,8},{10,11... | collective-permute-start | bytes 49160 | tf_op jit(solution)/shard_map/ppermute | solution.py:621
  12.8 1.1 %collective-permute-done.6.refs_3_ = f32[4,8,128]{2,1,0:T(8,128)S(1)} collective-permute-done((f32[4,8,128]{2,1,0:T(8,128)S(1)}, f32[4,8,128]{2,1,0:T(8,128)S(1)}, u32[]{:S(2)}, u32[]{:S(2)}) %collective-permute-start.6) | collective-permute-done | bytes 16416 | tf_op jit(solution)/shard_map/ppermute | solution.py:621
  13.9 1.6 %collective-permute-done.5.refs_2_ = f32[4,8,128]{2,1,0:T(8,128)S(1)} collective-permute-done((f32[4,8,128]{2,1,0:T(8,128)S(1)}, f32[4,8,128]{2,1,0:T(8,128)S(1)}, u32[]{:S(2)}, u32[]{:S(2)}) %collective-permute-start.5) | collective-permute-done | bytes 16416 | tf_op jit(solution)/shard_map/ppermute | solution.py:621
  15.5 0.5 %collective-permute-done.4.refs_1_ = f32[4,8,128]{2,1,0:T(8,128)S(1)} collective-permute-done((f32[4,8,128]{2,1,0:T(8,128)S(1)}, f32[4,8,128]{2,1,0:T(8,128)S(1)}, u32[]{:S(2)}, u32[]{:S(2)}) %collective-permute-start.4) | collective-permute-done | bytes 16416 | tf_op jit(solution)/shard_map/ppermute | solution.py:621
  16.0 1.0 %shard_map.108 = (f32[64,128]{1,0:T(8,128)}, f32[64,128]{1,0:T(8,128)}) custom-call(f32[4,8,128]{2,1,0:T(8,128)S(1)} %get-tuple-element.33.refs_0_, f32[4,8,128]{2,1,0:T(8,128)S(1)} %collective-permute-done.4.refs_1_, f32[4,8,128]{2,1,0:T(8,128)S(1)} %collective-permute-done.5.refs_2_, f32[4,8,128]{2,1,0:T(8,128)S(1)} %collective-permute-done.6.refs_3_, ...), custom_call_target="tpu_custom_call" | custom-call | tf_op jit(solution)/shard_map/pallas_call | solution.py:624
  (2 shorter events, 0.0 us)
Async XLA Ops:
  1.5 6.1 %collective-permute-start.1 = (f32[200,128]{1,0:T(8,128)S(1)}, f32[200,128]{1,0:T(8,128)S(1)}, u32[]{:S(2)}, u32[]{:S(2)}) collective-permute-start(f32[200,128]{1,0:T(8,128)S(1)} %shard_map.104.near), channel_id=1, source_target_pairs={{0,1},{1,0},{2,3},{3,2},{4,8},{5,9},{6,10},{7,11},{8,4},{9,5},{10,... | collective-permute-start | bytes 307208 | tf_op jit(solution)/shard_map/ppermute | solution.py:584
  4.5 3.2 %collective-permute-start = (f32[200,128]{1,0:T(8,128)S(1)}, f32[200,128]{1,0:T(8,128)S(1)}, u32[]{:S(2)}, u32[]{:S(2)}) collective-permute-start(f32[200,128]{1,0:T(8,128)S(1)} %shard_map.104.near), channel_id=1, source_target_pairs={{0,4},{1,5},{2,6},{3,7},{4,0},{5,1},{6,2},{7,3},{8,12},{9,13},{10,... | collective-permute-start | bytes 307208 | tf_op jit(solution)/shard_map/ppermute | solution.py:589
  4.7 3.3 %collective-permute-start.2 = (f32[72,128]{1,0:T(8,128)S(1)}, f32[72,128]{1,0:T(8,128)S(1)}, u32[]{:S(2)}, u32[]{:S(2)}) collective-permute-start(f32[72,128]{1,0:T(8,128)S(1)} %slice.8), channel_id=1, source_target_pairs={{0,8},{1,9},{2,10},{3,11},{4,0},{5,1},{6,2},{7,3},{8,16},{9,17},{1... | collective-permute-start | bytes 110600 | tf_op jit(solution)/shard_map/ppermute | solution.py:588
  7.6 1.3 %collective-permute-start.3 = (f32[72,128]{1,0:T(8,128)S(1)}, f32[72,128]{1,0:T(8,128)S(1)}, u32[]{:S(2)}, u32[]{:S(2)}) collective-permute-start(f32[72,128]{1,0:T(8,128)S(1)} %slice.9), channel_id=1, source_target_pairs={{0,4},{1,5},{2,6},{3,7},{4,0},{5,1},{6,2},{7,3},{8,12},{9,13},{10,... | collective-permute-start | bytes 110600 | tf_op jit(solution)/shard_map/ppermute | solution.py:591
  9.2 4.7 %collective-permute-start.6 = (f32[4,8,128]{2,1,0:T(8,128)S(1)}, f32[4,8,128]{2,1,0:T(8,128)S(1)}, u32[]{:S(2)}, u32[]{:S(2)}) collective-permute-start(f32[4,8,128]{2,1,0:T(8,128)S(1)} %get-tuple-element.33.refs_0_), channel_id=1, source_target_pairs={{0,3},{1,2},{2,1},{3,0},{4,7},{5,6},{6,5},{7,4},{8,11},{9,10},{10,... | collective-permute-start | bytes 49160 | tf_op jit(solution)/shard_map/ppermute | solution.py:621
  11.7 3.7 %collective-permute-start.5 = (f32[4,8,128]{2,1,0:T(8,128)S(1)}, f32[4,8,128]{2,1,0:T(8,128)S(1)}, u32[]{:S(2)}, u32[]{:S(2)}) collective-permute-start(f32[4,8,128]{2,1,0:T(8,128)S(1)} %get-tuple-element.33.refs_0_), channel_id=1, source_target_pairs={{0,2},{1,3},{2,0},{3,1},{4,6},{5,7},{6,4},{7,5},{8,10},{9,11},{10,... | collective-permute-start | bytes 49160 | tf_op jit(solution)/shard_map/ppermute | solution.py:621
  12.2 3.7 %collective-permute-start.4 = (f32[4,8,128]{2,1,0:T(8,128)S(1)}, f32[4,8,128]{2,1,0:T(8,128)S(1)}, u32[]{:S(2)}, u32[]{:S(2)}) collective-permute-start(f32[4,8,128]{2,1,0:T(8,128)S(1)} %get-tuple-element.33.refs_0_), channel_id=1, source_target_pairs={{0,1},{1,0},{2,3},{3,2},{4,5},{5,4},{6,7},{7,6},{8,9},{9,8},{10,11... | collective-permute-start | bytes 49160 | tf_op jit(solution)/shard_map/ppermute | solution.py:621

commit v9 on v8

--- a/solution.py
+++ b/solution.py
@@ -41,35 +41,26 @@
     return copies
 
 
-def first_kernel(voltage_in, gating_in, fwd_v_in, fwd_g_in, label_in, near, v, g, label, sems):
+def first_kernel(fwd_v_in, fwd_g_in, label_in, tile, gains, v, g, label, sems):
     later = fwd_v_in.shape[0] - 1
-    copies = start_copies(
-        [
-            (fwd_v_in.at[later], v), (fwd_g_in.at[later], g), (label_in, label),
-            (gating_in, near.at[LEAD]), (voltage_in, near.at[pl.ds(0, HB)]),
-        ],
-        sems,
-    )
-    for copy in copies[:3]:
+    copies = start_copies([(fwd_v_in.at[later], v), (fwd_g_in.at[later], g), (label_in, label)], sems)
+    for copy in copies:
         copy.wait()
-    near[GAIN] = gain(v[...].astype(F32), g[...].astype(F32))
+    gains[...] = gain(v[...].astype(F32), g[...].astype(F32))
     blocks = label.shape[0]
-    near[HB:FAR] = jnp.zeros((8, near.shape[1]), F32)
-    near[HB : HB + blocks, 0:HB] = label[...].astype(F32)
-    for copy in copies[3:]:
-        copy.wait()
-
-
-def lookup(label, axial, shear):
+    tile[...] = jnp.zeros(tile.shape, F32)
+    tile[0:blocks, 0:HB] = label[...].astype(F32)
+
+
+def lookup(label, regions):
+    count = regions.shape[0] // 3
     zero = jnp.zeros(label.shape, F32)
     tables = [zero, zero, zero]
-    for region in range(1, axial.shape[1]):
+    for region in range(1, count):
         here = label == float(region)
-        for k, value in enumerate(
-            (axial[0:1, region : region + 1], axial[1:2, region : region + 1],
-             shear[0:1, region : region + 1])
-        ):
-            tables[k] = jnp.where(here, value, tables[k])
+        for k in range(3):
+            at = k * count + region
+            tables[k] = jnp.where(here, regions[at : at + 1], tables[k])
     tables.append((label > 0.0).astype(F32))
     return tables
 
@@ -88,7 +79,8 @@
 
 def aside_kernel(
     near, gating_in, fwd_v_in, fwd_g_in, axial_in, shear_in, rate_in, inverse_in,
-    axial, shear, numbers, vectors, own, lines, planes, early, w, v, g, label, inverse, rate, sems,
+    regions, numbers, vectors, own, lines, planes, early,
+    w, v, g, label, inverse, rate, axial, shear, sems,
 ):
     width = w.shape[1]
     label_blocks = width // LB
@@ -111,9 +103,14 @@
     lines[0:1] = inner
     lines[1:2] = outer
     lines[2:3] = jnp.broadcast_to(bridge, (1, ZB))
+    count = axial.shape[1]
+    for region in range(count):
+        for k, table in enumerate((axial[0:1], axial[1:2], shear[...])):
+            at = k * count + region
+            regions[at : at + 1] = jnp.broadcast_to(table[:, region : region + 1], (1, LB))
     label[...] = jnp.zeros(label.shape, F32)
     label[0:label_blocks] = near[HB : HB + label_blocks, :LB]
-    for k, table in enumerate(lookup(label[...], axial, shear)):
+    for k, table in enumerate(lookup(label[...], regions)):
         fill_plane(planes.at[k], table, 0, label_blocks)
     tissue = planes[3]
     late_v, early_v = v[1].astype(F32), v[0].astype(F32)
@@ -233,13 +230,13 @@
 
 
 def gather_kernel(
-    near, pair, after, axial, shear, vectors, own, lines, here,
+    near, pair, after, regions, vectors, own, lines, here,
     share, solved, centres, partial, beside, rows,
 ):
     width = near.shape[1]
     label_blocks = width // LB
     given = {1: after, 2: near, 3: pair}
-    tables = lookup(label_rows(rows, {1: after, 3: pair}, label_blocks), axial, shear)
+    tables = lookup(label_rows(rows, {1: after, 3: pair}, label_blocks), regions)
     for k in range(4):
         for slot in (1, 3):
             fill_plane(beside.at[2 * k + slot // 2], tables[k], slot * label_blocks, label_blocks)
@@ -269,13 +266,13 @@
 
 
 def complete_kernel(
-    near, pair, after, before, beyond, axial, shear, vectors, own, lines, here,
+    near, pair, after, before, beyond, regions, vectors, own, lines, here,
     begun, most, beside, share, outside, distant, rows,
 ):
     width = near.shape[1]
     label_blocks = width // LB
     given = {0: before, 1: after, 2: near, 3: pair, 4: beyond}
-    tables = lookup(label_rows(rows, given, label_blocks), axial, shear)
+    tables = lookup(label_rows(rows, given, label_blocks), regions)
     for k in range(2):
         for slot in (0, 4):
             fill_plane(
@@ -542,30 +539,32 @@
     in_hbm = lambda *arrays: [pltpu.with_memory_space_constraint(x, pltpu.HBM) for x in arrays]
     voltages, gatings = fwd_voltage[:, 0], fwd_gating[:, 0]
     late = pltpu.VMEM((HB, width), fwd_voltage.dtype)
-    near = pl.pallas_call(
+    tile, gains = pl.pallas_call(
         first_kernel,
-        out_shape=shape((3 * HB + 8, width), F32),
-        in_specs=[HBM] * 5,
-        out_specs=VMEM,
+        out_shape=(shape((8, width), F32), shape((HB, width), F32)),
+        in_specs=[HBM] * 3,
+        out_specs=(VMEM,) * 2,
         scratch_shapes=[
-            late, late, pltpu.VMEM((label_blocks, HB), jnp.int32), pltpu.SemaphoreType.DMA((5,)),
+            late, late, pltpu.VMEM((label_blocks, HB), jnp.int32), pltpu.SemaphoreType.DMA((3,)),
         ],
         compiler_params=room,
-    )(*in_hbm(adj_voltage[0], adj_gating[0], voltages, gatings, region_labels[0].T))
+    )(*in_hbm(voltages, gatings, region_labels[0].T))
+    near = jnp.concatenate([adj_voltage[0], tile, gains, adj_gating[0]], axis=0)
     both = pltpu.VMEM((2, HB, width), fwd_voltage.dtype)
-    axial, shear, numbers, vectors, own, own_rows, here, early = pl.pallas_call(
+    regions, numbers, vectors, own, own_rows, here, early = pl.pallas_call(
         aside_kernel,
         out_shape=(
-            shape(region_axial.shape, F32), shape((1,) + region_shear.shape, F32),
+            shape((3 * region_axial.shape[1], LB), F32),
             shape((KINDS * block_inverse.shape[0], width), F32),
             shape((2, HB, width), F32), shape((HB, 4 * HB), jnp.bfloat16), shape((8, ZB), F32),
             shape((4, HB, width), F32), shape((4, HB, width), F32),
         ),
         in_specs=[VMEM] + [HBM] * 7,
-        out_specs=(VMEM,) * 8,
+        out_specs=(VMEM,) * 7,
         scratch_shapes=[
             pltpu.VMEM((HB, width), F32), both, both, pltpu.VMEM((8, LB), F32),
             pltpu.VMEM(block_inverse.shape, F32), pltpu.VMEM((1,) + block_rate.shape, F32),
+            pltpu.VMEM(region_axial.shape, F32), pltpu.VMEM((1,) + region_shear.shape, F32),
             pltpu.SemaphoreType.DMA((7,)),
         ],
         compiler_params=room,
@@ -598,23 +597,23 @@
             shape(share_shape, F32), shape((HB, width), F32), shape((3, HB, width), F32),
             shape((3, HB, width), F32), shape((8, HB, width), F32),
         ),
-        in_specs=[VMEM] * 9,
+        in_specs=[VMEM] * 8,
         out_specs=(VMEM,) * 5,
         scratch_shapes=label_scratch,
         compiler_params=room,
         cost_estimate=pl.CostEstimate(flops=1 << 20, bytes_accessed=1 << 20, transcendentals=0),
-    )(near, pair, after, axial, shear, vectors, own, own_rows, here)
+    )(near, pair, after, regions, vectors, own, own_rows, here)
     share, outside, distant = pl.pallas_call(
         complete_kernel,
         out_shape=(
             shape(share_shape, F32), shape((2, HB, width), F32), shape((4, HB, width), F32),
         ),
-        in_specs=[VMEM] * 14,
+        in_specs=[VMEM] * 13,
         out_specs=(VMEM,) * 3,
         scratch_shapes=label_scratch,
         compiler_params=room,
     )(
-        near, pair, after, before, beyond, axial, shear, vectors, own, own_rows, here, begun,
+        near, pair, after, before, beyond, regions, vectors, own, own_rows, here, begun,
         partial, beside,
     )
     shares = [share] + [

time: 17.3 us -> 17.2 us (level)
  no operation moved by 1% of the time
where the time goes in v9:
time: 17.2 us; the launch traced here: 17 us
  starting transfers between devices  8.4 us (49%)
  waiting for transfers between devices  4.07 us (24%)
  Pallas kernels  3.81 us (22%)
  between operations  0.73 us (4%)
    ppermute x3, starting transfers between devices, per_device(): lax.ppermute(share, BOTH, swaps(lines, lanes, lambda i, j: (i, j ^ d)))  3.55 us
    ppermute x3, waiting for transfers between devices, per_device(): lax.ppermute(share, BOTH, swaps(lines, lanes, lambda i, j: (i, j ^ d)))  3.2 us
    ppermute x1, starting transfers between devices, per_device(): lax.ppermute(near, BOTH, swaps(lines, lanes, lambda i, j: (i, j ^ 1) if i...  3 us
    ppermute x1, starting transfers between devices, per_device(): lax.ppermute(near[:FAR], BOTH, swaps(lines, lanes, lambda i, j: (onward[i...  1.58 us
    pallas_call x1, Pallas kernels, per_device(): pl.pallas_call(aside_kernel, out_shape=(shape((3 * region_axial.shape[1],...  1.35 us
    pallas_call x1, Pallas kernels, per_device(): pl.pallas_call(lambda *refs: finish_kernel(lanes, *refs), out_shape=(shap...  1.05 us
    ppermute x1, waiting for transfers between devices, per_device(): beyond = lax.ppermute(relayed, BOTH, pairing)  0.86 us
    pallas_call x1, Pallas kernels, per_device(): pl.pallas_call(first_kernel, out_shape=(shape((8, width), F32), shape((HB...  0.79 us
  transfers between devices with their start and end apart: 7, of which 4 were waited for; matrix products, arithmetic and copies ran while one was open for 0% of the time, Pallas kernels for 10%

profile of v9, /device:TPU:0, one launch (start us, length us, event | category | flops | bytes accessed | tf_op | source)
XLA Modules:
  0.0 17.0 jit_solution(258106997937849039)
XLA Ops:
  0.6 0.0 copy-start
  0.6 0.0 copy-start.1
  0.7 0.8 %shard_map.104 = (f32[8,128]{1,0:T(8,128)S(1)}, f32[64,128]{1,0:T(8,128)S(1)}) custom-call(bf16[2,64,128]{2,1,0:T(8,128)(2,1)} %bitcast.13, bf16[2,64,128]{2,1,0:T(8,128)(2,1)} %bitcast.15, s32[1,64]{1,0:T(1,128)} %bitcast.17), custom_call_target="tpu_custom_call" | custom-call | tf_op jit(solution)/shard_map/pallas_call | solution.py:542
  1.4 0.0 copy-done
  1.5 0.0 copy-done.1
  1.5 3.0 %collective-permute-start.1 = (f32[200,128]{1,0:T(8,128)S(1)}, f32[200,128]{1,0:T(8,128)S(1)}, u32[]{:S(2)}, u32[]{:S(2)}) collective-permute-start(f32[200,128]{1,0:T(8,128)S(1)} %pad_maximum_fusion.near), channel_id=1, source_target_pairs={{0,1},{1,0},{2,3},{3,2},{4,8},{5,9},{6,10},{7,11},{8,4},{9,5},{10,... | collective-permute-start | bytes 307208 | tf_op jit(solution)/shard_map/ppermute | solution.py:583
  4.5 0.2 %collective-permute-start = (f32[200,128]{1,0:T(8,128)S(1)}, f32[200,128]{1,0:T(8,128)S(1)}, u32[]{:S(2)}, u32[]{:S(2)}) collective-permute-start(f32[200,128]{1,0:T(8,128)S(1)} %pad_maximum_fusion.near), channel_id=1, source_target_pairs={{0,4},{1,5},{2,6},{3,7},{4,0},{5,1},{6,2},{7,3},{8,12},{9,13},{10,... | collective-permute-start | bytes 307208 | tf_op jit(solution)/shard_map/ppermute | solution.py:588
  4.7 1.6 %collective-permute-start.2 = (f32[72,128]{1,0:T(8,128)S(1)}, f32[72,128]{1,0:T(8,128)S(1)}, u32[]{:S(2)}, u32[]{:S(2)}) collective-permute-start(f32[72,128]{1,0:T(8,128)S(1)} %pad_maximum_fusion.1), channel_id=1, source_target_pairs={{0,8},{1,9},{2,10},{3,11},{4,0},{5,1},{6,2},{7,3},{8,16},{9,17},{1... | collective-permute-start | bytes 110600 | tf_op jit(solution)/shard_map/ppermute | solution.py:587
  6.3 1.3 %shard_map.105 = (f32[24,128]{1,0:T(8,128)S(1)}, f32[22,128]{1,0:T(8,128)S(1)}, f32[2,64,128]{2,1,0:T(8,128)S(1)}, bf16[64,256]{1,0:T(8,128)(2,1)S(1)}, f32[8,12...) custom-call(f32[200,128]{1,0:T(8,128)S(1)} %pad_maximum_fusion.near, f32[64,128]{1,0:T(8,128)} %bitcast.11, ...), custom_call_target="tpu_custom_call" | custom-call | flops 1048576 | bytes 1048576 | tf_op jit(solution)/shard_map/pallas_call | solution.py:554
  7.6 0.0 collective-permute-done.1.after
  7.6 0.1 collective-permute-start.3
  7.7 0.0 collective-permute-done.pair
  7.7 0.3 %shard_map.106 = (f32[4,8,128]{2,1,0:T(8,128)S(1)}, f32[64,128]{1,0:T(8,128)S(1)}, f32[3,64,128]{2,1,0:T(8,128)S(1)}, f32[3,64,128]{2,1,0:T(8,128)S(1)}, f32[8,64,128]{2,1,0:T(8,128)S(1)}) custom-call(f32[200,128]{1,0:T(8,128)S(1)} %pad_maximum_fusion.near, f32[200,128]{1,0:T(8,128)S(1)} %collective-permute-done.pair, ...), custom_call_target="tpu_custom_call" | custom-call | flops 1048576 | bytes 1048576 | tf_op jit(solution)/shard_map/pallas_call | solution.py:594
  8.1 0.0 collective-permute-done.2.before
  8.1 0.9 %collective-permute-done.3.beyond = f32[72,128]{1,0:T(8,128)S(1)} collective-permute-done((f32[72,128]{1,0:T(8,128)S(1)}, f32[72,128]{1,0:T(8,128)S(1)}, u32[]{:S(2)}, u32[]{:S(2)}) %collective-permute-start.3) | collective-permute-done | bytes 36896 | tf_op jit(solution)/shard_map/ppermute | solution.py:590
  8.9 0.3 %shard_map.107 = (f32[4,8,128]{2,1,0:T(8,128)S(1)}, f32[2,64,128]{2,1,0:T(8,128)S(1)}, f32[4,64,128]{2,1,0:T(8,128)S(1)}) custom-call(f32[200,128]{1,0:T(8,128)S(1)} %pad_maximum_fusion.near, f32[200,128]{1,0:T(8,128)S(1)} %collective-permute-done.pair, f32[200,128]{1,0:T(8,128)S(1)} %collective-permute-done.1.after, ...), custom_call_target="tpu_custom_call" | custom-call | tf_op jit(solution)/shard_map/pallas_call | solution.py:606
  9.2 2.5 %collective-permute-start.6 = (f32[4,8,128]{2,1,0:T(8,128)S(1)}, f32[4,8,128]{2,1,0:T(8,128)S(1)}, u32[]{:S(2)}, u32[]{:S(2)}) collective-permute-start(f32[4,8,128]{2,1,0:T(8,128)S(1)} %get-tuple-element.35.refs_0_), channel_id=1, source_target_pairs={{0,3},{1,2},{2,1},{3,0},{4,7},{5,6},{6,5},{7,4},{8,11},{9,10},{10,... | collective-permute-start | bytes 49160 | tf_op jit(solution)/shard_map/ppermute | solution.py:620
  11.8 0.5 %collective-permute-start.5 = (f32[4,8,128]{2,1,0:T(8,128)S(1)}, f32[4,8,128]{2,1,0:T(8,128)S(1)}, u32[]{:S(2)}, u32[]{:S(2)}) collective-permute-start(f32[4,8,128]{2,1,0:T(8,128)S(1)} %get-tuple-element.35.refs_0_), channel_id=1, source_target_pairs={{0,2},{1,3},{2,0},{3,1},{4,6},{5,7},{6,4},{7,5},{8,10},{9,11},{10,... | collective-permute-start | bytes 49160 | tf_op jit(solution)/shard_map/ppermute | solution.py:620
  12.3 0.5 %collective-permute-start.4 = (f32[4,8,128]{2,1,0:T(8,128)S(1)}, f32[4,8,128]{2,1,0:T(8,128)S(1)}, u32[]{:S(2)}, u32[]{:S(2)}) collective-permute-start(f32[4,8,128]{2,1,0:T(8,128)S(1)} %get-tuple-element.35.refs_0_), channel_id=1, source_target_pairs={{0,1},{1,0},{2,3},{3,2},{4,5},{5,4},{6,7},{7,6},{8,9},{9,8},{10,11... | collective-permute-start | bytes 49160 | tf_op jit(solution)/shard_map/ppermute | solution.py:620
  12.8 1.1 %collective-permute-done.6.refs_3_ = f32[4,8,128]{2,1,0:T(8,128)S(1)} collective-permute-done((f32[4,8,128]{2,1,0:T(8,128)S(1)}, f32[4,8,128]{2,1,0:T(8,128)S(1)}, u32[]{:S(2)}, u32[]{:S(2)}) %collective-permute-start.6) | collective-permute-done | bytes 16416 | tf_op jit(solution)/shard_map/ppermute | solution.py:620
  13.9 1.5 %collective-permute-done.5.refs_2_ = f32[4,8,128]{2,1,0:T(8,128)S(1)} collective-permute-done((f32[4,8,128]{2,1,0:T(8,128)S(1)}, f32[4,8,128]{2,1,0:T(8,128)S(1)}, u32[]{:S(2)}, u32[]{:S(2)}) %collective-permute-start.5) | collective-permute-done | bytes 16416 | tf_op jit(solution)/shard_map/ppermute | solution.py:620
  15.5 0.5 %collective-permute-done.4.refs_1_ = f32[4,8,128]{2,1,0:T(8,128)S(1)} collective-permute-done((f32[4,8,128]{2,1,0:T(8,128)S(1)}, f32[4,8,128]{2,1,0:T(8,128)S(1)}, u32[]{:S(2)}, u32[]{:S(2)}) %collective-permute-start.4) | collective-permute-done | bytes 16416 | tf_op jit(solution)/shard_map/ppermute | solution.py:620
  16.0 1.0 %shard_map.108 = (f32[64,128]{1,0:T(8,128)}, f32[64,128]{1,0:T(8,128)}) custom-call(f32[4,8,128]{2,1,0:T(8,128)S(1)} %get-tuple-element.35.refs_0_, f32[4,8,128]{2,1,0:T(8,128)S(1)} %collective-permute-done.4.refs_1_, f32[4,8,128]{2,1,0:T(8,128)S(1)} %collective-permute-done.5.refs_2_, f32[4,8,128]{2,1,0:T(8,128)S(1)} %collective-permute-done.6.refs_3_, ...), custom_call_target="tpu_custom_call" | custom-call | tf_op jit(solution)/shard_map/pallas_call | solution.py:623
  (3 shorter events, 0.0 us)
Async XLA Ops:
  0.6 0.8 %copy-start = (f32[1,64,128]{2,1,0:T(8,128)S(1)}, f32[1,64,128]{2,1,0:T(8,128)}, u32[]{:S(2)}) copy-start(f32[1,64,128]{2,1,0:T(8,128)} %param.9) | copy-start | bytes 98308
  0.6 0.8 %copy-start.1 = (f32[1,64,128]{2,1,0:T(8,128)S(1)}, f32[1,64,128]{2,1,0:T(8,128)}, u32[]{:S(2)}) copy-start(f32[1,64,128]{2,1,0:T(8,128)} %param.10) | copy-start | bytes 98308
  1.5 6.1 %collective-permute-start.1 = (f32[200,128]{1,0:T(8,128)S(1)}, f32[200,128]{1,0:T(8,128)S(1)}, u32[]{:S(2)}, u32[]{:S(2)}) collective-permute-start(f32[200,128]{1,0:T(8,128)S(1)} %pad_maximum_fusion.near), channel_id=1, source_target_pairs={{0,1},{1,0},{2,3},{3,2},{4,8},{5,9},{6,10},{7,11},{8,4},{9,5},{10,... | collective-permute-start | bytes 307208 | tf_op jit(solution)/shard_map/ppermute | solution.py:583
  4.5 3.2 %collective-permute-start = (f32[200,128]{1,0:T(8,128)S(1)}, f32[200,128]{1,0:T(8,128)S(1)}, u32[]{:S(2)}, u32[]{:S(2)}) collective-permute-start(f32[200,128]{1,0:T(8,128)S(1)} %pad_maximum_fusion.near), channel_id=1, source_target_pairs={{0,4},{1,5},{2,6},{3,7},{4,0},{5,1},{6,2},{7,3},{8,12},{9,13},{10,... | collective-permute-start | bytes 307208 | tf_op jit(solution)/shard_map/ppermute | solution.py:588
  4.7 3.4 %collective-permute-start.2 = (f32[72,128]{1,0:T(8,128)S(1)}, f32[72,128]{1,0:T(8,128)S(1)}, u32[]{:S(2)}, u32[]{:S(2)}) collective-permute-start(f32[72,128]{1,0:T(8,128)S(1)} %pad_maximum_fusion.1), channel_id=1, source_target_pairs={{0,8},{1,9},{2,10},{3,11},{4,0},{5,1},{6,2},{7,3},{8,16},{9,17},{1... | collective-permute-start | bytes 110600 | tf_op jit(solution)/shard_map/ppermute | solution.py:587
  7.6 1.3 %collective-permute-start.3 = (f32[72,128]{1,0:T(8,128)S(1)}, f32[72,128]{1,0:T(8,128)S(1)}, u32[]{:S(2)}, u32[]{:S(2)}) collective-permute-start(f32[72,128]{1,0:T(8,128)S(1)} %slice.6), channel_id=1, source_target_pairs={{0,4},{1,5},{2,6},{3,7},{4,0},{5,1},{6,2},{7,3},{8,12},{9,13},{10,... | collective-permute-start | bytes 110600 | tf_op jit(solution)/shard_map/ppermute | solution.py:590
  9.2 4.7 %collective-permute-start.6 = (f32[4,8,128]{2,1,0:T(8,128)S(1)}, f32[4,8,128]{2,1,0:T(8,128)S(1)}, u32[]{:S(2)}, u32[]{:S(2)}) collective-permute-start(f32[4,8,128]{2,1,0:T(8,128)S(1)} %get-tuple-element.35.refs_0_), channel_id=1, source_target_pairs={{0,3},{1,2},{2,1},{3,0},{4,7},{5,6},{6,5},{7,4},{8,11},{9,10},{10,... | collective-permute-start | bytes 49160 | tf_op jit(solution)/shard_map/ppermute | solution.py:620
  11.8 3.7 %collective-permute-start.5 = (f32[4,8,128]{2,1,0:T(8,128)S(1)}, f32[4,8,128]{2,1,0:T(8,128)S(1)}, u32[]{:S(2)}, u32[]{:S(2)}) collective-permute-start(f32[4,8,128]{2,1,0:T(8,128)S(1)} %get-tuple-element.35.refs_0_), channel_id=1, source_target_pairs={{0,2},{1,3},{2,0},{3,1},{4,6},{5,7},{6,4},{7,5},{8,10},{9,11},{10,... | collective-permute-start | bytes 49160 | tf_op jit(solution)/shard_map/ppermute | solution.py:620
  12.3 3.7 %collective-permute-start.4 = (f32[4,8,128]{2,1,0:T(8,128)S(1)}, f32[4,8,128]{2,1,0:T(8,128)S(1)}, u32[]{:S(2)}, u32[]{:S(2)}) collective-permute-start(f32[4,8,128]{2,1,0:T(8,128)S(1)} %get-tuple-element.35.refs_0_), channel_id=1, source_target_pairs={{0,1},{1,0},{2,3},{3,2},{4,5},{5,4},{6,7},{7,6},{8,9},{9,8},{10,11... | collective-permute-start | bytes 49160 | tf_op jit(solution)/shard_map/ppermute | solution.py:620

commit v10 on v9

--- a/solution.py
+++ b/solution.py
@@ -78,9 +78,9 @@
 
 
 def aside_kernel(
-    near, gating_in, fwd_v_in, fwd_g_in, axial_in, shear_in, rate_in, inverse_in,
+    near, inverse, gating_in, fwd_v_in, fwd_g_in, axial_in, shear_in, rate_in,
     regions, numbers, vectors, own, lines, planes, early,
-    w, v, g, label, inverse, rate, axial, shear, sems,
+    w, v, g, label, rate, axial, shear, sems,
 ):
     width = w.shape[1]
     label_blocks = width // LB
@@ -88,7 +88,7 @@
     upper, mine = lax.rem(me, 2) == 1, lax.div(me, 2)
     for copy in start_copies(
         [
-            (inverse_in, inverse), (axial_in, axial), (shear_in, shear), (rate_in, rate),
+            (axial_in, axial), (shear_in, shear), (rate_in, rate),
             (gating_in, w), (fwd_v_in, v), (fwd_g_in, g),
         ],
         sems,
@@ -559,21 +559,21 @@
             shape((2, HB, width), F32), shape((HB, 4 * HB), jnp.bfloat16), shape((8, ZB), F32),
             shape((4, HB, width), F32), shape((4, HB, width), F32),
         ),
-        in_specs=[VMEM] + [HBM] * 7,
+        in_specs=[VMEM] * 2 + [HBM] * 6,
         out_specs=(VMEM,) * 7,
         scratch_shapes=[
             pltpu.VMEM((HB, width), F32), both, both, pltpu.VMEM((8, LB), F32),
-            pltpu.VMEM(block_inverse.shape, F32), pltpu.VMEM((1,) + block_rate.shape, F32),
+            pltpu.VMEM((1,) + block_rate.shape, F32),
             pltpu.VMEM(region_axial.shape, F32), pltpu.VMEM((1,) + region_shear.shape, F32),
-            pltpu.SemaphoreType.DMA((7,)),
+            pltpu.SemaphoreType.DMA((6,)),
         ],
         compiler_params=room,
         cost_estimate=pl.CostEstimate(flops=1 << 20, bytes_accessed=1 << 20, transcendentals=0),
     )(
         near,
+        block_inverse,
         *in_hbm(
             adj_gating[0], voltages, gatings, region_axial, region_shear[None], block_rate[None],
-            block_inverse,
         ),
     )
     ends = (0, lines - 1)

time: 17.2 us -> 17.3 us (level)
  transfers between devices with their start and end apart: 7 -> 7, of which waited for: 4 -> 4; matrix products, arithmetic and copies ran while one was open for 0% -> 0% of each run, Pallas kernels for 10% -> 9%
where the time goes in v10:
time: 17.3 us; the launch traced here: 17 us
  starting transfers between devices  8.4 us (49%)
  waiting for transfers between devices  4.1 us (24%)
  Pallas kernels  3.72 us (22%)
  between operations  0.74 us (4%)
    ppermute x3, starting transfers between devices, per_device(): lax.ppermute(share, BOTH, swaps(lines, lanes, lambda i, j: (i, j ^ d)))  3.55 us
    ppermute x3, waiting for transfers between devices, per_device(): lax.ppermute(share, BOTH, swaps(lines, lanes, lambda i, j: (i, j ^ d)))  3.23 us
    ppermute x1, starting transfers between devices, per_device(): lax.ppermute(near, BOTH, swaps(lines, lanes, lambda i, j: (i, j ^ 1) if i...  3 us
    ppermute x1, starting transfers between devices, per_device(): lax.ppermute(near[:FAR], BOTH, swaps(lines, lanes, lambda i, j: (onward[i...  1.58 us
    pallas_call x1, Pallas kernels, per_device(): pl.pallas_call(aside_kernel, out_shape=(shape((3 * region_axial.shape[1],...  1.26 us
    pallas_call x1, Pallas kernels, per_device(): pl.pallas_call(lambda *refs: finish_kernel(lanes, *refs), out_shape=(shap...  1.05 us
    ppermute x1, waiting for transfers between devices, per_device(): beyond = lax.ppermute(relayed, BOTH, pairing)  0.86 us
    pallas_call x1, Pallas kernels, per_device(): pl.pallas_call(first_kernel, out_shape=(shape((8, width), F32), shape((HB...  0.79 us
  transfers between devices with their start and end apart: 7, of which 4 were waited for; matrix products, arithmetic and copies ran while one was open for 0% of the time, Pallas kernels for 9%

profile of v10, /device:TPU:0, one launch (start us, length us, event | category | flops | bytes accessed | tf_op | source)
XLA Modules:
  0.0 17.0 jit_solution(9280535860078742278)
XLA Ops:
  0.6 0.0 copy-start.1
  0.6 0.0 copy-start.2
  0.7 0.8 %shard_map.104 = (f32[8,128]{1,0:T(8,128)S(1)}, f32[64,128]{1,0:T(8,128)S(1)}) custom-call(bf16[2,64,128]{2,1,0:T(8,128)(2,1)} %bitcast.13, bf16[2,64,128]{2,1,0:T(8,128)(2,1)} %bitcast.15, s32[1,64]{1,0:T(1,128)} %bitcast.17), custom_call_target="tpu_custom_call" | custom-call | tf_op jit(solution)/shard_map/pallas_call | solution.py:542
  1.4 0.0 copy-done.1
  1.5 0.0 copy-done.2
  1.5 0.0 copy-start
  1.5 3.0 %collective-permute-start.1 = (f32[200,128]{1,0:T(8,128)S(1)}, f32[200,128]{1,0:T(8,128)S(1)}, u32[]{:S(2)}, u32[]{:S(2)}) collective-permute-start(f32[200,128]{1,0:T(8,128)S(1)} %pad_maximum_fusion.near), channel_id=1, source_target_pairs={{0,1},{1,0},{2,3},{3,2},{4,8},{5,9},{6,10},{7,11},{8,4},{9,5},{10,... | collective-permute-start | bytes 307208 | tf_op jit(solution)/shard_map/ppermute | solution.py:583
  4.5 0.2 %collective-permute-start = (f32[200,128]{1,0:T(8,128)S(1)}, f32[200,128]{1,0:T(8,128)S(1)}, u32[]{:S(2)}, u32[]{:S(2)}) collective-permute-start(f32[200,128]{1,0:T(8,128)S(1)} %pad_maximum_fusion.near), channel_id=1, source_target_pairs={{0,4},{1,5},{2,6},{3,7},{4,0},{5,1},{6,2},{7,3},{8,12},{9,13},{10,... | collective-permute-start | bytes 307208 | tf_op jit(solution)/shard_map/ppermute | solution.py:588
  4.7 1.6 %collective-permute-start.2 = (f32[72,128]{1,0:T(8,128)S(1)}, f32[72,128]{1,0:T(8,128)S(1)}, u32[]{:S(2)}, u32[]{:S(2)}) collective-permute-start(f32[72,128]{1,0:T(8,128)S(1)} %pad_maximum_fusion.1), channel_id=1, source_target_pairs={{0,8},{1,9},{2,10},{3,11},{4,0},{5,1},{6,2},{7,3},{8,16},{9,17},{1... | collective-permute-start | bytes 110600 | tf_op jit(solution)/shard_map/ppermute | solution.py:587
  6.3 0.0 copy-done
  6.3 1.3 %shard_map.105 = (f32[24,128]{1,0:T(8,128)S(1)}, f32[22,128]{1,0:T(8,128)S(1)}, f32[2,64,128]{2,1,0:T(8,128)S(1)}, bf16[64,256]{1,0:T(8,128)(2,1)S(1)}, f32[8,12...) custom-call(f32[200,128]{1,0:T(8,128)S(1)} %pad_maximum_fusion.near, ...), custom_call_target="tpu_custom_call" | custom-call | flops 1048576 | bytes 1048576 | tf_op jit(solution)/shard_map/pallas_call | solution.py:554
  7.6 0.0 collective-permute-done.1.after
  7.6 0.1 collective-permute-start.3
  7.7 0.0 collective-permute-done.pair
  7.7 0.3 %shard_map.106 = (f32[4,8,128]{2,1,0:T(8,128)S(1)}, f32[64,128]{1,0:T(8,128)S(1)}, f32[3,64,128]{2,1,0:T(8,128)S(1)}, f32[3,64,128]{2,1,0:T(8,128)S(1)}, f32[8,64,128]{2,1,0:T(8,128)S(1)}) custom-call(f32[200,128]{1,0:T(8,128)S(1)} %pad_maximum_fusion.near, f32[200,128]{1,0:T(8,128)S(1)} %collective-permute-done.pair, ...), custom_call_target="tpu_custom_call" | custom-call | flops 1048576 | bytes 1048576 | tf_op jit(solution)/shard_map/pallas_call | solution.py:594
  8.0 0.0 collective-permute-done.2.before
  8.0 0.9 %collective-permute-done.3.beyond = f32[72,128]{1,0:T(8,128)S(1)} collective-permute-done((f32[72,128]{1,0:T(8,128)S(1)}, f32[72,128]{1,0:T(8,128)S(1)}, u32[]{:S(2)}, u32[]{:S(2)}) %collective-permute-start.3) | collective-permute-done | bytes 36896 | tf_op jit(solution)/shard_map/ppermute | solution.py:590
  8.9 0.3 %shard_map.107 = (f32[4,8,128]{2,1,0:T(8,128)S(1)}, f32[2,64,128]{2,1,0:T(8,128)S(1)}, f32[4,64,128]{2,1,0:T(8,128)S(1)}) custom-call(f32[200,128]{1,0:T(8,128)S(1)} %pad_maximum_fusion.near, f32[200,128]{1,0:T(8,128)S(1)} %collective-permute-done.pair, f32[200,128]{1,0:T(8,128)S(1)} %collective-permute-done.1.after, ...), custom_call_target="tpu_custom_call" | custom-call | tf_op jit(solution)/shard_map/pallas_call | solution.py:606
  9.2 2.5 %collective-permute-start.6 = (f32[4,8,128]{2,1,0:T(8,128)S(1)}, f32[4,8,128]{2,1,0:T(8,128)S(1)}, u32[]{:S(2)}, u32[]{:S(2)}) collective-permute-start(f32[4,8,128]{2,1,0:T(8,128)S(1)} %get-tuple-element.35.refs_0_), channel_id=1, source_target_pairs={{0,3},{1,2},{2,1},{3,0},{4,7},{5,6},{6,5},{7,4},{8,11},{9,10},{10,... | collective-permute-start | bytes 49160 | tf_op jit(solution)/shard_map/ppermute | solution.py:620
  11.7 0.5 %collective-permute-start.5 = (f32[4,8,128]{2,1,0:T(8,128)S(1)}, f32[4,8,128]{2,1,0:T(8,128)S(1)}, u32[]{:S(2)}, u32[]{:S(2)}) collective-permute-start(f32[4,8,128]{2,1,0:T(8,128)S(1)} %get-tuple-element.35.refs_0_), channel_id=1, source_target_pairs={{0,2},{1,3},{2,0},{3,1},{4,6},{5,7},{6,4},{7,5},{8,10},{9,11},{10,... | collective-permute-start | bytes 49160 | tf_op jit(solution)/shard_map/ppermute | solution.py:620
  12.2 0.5 %collective-permute-start.4 = (f32[4,8,128]{2,1,0:T(8,128)S(1)}, f32[4,8,128]{2,1,0:T(8,128)S(1)}, u32[]{:S(2)}, u32[]{:S(2)}) collective-permute-start(f32[4,8,128]{2,1,0:T(8,128)S(1)} %get-tuple-element.35.refs_0_), channel_id=1, source_target_pairs={{0,1},{1,0},{2,3},{3,2},{4,5},{5,4},{6,7},{7,6},{8,9},{9,8},{10,11... | collective-permute-start | bytes 49160 | tf_op jit(solution)/shard_map/ppermute | solution.py:620
  12.7 1.1 %collective-permute-done.6.refs_3_ = f32[4,8,128]{2,1,0:T(8,128)S(1)} collective-permute-done((f32[4,8,128]{2,1,0:T(8,128)S(1)}, f32[4,8,128]{2,1,0:T(8,128)S(1)}, u32[]{:S(2)}, u32[]{:S(2)}) %collective-permute-start.6) | collective-permute-done | bytes 16416 | tf_op jit(solution)/shard_map/ppermute | solution.py:620
  13.9 1.6 %collective-permute-done.5.refs_2_ = f32[4,8,128]{2,1,0:T(8,128)S(1)} collective-permute-done((f32[4,8,128]{2,1,0:T(8,128)S(1)}, f32[4,8,128]{2,1,0:T(8,128)S(1)}, u32[]{:S(2)}, u32[]{:S(2)}) %collective-permute-start.5) | collective-permute-done | bytes 16416 | tf_op jit(solution)/shard_map/ppermute | solution.py:620
  15.4 0.5 %collective-permute-done.4.refs_1_ = f32[4,8,128]{2,1,0:T(8,128)S(1)} collective-permute-done((f32[4,8,128]{2,1,0:T(8,128)S(1)}, f32[4,8,128]{2,1,0:T(8,128)S(1)}, u32[]{:S(2)}, u32[]{:S(2)}) %collective-permute-start.4) | collective-permute-done | bytes 16416 | tf_op jit(solution)/shard_map/ppermute | solution.py:620
  16.0 1.0 %shard_map.108 = (f32[64,128]{1,0:T(8,128)}, f32[64,128]{1,0:T(8,128)}) custom-call(f32[4,8,128]{2,1,0:T(8,128)S(1)} %get-tuple-element.35.refs_0_, f32[4,8,128]{2,1,0:T(8,128)S(1)} %collective-permute-done.4.refs_1_, f32[4,8,128]{2,1,0:T(8,128)S(1)} %collective-permute-done.5.refs_2_, f32[4,8,128]{2,1,0:T(8,128)S(1)} %collective-permute-done.6.refs_3_, ...), custom_call_target="tpu_custom_call" | custom-call | tf_op jit(solution)/shard_map/pallas_call | solution.py:623
  (3 shorter events, 0.0 us)
Async XLA Ops:
  0.6 0.8 %copy-start.1 = (f32[1,64,128]{2,1,0:T(8,128)S(1)}, f32[1,64,128]{2,1,0:T(8,128)}, u32[]{:S(2)}) copy-start(f32[1,64,128]{2,1,0:T(8,128)} %param.9) | copy-start | bytes 98308
  0.6 0.8 %copy-start.2 = (f32[1,64,128]{2,1,0:T(8,128)S(1)}, f32[1,64,128]{2,1,0:T(8,128)}, u32[]{:S(2)}) copy-start(f32[1,64,128]{2,1,0:T(8,128)} %param.10) | copy-start | bytes 98308
  1.5 4.8 %copy-start = (f32[2,128,128]{2,1,0:T(8,128)S(1)}, f32[2,128,128]{2,1,0:T(8,128)}, u32[]{:S(2)}) copy-start(f32[2,128,128]{2,1,0:T(8,128)} %inverse.1) | copy-start | bytes 393220
  1.5 6.1 %collective-permute-start.1 = (f32[200,128]{1,0:T(8,128)S(1)}, f32[200,128]{1,0:T(8,128)S(1)}, u32[]{:S(2)}, u32[]{:S(2)}) collective-permute-start(f32[200,128]{1,0:T(8,128)S(1)} %pad_maximum_fusion.near), channel_id=1, source_target_pairs={{0,1},{1,0},{2,3},{3,2},{4,8},{5,9},{6,10},{7,11},{8,4},{9,5},{10,... | collective-permute-start | bytes 307208 | tf_op jit(solution)/shard_map/ppermute | solution.py:583
  4.5 3.2 %collective-permute-start = (f32[200,128]{1,0:T(8,128)S(1)}, f32[200,128]{1,0:T(8,128)S(1)}, u32[]{:S(2)}, u32[]{:S(2)}) collective-permute-start(f32[200,128]{1,0:T(8,128)S(1)} %pad_maximum_fusion.near), channel_id=1, source_target_pairs={{0,4},{1,5},{2,6},{3,7},{4,0},{5,1},{6,2},{7,3},{8,12},{9,13},{10,... | collective-permute-start | bytes 307208 | tf_op jit(solution)/shard_map/ppermute | solution.py:588
  4.7 3.3 %collective-permute-start.2 = (f32[72,128]{1,0:T(8,128)S(1)}, f32[72,128]{1,0:T(8,128)S(1)}, u32[]{:S(2)}, u32[]{:S(2)}) collective-permute-start(f32[72,128]{1,0:T(8,128)S(1)} %pad_maximum_fusion.1), channel_id=1, source_target_pairs={{0,8},{1,9},{2,10},{3,11},{4,0},{5,1},{6,2},{7,3},{8,16},{9,17},{1... | collective-permute-start | bytes 110600 | tf_op jit(solution)/shard_map/ppermute | solution.py:587
  7.6 1.3 %collective-permute-start.3 = (f32[72,128]{1,0:T(8,128)S(1)}, f32[72,128]{1,0:T(8,128)S(1)}, u32[]{:S(2)}, u32[]{:S(2)}) collective-permute-start(f32[72,128]{1,0:T(8,128)S(1)} %slice.6), channel_id=1, source_target_pairs={{0,4},{1,5},{2,6},{3,7},{4,0},{5,1},{6,2},{7,3},{8,12},{9,13},{10,... | collective-permute-start | bytes 110600 | tf_op jit(solution)/shard_map/ppermute | solution.py:590
  9.2 4.7 %collective-permute-start.6 = (f32[4,8,128]{2,1,0:T(8,128)S(1)}, f32[4,8,128]{2,1,0:T(8,128)S(1)}, u32[]{:S(2)}, u32[]{:S(2)}) collective-permute-start(f32[4,8,128]{2,1,0:T(8,128)S(1)} %get-tuple-element.35.refs_0_), channel_id=1, source_target_pairs={{0,3},{1,2},{2,1},{3,0},{4,7},{5,6},{6,5},{7,4},{8,11},{9,10},{10,... | collective-permute-start | bytes 49160 | tf_op jit(solution)/shard_map/ppermute | solution.py:620
  11.7 3.7 %collective-permute-start.5 = (f32[4,8,128]{2,1,0:T(8,128)S(1)}, f32[4,8,128]{2,1,0:T(8,128)S(1)}, u32[]{:S(2)}, u32[]{:S(2)}) collective-permute-start(f32[4,8,128]{2,1,0:T(8,128)S(1)} %get-tuple-element.35.refs_0_), channel_id=1, source_target_pairs={{0,2},{1,3},{2,0},{3,1},{4,6},{5,7},{6,4},{7,5},{8,10},{9,11},{10,... | collective-permute-start | bytes 49160 | tf_op jit(solution)/shard_map/ppermute | solution.py:620
  12.2 3.7 %collective-permute-start.4 = (f32[4,8,128]{2,1,0:T(8,128)S(1)}, f32[4,8,128]{2,1,0:T(8,128)S(1)}, u32[]{:S(2)}, u32[]{:S(2)}) collective-permute-start(f32[4,8,128]{2,1,0:T(8,128)S(1)} %get-tuple-element.35.refs_0_), channel_id=1, source_target_pairs={{0,1},{1,0},{2,3},{3,2},{4,5},{5,4},{6,7},{7,6},{8,9},{9,8},{10,11... | collective-permute-start | bytes 49160 | tf_op jit(solution)/shard_map/ppermute | solution.py:620
